TPU v7x, 128 devices: a whole 4x4x4 slice. The times are simulated.
128 devices in a mesh: wave: 8 (over x, core), band: 16 (over y, z).
Axes of the slice: x: 4, y: 4, z: 4, core: 2. Of those that a mesh axis runs over, the one named last changes fastest.
Arguments:
- control: float32 [256, 224, 192], P('band', 'wave'), may hold values from -6 to 6
- spectral_scale: float32 [256, 224, 192], P('band', 'wave'), may hold values from 0.3 to 3
- vertical_root: float32 [96, 96], replicated, may hold values from -0.625 to 0.625
- legendre: float32 [224, 448, 256], P('wave'), may hold values from -0.375 to 0.375
- zonal_number: int32 [224], replicated, may hold values from 0 to 223, each once
- courant: float32 [448, 96, 1024], P('band', None, 'wave'), may hold values from 0.05 to 0.9
- lidar_coef: float32 [12], replicated, may hold values from 0.2 to 1
- aod_coef: float32 [96], replicated, may hold values from 0.02 to 0.2
- obs_count: int32 [128, 128], P(('wave', 'band')), may hold values from 0 to 128, as said below
- obs_column: int32 [16384, 128], P(('wave', 'band')), may hold values from 0 to 3583
- obs_level: int32 [16384, 128], P(('wave', 'band')), may hold values from 0 to 7
- lidar_obs: float32 [16384, 128], P(('wave', 'band')), may hold values from -6 to 6
- aod_obs: float32 [16384, 128], P(('wave', 'band')), may hold values from -6 to 6
- obs_weight: float32 [16384, 128], P(('wave', 'band')), may hold values from 0.5 to 2
Outputs:
- gradient: float32 [256, 224, 192], P('band', 'wave')
- state_increment: float32 [448, 96, 1024], P('band', None, 'wave')
Inputs may be any that keep to these rules, and one draw needn't show every extreme that they name: `obs_count`: live slots from a device to an owner; in every draw one owner receives 128 from every device. `zonal_number`: each number of 0 to 223 once.
All inputs are finite; a program needn't handle non-finite values.
Results may differ from a plain program's by a relative error of at most 0.0003.
Values sent between devices are 32-bit elements; how exact they have to be, the bound alone decides.
No kernel may reach another device: no remote copies, remote signals or barrier semaphores. Data moves between devices by JAX's collectives and lax.ppermute only.
A program may use at most 128 MiB of HBM per device.

v0:
```python
import math

import jax
import jax.numpy as jnp
from jax import lax
from jax.sharding import Mesh
from jax.sharding import PartitionSpec as P

MW = 224
LEV = 8
BINS = 12
STEPS = 4
WAVE = ("wave_0", "wave_1")
WAVE_BAND = ("wave_0", "wave_1", "band")


highest = lax.Precision.HIGHEST


def split_up(value, dim, length):
    lengths = value.shape
    tiles = value.reshape(*lengths[:dim], length, lengths[dim] // length, *lengths[dim + 1 :])
    return jnp.moveaxis(tiles, dim, 0)


def laid_out(tiles, dim):
    lengths = list(tiles.shape[1:])
    lengths[dim] *= tiles.shape[0]
    return jnp.moveaxis(tiles, 0, dim).reshape(lengths)


def turned_blocks(tiles, axes, order):
    lengths = [lax.axis_size(a) for a in axes]
    tiles = tiles.reshape(*lengths, *tiles.shape[1:])
    for k in order:
        tiles = lax.all_to_all(tiles, axes[k], split_axis=k, concat_axis=k, tiled=True)
    return tiles.reshape(-1, *tiles.shape[len(axes) :])


def exchange_by_chip(value, groups, order, split_dim, concat_dim):
    length = lax.axis_size(groups[0]) * lax.axis_size(groups[1])
    tiles = split_up(value, split_dim, length)
    return laid_out(turned_blocks(tiles, groups, order), concat_dim)


def in_one_piece(arrays, axis, split_dim, concat_dim, along):
    ends, at = ([], 0)
    for a in arrays[:-1]:
        at += a.shape[along]
        ends.append(at)
    both = jnp.concatenate(arrays, axis=along)
    return tuple(
        jnp.split(
            lax.all_to_all(both, axis, split_axis=split_dim, concat_axis=concat_dim, tiled=True),
            ends,
            axis=along,
        )
    )


def trig_tables(numbers, lon_count, lon_total, factor):
    longitudes = jnp.arange(lon_count, dtype=jnp.int32)
    phases = numbers[:, None] * longitudes[None, :] % lon_total
    angles = phases.astype(jnp.float32) * (2.0 * math.pi / lon_total)
    return (jnp.cos(angles) * factor, jnp.sin(angles) * factor)


def settle(tracer, courant):
    outflow = courant * tracer
    inflow = jnp.concatenate([jnp.zeros_like(outflow[:, :BINS]), outflow[:, :-BINS]], axis=1)
    return tracer - outflow + inflow


def settle_adjoint(adjoint, courant):
    below = jnp.concatenate([adjoint[:, BINS:], jnp.zeros_like(adjoint[:, :BINS])], axis=1)
    return adjoint + courant * (below - adjoint)


def departures(profile, levels, active, lidar_vals, aod_vals, weights, lidar_coef, aod_coef):
    chosen = (jnp.arange(LEV, dtype=jnp.int32)[None, :] == levels[:, None]).astype(profile.dtype)
    layered = profile.reshape(-1, LEV, BINS)
    at_level = jnp.sum(chosen[:, :, None] * layered, axis=1)
    lidar_model = jnp.sum(at_level * lidar_coef[None, :], axis=1)
    aod_model = jnp.sum(profile * aod_coef[None, :], axis=1)
    lidar_resid = active * weights * (lidar_model - lidar_vals)
    aod_resid = active * weights * (aod_model - aod_vals)
    spread = lidar_resid[:, None, None] * chosen[:, :, None] * lidar_coef[None, None, :]
    return spread.reshape(-1, LEV * BINS) + aod_resid[:, None] * aod_coef[None, :]


def synthesis_sum(cosine, sine_table, parts):
    return jnp.einsum("mo,mtc->tco", cosine, parts[..., 0], precision=highest) - jnp.einsum(
        "mo,mtc->tco", sine_table, parts[..., 1], precision=highest
    )


def analysis(cosine, sine_table, field):
    real_adj = jnp.einsum("mo,tco->mtc", cosine, field, precision=highest)
    imag_adj = -jnp.einsum("mo,tco->mtc", sine_table, field, precision=highest)
    stacked = jnp.stack([real_adj, imag_adj], axis=-1)
    return stacked.reshape(stacked.shape[0], stacked.shape[1], -1)


def body(
    control,
    spectral_scale,
    vertical_root,
    legendre,
    zonal_number,
    courant,
    lidar_coef,
    aod_coef,
    obs_count,
    obs_column,
    obs_level,
    lidar_obs,
    aod_obs,
    obs_weight,
):
    modes_here, waves_here, width = control.shape
    channels = width // 2
    wave_count = lax.axis_size(WAVE)
    band_count = lax.axis_size("band")
    lon_here = courant.shape[2]
    lon_total = lon_here * wave_count
    factor = MW ** (-0.5)
    paired = control.reshape(modes_here, waves_here, channels, 2)
    mixed = jnp.einsum("nmcp,cd->nmdp", paired, vertical_root, precision=highest).reshape(
        modes_here, waves_here, width
    )
    scaled = spectral_scale * mixed
    all_modes = lax.all_to_all(scaled, "band", split_axis=2, concat_axis=0, tiled=True)
    every_lat = jnp.einsum("mln,nmc->mlc", legendre, all_modes, precision=highest)
    spectral = lax.all_to_all(every_lat, "band", split_axis=1, concat_axis=2, tiled=True)
    received = lax.all_to_all(spectral, WAVE, split_axis=2, concat_axis=0, tiled=True)
    lat_items = received.shape[1]
    block_width = received.shape[2] // 2
    cosine, sine_table = trig_tables(zonal_number, lon_total, lon_total, factor)
    parts = received.reshape(received.shape[0], lat_items, block_width, 2)
    whole_row = synthesis_sum(cosine, sine_table, parts)
    tracer = exchange_by_chip(whole_row, ("wave_0", "wave_1"), (1, 0), 2, 1)
    for repeat in range(STEPS):
        tracer = settle(tracer, courant)
    devices = wave_count * band_count
    counts = obs_count.reshape(devices, 1)
    arrived = (
        *in_one_piece((counts, obs_column, obs_level), WAVE_BAND, 0, 0, 1),
        *in_one_piece((lidar_obs, aod_obs, obs_weight), WAVE_BAND, 0, 0, 1),
    )
    got_counts, columns, levels, lidar_vals, aod_vals, weights = arrived
    slot_count = columns.shape[1]
    active = (
        (jnp.arange(slot_count, dtype=jnp.int32)[None, :] < got_counts)
        .astype(jnp.float32)
        .reshape(-1)
    )
    lat_index = (columns // lon_here).reshape(-1)
    lon_index = (columns % lon_here).reshape(-1)
    profile = tracer[lat_index, :, lon_index]
    contrib = departures(
        profile,
        levels.reshape(-1),
        active,
        lidar_vals.reshape(-1),
        aod_vals.reshape(-1),
        weights.reshape(-1),
        lidar_coef,
        aod_coef,
    )
    adjoint = jnp.zeros_like(tracer).at[lat_index, :, lon_index].add(contrib)
    for repeat in range(STEPS):
        adjoint = settle_adjoint(adjoint, courant)
    cosine, sine_table = trig_tables(zonal_number, lon_total, lon_total, factor)
    modes = analysis(
        cosine, sine_table, lax.all_to_all(adjoint, WAVE, split_axis=1, concat_axis=2, tiled=True)
    )
    spectral_adj = lax.all_to_all(modes, WAVE, split_axis=0, concat_axis=2, tiled=True)
    all_lats = lax.all_to_all(spectral_adj, "band", split_axis=2, concat_axis=1, tiled=True)
    mode_block = jnp.einsum("mtn,mtc->nmc", legendre, all_lats, precision=highest)
    scaled_adj = lax.all_to_all(mode_block, "band", split_axis=0, concat_axis=2, tiled=True)
    mixed_adj = (spectral_scale * scaled_adj).reshape(modes_here, waves_here, channels, 2)
    control_adj = jnp.einsum("nmdp,cd->nmcp", mixed_adj, vertical_root, precision=highest).reshape(
        modes_here, waves_here, width
    )
    return (control + control_adj, tracer)


def solution(mesh):
    finer = Mesh(mesh.devices.reshape(4, 2, mesh.shape["band"]), ("wave_0", "wave_1", "band"))
    placed = (
        P("band", WAVE, None),
        P("band", WAVE, None),
        P(),
        P(WAVE, None, None),
        P(),
        P("band", None, WAVE),
        P(),
        P(),
        P(WAVE_BAND, None),
        P(WAVE_BAND, None),
        P(WAVE_BAND, None),
        P(WAVE_BAND, None),
        P(WAVE_BAND, None),
        P(WAVE_BAND, None),
    )
    return jax.shard_map(
        body,
        mesh=finer,
        in_specs=placed,
        out_specs=(P("band", WAVE, None), P("band", None, WAVE)),
        check_vma=False,
    )
```

profile of v0, /device:TPU:0, one launch (start us, length us, event | category | flops | bytes accessed | tf_op | source)
XLA Modules:
  0.0 684.6 jit_solution(10554722234789552446)
XLA Ops:
  14.1 17.5 %all_to_all.157 = f32[16,1,5376]{2,1,0:T(1,128)S(1)} all-to-all(f32[16,1,5376]{2,1,0:T(1,128)S(1)} %reshape.273), channel_id=1, replica_groups=mesh['wave_0'=4,'wave_1'=2,'band'=16] {'band'}, dimensions={0} | all-to-all | bytes 688128 | tf_op jit(solution)/shard_map/all_to_all | solution.py:132
  38.9 13.5 %convolution_bitcast_fusion = f32[28,448,12]{1,2,0:T(8,128)S(1)} fusion(f32[256,28,12]{0,2,1:T(8,128)S(1)} %copy.324, f32[28,448,256]{2,1,0:T(8,128)} %param.17), kind=kOutput, calls=%fused_computation.28 | convolution fusion | flops 462422016 | bytes 13791232 | tf_op jit(solution)/shard_map/mln,nmc->mlc/dot_general | solution.py:133
  55.1 4.5 reshape.275
  64.5 10.1 %all-to-all-done.3 = f32[16,1,9408]{2,1,0:T(1,128)S(1)} async-done(((f32[16,1,9408]{2,1,0:T(1,128)}), f32[16,1,9408]{2,1,0:T(1,128)S(1)}, u32[]{:S(2)}, u32[]{:S(2)}) %all-to-all-start.3) | async-done | bytes 602144 | tf_op jit(solution)/shard_map/all_to_all | solution.py:134
  75.4 7.0 %all-to-all-start = ((s32[128,1,257]{2,1,0:T(1,128)}), s32[128,1,257]{2,1,0:T(1,128)S(1)}, u32[]{:S(2)}, u32[]{:S(2)}) async-start(s32[128,1,257]{2,1,0:T(1,128)} %copy.314), calls=%async_computation | async-start | bytes 393216 | tf_op jit(solution)/shard_map/all_to_all | solution.py:54
  91.2 5.2 copy.327
  109.9 6.0 all-to-all-done.4
  124.0 4.9 copy.329
  134.6 4.9 fusion.21
  139.4 6.1 convolution_subtract_fusion
  149.9 5.7 all_to_all.158
  155.7 8.9 %all-to-all-start.1 = ((f32[128,1,384]{2,1,0:T(1,128)}), f32[128,1,384]{2,1,0:T(1,128)}, u32[]{:S(2)}, u32[]{:S(2)}) async-start(f32[128,1,384]{2,1,0:T(1,128)} %all_to_all.114), calls=%async_computation.1 | async-start | bytes 393216 | tf_op jit(solution)/shard_map/all_to_all | solution.py:54
  174.6 4.3 all-to-all-start.6
  182.2 15.6 %all-to-all-done.6 = f32[4,2,28,12,128]{4,1,3,2,0:T(2,128)} async-done(((f32[4,2,28,12,128]{4,1,3,2,0:T(2,128)}), f32[4,2,28,12,128]{4,1,3,2,0:T(2,128)}, u32[]{:S(2)}, u32[]{:S(2)}) %all-to-all-start.6) | async-done | bytes 1376288 | tf_op jit(solution)/shard_map/all_to_all | solution.py:36
  212.6 177.1 %gather_fusion = f32[16384,96]{1,0:T(8,128)} fusion(f32[28,96,128]{1,2,0:T(8,128)S(1)} %pad_add_fusion, s32[16384]{0:T(1024)S(1)} %bitcast.152), kind=kCustom, calls=%fused_computation | custom fusion | bytes 12713984 | tf_op jit(solution)/shard_map/gather | solution.py:159
  389.7 8.7 %copy.343 = f32[16384,96]{0,1:T(8,128)} copy(f32[16384,96]{1,0:T(8,128)} %gather_fusion) | data formatting | bytes 12582912 | tf_op jit(solution)/shard_map/gather | solution.py:159
  398.4 6.5 reshape.245
  408.4 4.7 multiply_reduce_fusion
  418.2 6.9 %mul.170 = f32[16384,96]{0,1:T(8,128)} reshape(f32[16384,8,12]{0,2,1:T(8,128)} %mul.169) | data formatting | bytes 12582912 | tf_op jit(solution)/shard_map/mul | solution.py:87
  425.1 6.3 multiply_add_fusion
  431.5 8.4 %copy.345 = f32[16384,96]{1,0:T(8,128)} copy(f32[16384,96]{0,1:T(8,128)} %multiply_add_fusion) | data formatting | bytes 12582912 | tf_op jit(solution)/shard_map/add | solution.py:88
  439.9 88.9 %scatter_custom_fusion = f32[3584,96]{1,0:T(8,128)} fusion(s32[16384]{0:T(1024)} %broadcast_select_fusion, f32[16384,96]{1,0:T(8,128)} %copy.345, f32[]{:T(128)} %constant.53.clone.1), kind=kCustom, calls=%fused_computation.44 | custom fusion | flops 1572864 | bytes 1376768
  538.0 24.4 %all_to_all.159 = f32[28,96,128]{2,0,1:T(8,128)S(1)} all-to-all(f32[28,96,128]{2,0,1:T(8,128)S(1)} %fusion.3), channel_id=1, replica_groups=mesh['wave_0'=4,'wave_1'=2,'band'=16] {'wave_0','wave_1'}, dimensions={1} | all-to-all | bytes 2752512 | tf_op jit(solution)/shard_map/all_to_all | solution.py:175
  564.8 6.3 fusion.14
  571.1 4.8 convolution_bitcast_fusion.2
  578.7 4.8 reshape.279
  583.5 13.6 %all_to_all.160 = f32[8,1,18816]{2,1,0:T(1,128)S(1)} all-to-all(f32[8,1,18816]{2,1,0:T(1,128)S(1)} %reshape.279), channel_id=1, replica_groups=mesh['wave_0'=4,'wave_1'=2,'band'=16] {'wave_0','wave_1'}, dimensions={0} | all-to-all | bytes 1204224 | tf_op jit(solution)/shard_map/all_to_all | solution.py:177
  599.2 5.0 reshape.280
  611.7 16.4 %all_to_all.161 = f32[16,1,9408]{2,1,0:T(1,128)S(1)} all-to-all(f32[16,1,9408]{2,1,0:T(1,128)S(1)} %reshape.281), channel_id=1, replica_groups=mesh['wave_0'=4,'wave_1'=2,'band'=16] {'band'}, dimensions={0} | all-to-all | bytes 1204224 | tf_op jit(solution)/shard_map/all_to_all | solution.py:178
  633.4 5.0 copy.375
  641.2 9.2 %convolution_bitcast_fusion.1 = f32[256,28,12]{0,2,1:T(8,128)S(1)} fusion(f32[28,448,12]{1,2,0:T(8,128)S(1)} %reshape.270, f32[28,448,256]{2,1,0:T(8,128)} %param.17), kind=kOutput, calls=%fused_computation.31 | convolution fusion | flops 462422016 | bytes 13791232 | tf_op jit(solution)/shard_map/mtn,mtc->nmc/dot_general | solution.py:179
  661.7 7.3 %all-to-all-done.10 = f32[16,1,5376]{2,1,0:T(1,128)S(1)} async-done(((f32[16,1,5376]{2,1,0:T(1,128)}), f32[16,1,5376]{2,1,0:T(1,128)S(1)}, u32[]{:S(2)}, u32[]{:S(2)}) %all-to-all-start.10) | async-done | bytes 344096 | tf_op jit(solution)/shard_map/all_to_all | solution.py:180
  (145 shorter events, 164.3 us)
Async XLA Ops:
  0.6 4.1 copy-start
  0.6 2.0 copy-start.14
  2.7 5.1 copy-start.4
  55.0 8.4 %copy-start.17 = (s32[128,128]{1,0:T(8,128)S(1)}, s32[128,128]{1,0:T(8,128)}, u32[]{:S(2)}) copy-start(s32[128,128]{1,0:T(8,128)} %param.24) | copy-start | bytes 196612
  55.0 8.5 %copy-start.18 = (s32[128,128]{1,0:T(8,128)S(1)}, s32[128,128]{1,0:T(8,128)}, u32[]{:S(2)}) copy-start(s32[128,128]{1,0:T(8,128)} %param.23) | copy-start | bytes 196612
  55.0 8.6 %copy-start.22 = (s32[1,128]{1,0:T(1,128)S(1)}, s32[1,128]{1,0:T(1,128)}, u32[]{:S(2)}) copy-start(s32[1,128]{1,0:T(1,128)} %param.22) | copy-start | bytes 1540
  59.6 22.8 %copy-start.2 = (f32[28,96,128]{2,1,0:T(8,128)S(1)}, f32[28,96,128]{2,1,0:T(8,128)}, u32[]{:S(2)}) copy-start(f32[28,96,128]{2,1,0:T(8,128)} %param.19) | copy-start | bytes 4128772
  59.6 15.0 %all-to-all-start.3 = ((f32[16,1,9408]{2,1,0:T(1,128)}), f32[16,1,9408]{2,1,0:T(1,128)S(1)}, u32[]{:S(2)}, u32[]{:S(2)}) async-start(f32[16,1,9408]{2,1,0:T(1,128)} %reshape.275), calls=%async_computation.3 | async-start | bytes 1212416 | tf_op jit(solution)/shard_map/all_to_all | solution.py:134
  74.6 0.8 copy-start.8
  75.4 25.2 %all-to-all-start = ((s32[128,1,257]{2,1,0:T(1,128)}), s32[128,1,257]{2,1,0:T(1,128)S(1)}, u32[]{:S(2)}, u32[]{:S(2)}) async-start(s32[128,1,257]{2,1,0:T(1,128)} %copy.314), calls=%async_computation | async-start | bytes 393216 | tf_op jit(solution)/shard_map/all_to_all | solution.py:54
  83.2 125.8 %copy-start.1 = (f32[28,96,128]{1,2,0:T(8,128)}, f32[28,96,128]{1,2,0:T(8,128)S(1)}, u32[]{:S(2)}) copy-start(f32[28,96,128]{1,2,0:T(8,128)S(1)} %copy.337) | copy-start | bytes 4128772
  96.4 8.4 %copy-start.19 = (f32[128,128]{1,0:T(8,128)S(1)}, f32[128,128]{1,0:T(8,128)}, u32[]{:S(2)}) copy-start(f32[128,128]{1,0:T(8,128)} %param.27) | copy-start | bytes 196612
  100.6 6.0 copy-start.21
  100.6 6.0 copy-start.11
  100.6 15.4 %all-to-all-start.4 = ((f32[8,1,18816]{2,1,0:T(1,128)}), f32[8,1,18816]{2,1,0:T(1,128)}, u32[]{:S(2)}, u32[]{:S(2)}) async-start(f32[8,1,18816]{2,1,0:T(1,128)} %reshape.277), calls=%async_computation.4 | async-start | bytes 1204224 | tf_op jit(solution)/shard_map/all_to_all | solution.py:135
  109.9 54.6 %copy-start.12 = (s32[128,128]{1,0:T(8,128)}, s32[128,128]{1,0:T(8,128)S(1)}, u32[]{:S(2)}) copy-start(s32[128,128]{1,0:T(8,128)S(1)} %copy.318) | copy-start | bytes 196612
  128.9 5.7 copy-start.25
  155.7 18.9 %all-to-all-start.1 = ((f32[128,1,384]{2,1,0:T(1,128)}), f32[128,1,384]{2,1,0:T(1,128)}, u32[]{:S(2)}, u32[]{:S(2)}) async-start(f32[128,1,384]{2,1,0:T(1,128)} %all_to_all.114), calls=%async_computation.1 | async-start | bytes 393216 | tf_op jit(solution)/shard_map/all_to_all | solution.py:54
  171.2 7.7 %copy-start.16 = (s32[128,128]{1,0:T(8,128)S(1)}, s32[128,128]{1,0:T(8,128)}, u32[]{:S(2)}) copy-start(s32[128,128]{1,0:T(8,128)} %copy.316) | copy-start | bytes 196612
  171.2 8.8 %copy-start.24 = (s32[2]{0:T(128)S(1)}, s32[2]{0:T(128)}, u32[]{:S(2)}) copy-start(s32[2]{0:T(128)} %constant.81) | copy-start | bytes 28
  171.2 9.1 %copy-start.23 = (s32[2]{0:T(128)S(1)}, s32[2]{0:T(128)}, u32[]{:S(2)}) copy-start(s32[2]{0:T(128)} %constant.84) | copy-start | bytes 28
  174.6 23.3 %all-to-all-start.6 = ((f32[4,2,28,12,128]{4,1,3,2,0:T(2,128)}), f32[4,2,28,12,128]{4,1,3,2,0:T(2,128)}, u32[]{:S(2)}, u32[]{:S(2)}) async-start(f32[4,2,28,12,128]{4,1,3,2,0:T(2,128)} %copy.334), calls=%async_computation.6 | async-start | bytes 2752512 | tf_op jit(solution)/shard_map/all_to_all | solution.py:36
  204.7 2.1 copy-start.3
  398.4 6.5 copy-start.20
  405.0 3.5 copy-start.9
  408.4 5.7 copy-start.13
  418.2 6.9 %copy-start.15 = (f32[16384]{0:T(1024)S(1)}, f32[16384]{0:T(1024)}, u32[]{:S(2)}) copy-start(f32[16384]{0:T(1024)} %get-tuple-element.24) | copy-start | bytes 196612
  531.8 1.8 copy-start.7
  564.8 6.3 copy-start.10
  656.4 12.6 %all-to-all-start.10 = ((f32[16,1,5376]{2,1,0:T(1,128)}), f32[16,1,5376]{2,1,0:T(1,128)S(1)}, u32[]{:S(2)}, u32[]{:S(2)}) async-start(f32[16,1,5376]{2,1,0:T(1,128)} %reshape.283), calls=%async_computation.10 | async-start | bytes 688128 | tf_op jit(solution)/shard_map/all_to_all | solution.py:180
  671.5 1.4 copy-start.6
  673.1 5.5 copy-start.5
where the time goes:
time: 692 us; the launch traced here: 685 us
  local copies, waits for them, and re-layouts  338 us (49%)
  other arithmetic  142 us (21%)
  blocking collectives  77.7 us (11%)
  matrix products  51 us (7%)
  waiting for transfers between devices  42.4 us (6%)
  starting transfers between devices  32 us (5%)
    gather x2, local copies, waits for them, and re-layouts, body(): profile = tracer[lat_index, :, lon_index]  186 us
    unnamed x4, other arithmetic  90.2 us
    unnamed x73, local copies, waits for them, and re-layouts  57.3 us
    all_to_all x1, blocking collectives, body(): lax.all_to_all(adjoint, WAVE, split_axis=1, concat_axis=2, tiled=True)  24.4 us
    all_to_all x1, blocking collectives, body(): lax.all_to_all(scaled, 'band', split_axis=2, concat_axis=0, tiled=True)  17.5 us
    all_to_all x1, blocking collectives, body(): lax.all_to_all(spectral_adj, 'band', split_axis=2, concat_axis=1, tiled=T...  16.4 us
    all_to_all x2, starting transfers between devices, in_one_piece(): lax.all_to_all(both, axis, split_axis=split_dim, concat_axis=concat_dim,...  15.9 us
    all_to_all x1, waiting for transfers between devices, turned_blocks(): lax.all_to_all(tiles, axes[k], split_axis=k, concat_axis=k, tiled=True)  15.6 us
  transfers between devices with their start and end apart: 6, of which 5 were waited for; matrix products, arithmetic and copies ran while one was open for 5% of the time, Pallas kernels for 0%

commit v1 on v0

v1 whole, which is shorter than its diff:
```python
import math

import jax
import jax.numpy as jnp
from jax import lax
from jax.experimental import pallas as pl
from jax.experimental.pallas import tpu as pltpu
from jax.sharding import PartitionSpec as P

MW = 224
LEV = 8
BINS = 12
CH = 96
STEPS = 4
WAVES = 8
BANDS = 16
DEVICES = 128
SLOT = 128
GROUPS = 7
NLON = 1024
NLAT = 448
NT = 256
FACTOR = MW ** (-0.5)
f32 = jnp.float32
bf16 = jnp.bfloat16
highest = lax.Precision.HIGHEST
LIMIT = 48 << 20


def params(**kw):
    return pltpu.CompilerParams(vmem_limit_bytes=LIMIT, **kw)


def split(x):
    hi = x.astype(bf16)
    return hi, (x - hi.astype(f32)).astype(bf16)


def mm(a, b):
    return lax.dot_general(a, b, (((1,), (0,)), ((), ())), preferred_element_type=f32)


def mm_nt(a, b):
    return lax.dot_general(a, b, (((1,), (1,)), ((), ())), preferred_element_type=f32)


def iota(shape, dim):
    return lax.broadcasted_iota(jnp.int32, shape, dim)


def turn(parts, axis, width):
    n = len(parts)
    size = parts[0].shape[axis]
    at = iota(parts[0].shape, axis)
    step = n // 2
    while step:
        keep = (at // (step * width)) % 2 == 0
        new = list(parts)
        for i in range(n):
            if (i // step) % 2 == 0:
                a, b = parts[i], parts[i + step]
                new[i] = jnp.where(keep, a, pltpu.roll(b, step * width, axis))
                new[i + step] = jnp.where(keep, pltpu.roll(a, size - step * width, axis), b)
        parts = new
        step //= 2
    return parts


def doubled_root(root):
    rows = (iota((2 * CH, CH), 0) // 2 == iota((2 * CH, CH), 1)).astype(f32)
    cols = (iota((CH, 2 * CH), 1) // 2 == iota((CH, 2 * CH), 0)).astype(f32)
    wide = jnp.dot(rows, root, precision=highest, preferred_element_type=f32)
    wide = jnp.dot(wide, cols, precision=highest, preferred_element_type=f32)
    same = iota((2 * CH, 2 * CH), 0) % 2 == iota((2 * CH, 2 * CH), 1) % 2
    return jnp.where(same, wide, 0.0)


def mix_kernel(control_ref, scale_ref, root_ref, out_ref):
    root = doubled_root(root_ref[...])
    rh, rl = split(root)
    tiles = []
    for m4 in range(4):
        x = jnp.concatenate([control_ref[4 * g + m4] for g in range(GROUPS)], axis=0)
        s = jnp.concatenate([scale_ref[4 * g + m4] for g in range(GROUPS)], axis=0)
        xh, xl = split(x)
        y = (mm(xh, rh) + mm(xl, rh) + mm(xh, rl)) * s
        y = jnp.concatenate([y, jnp.zeros((16, 2 * CH), f32)], axis=0)
        tiles.append(y.T.reshape(24, 8, 128))
    for j, z in enumerate(turn(tiles, 1, 2)):
        out_ref[:, j] = z


def legendre_kernel(modes_ref, table_ref, out_ref, x_ref, order_ref):
    g = pl.program_id(0)

    @pl.when(g == 0)
    def _():
        for half in range(2):
            for c in range(6):
                got = [modes_ref[8 * half + s, 8 * c : 8 * c + 8] for s in range(8)]
                for k, z in enumerate(turn(got, 1, 16)):
                    x_ref[k, 8 * c : 8 * c + 8, 128 * half : 128 * half + 128] = z
        order_ref[...] = lat_order()

    x = x_ref[g]
    slot = (iota((48, NT), 0) % 8) // 2
    acc = None
    for m4 in range(4):
        xh, xl = split(jnp.where(slot == m4, x, 0.0))
        th, tl = split(table_ref[m4])
        both = mm_nt(jnp.concatenate([xh, xl], axis=0), th)
        part = both[:48] + both[48:] + mm_nt(xh, tl)
        acc = part if acc is None else acc + part
    ah, al = split(acc)
    both = mm(jnp.concatenate([ah, al], axis=0), order_ref[...])
    out = both[:48] + both[48:]
    for q in range(4):
        for hc in range(2):
            out_ref[2 * q + hc] = out[24 * hc : 24 * hc + 24, 128 * q : 128 * q + 128]


def lat_order():
    at = iota((NLAT, 512), 1)
    lat = ((at // 8) % 16) * 28 + (at // 128) * 7 + at % 8
    return jnp.where((iota((NLAT, 512), 0) == lat) & (at % 8 < 7), 1.0, 0.0).astype(bf16)


def wave_table_kernel(number_ref, high_ref, low_ref):
    rows = 16
    half = NLON // 2
    row = iota((rows, MW), 0)
    slot = iota((rows, MW), 1)
    part = iota((rows, half), 0) % 2
    lon = iota((rows, half), 1)
    numbers = number_ref[...].astype(f32)
    coefs = [(-1.0) ** k / math.factorial(2 * k + 1) for k in range(6)]

    @pl.loop(0, 2 * MW // rows)
    def _(i):
        first = pl.multiple_of(i * rows, rows)
        mine = (row + first) // 2 == slot
        n = jnp.sum(jnp.where(mine, numbers, 0.0), axis=1, keepdims=True).astype(jnp.int32)
        phase = (n * lon + 256 * part) & (NLON - 1)
        turn_at = (jnp.abs(phase - half) - half // 2).astype(f32)
        y = turn_at * (2.0 * math.pi / NLON)
        y2 = y * y
        value = coefs[5]
        for k in range(4, -1, -1):
            value = value * y2 + coefs[k]
        value = value * y * FACTOR
        vh, vl = split(value)
        high_ref[pl.ds(first, rows), :half] = vh
        low_ref[pl.ds(first, rows), :half] = vl
        sign = (1 - 2 * (n & 1)).astype(f32)
        vh, vl = split(value * sign)
        high_ref[pl.ds(first, rows), half:] = vh
        low_ref[pl.ds(first, rows), half:] = vl


def synthesis_kernel(spec_ref, high_ref, low_ref, out_ref, lhs_ref):
    @pl.when(pl.program_id(0) == 0)
    def _():
        for c in range(3):
            s = spec_ref[:, :, c].reshape(2 * MW, 128).T
            sh, sl = split(s)
            lhs_ref[128 * c : 128 * c + 128] = sh
            lhs_ref[384 + 128 * c : 512 + 128 * c] = sl

    both = mm(lhs_ref[...], high_ref[...])
    out = both[:384] + both[384:] + mm(lhs_ref[:384], low_ref[...])
    for c in range(3):
        for w in range(2):
            tile = out[128 * c : 128 * c + 128, 128 * w : 128 * w + 128]
            out_ref[w, :, c] = tile.reshape(BANDS, 8, 128)


def analysis_kernel(grid_ref, high_ref, low_ref, out_ref, acc_ref):
    i = pl.program_id(0)
    for c in range(3):
        rows = jnp.concatenate(
            [grid_ref[w, :, c].reshape(128, 128) for w in range(2)], axis=1
        )
        gh, gl = split(rows)
        high = high_ref[...]
        part = mm_nt(high, gh) + mm_nt(high, gl) + mm_nt(low_ref[...], gh)

        @pl.when(i == 0)
        def _():
            acc_ref[c] = part

        @pl.when((i > 0) & (i < 3))
        def _():
            acc_ref[c] += part

        @pl.when(i == 3)
        def _():
            out_ref[:, :, c] = (acc_ref[c] + part).reshape(WAVES, GROUPS, 8, 128)


def legendre_adjoint_kernel(spec_ref, table_ref, out_ref, x_ref, order_ref):
    g = pl.program_id(0)

    @pl.when(g == 0)
    def _():
        order_ref[...] = lat_order()
        x_ref[GROUPS] = jnp.zeros((48, NT), f32)

    parts = []
    for hc in range(2):
        cols = [spec_ref[2 * q + hc].reshape(24, 128) for q in range(4)]
        parts.append(jnp.concatenate(cols, axis=1))
    s = jnp.concatenate(parts, axis=0)
    sh, sl = split(s)
    both = mm_nt(jnp.concatenate([sh, sl], axis=0), order_ref[...])
    x = both[:48] + both[48:]
    slot = (iota((48, NLAT), 0) % 8) // 2
    acc = None
    for m4 in range(4):
        xh, xl = split(jnp.where(slot == m4, x, 0.0))
        th, tl = split(table_ref[m4])
        both = mm(jnp.concatenate([xh, xl], axis=0), th)
        part = both[:48] + both[48:] + mm(xh, tl)
        acc = part if acc is None else acc + part
    x_ref[g] = acc

    @pl.when(g == GROUPS - 1)
    def _():
        for half in range(2):
            for c in range(6):
                got = [
                    x_ref[k, 8 * c : 8 * c + 8, 128 * half : 128 * half + 128]
                    for k in range(8)
                ]
                for s, z in enumerate(turn(got, 1, 16)):
                    out_ref[8 * half + s, 8 * c : 8 * c + 8] = z


def unmix_kernel(modes_ref, control_ref, scale_ref, root_ref, out_ref):
    root = doubled_root(root_ref[...])
    rh, rl = split(root)
    tiles = turn([modes_ref[:, j] for j in range(4)], 1, 2)
    for m4 in range(4):
        y = tiles[m4].reshape(2 * CH, 128).T[: 16 * GROUPS]
        s = jnp.concatenate([scale_ref[4 * g + m4] for g in range(GROUPS)], axis=0)
        yh, yl = split(y * s)
        z = mm_nt(yh, rh) + mm_nt(yl, rh) + mm_nt(yh, rl)
        for g in range(GROUPS):
            m = 4 * g + m4
            out_ref[m] = control_ref[m] + z[16 * g : 16 * g + 16]


def pack_kernel(count_ref, column_ref, level_ref, lidar_ref, aod_ref, weight_ref, out_ref):
    counts = jnp.broadcast_to(count_ref[...].astype(f32), (DEVICES, DEVICES)).T
    live = iota((DEVICES, SLOT), 1).astype(f32) < counts
    weight = jnp.where(live, weight_ref[...], 0.0)
    out_ref[:, 0, :] = column_ref[...].astype(f32)
    out_ref[:, 1, :] = level_ref[...].astype(f32)
    out_ref[:, 2, :] = weight
    out_ref[:, 3, :] = weight * lidar_ref[...]
    out_ref[:, 4, :] = weight * aod_ref[...]
    for k in range(5, 8):
        out_ref[:, k, :] = jnp.zeros((DEVICES, SLOT), f32)


def sums_kernel(obs_ref, out_ref, acc_ref):
    i = pl.program_id(0)
    count = obs_ref.shape[0]

    def line(k):
        return jnp.concatenate([obs_ref[s, k : k + 1, :] for s in range(count)], axis=1)

    wide = count * SLOT
    column = line(0).astype(jnp.int32)
    level = line(1).astype(jnp.int32)
    lat = column // 128
    lon = column % 128
    q = (lat >= 7).astype(jnp.int32) + (lat >= 14).astype(jnp.int32) + (lat >= 21).astype(jnp.int32)
    row = q * 64 + level * 8 + (lat - 7 * q)
    rows = jnp.where(iota((256, wide), 0) == row, 1.0, 0.0).astype(bf16)
    cols = jnp.where(iota((128, wide), 0) == lon, 1.0, 0.0).astype(bf16)
    values = []
    for k in range(2, 5):
        for v in split(line(k)):
            values.append(cols * v)
    part = mm_nt(rows, jnp.concatenate(values, axis=0))

    @pl.when(i == 0)
    def _():
        acc_ref[...] = part

    @pl.when(i > 0)
    def _():
        acc_ref[...] += part

    @pl.when(i == pl.num_programs(0) - 1)
    def _():
        for k in range(3):
            out_ref[k] = (
                acc_ref[:, 256 * k : 256 * k + 128] + acc_ref[:, 256 * k + 128 : 256 * k + 256]
            )


def grid_kernel(
    grid_ref, courant_ref, sums_ref, lidar_ref, aod_ref, state_ref, adjoint_ref, flow_ref, hold_ref
):
    for h in range(12):
        rows = [courant_ref[min(t, 6), 8 * h : 8 * h + 8] for t in range(8)]
        for j, z in enumerate(turn(rows, 0, 1)):
            flow_ref[8 * h + j] = z

    chains = [(b2, hc, c) for b2 in range(2) for hc in range(2) for c in range(3)]
    lidar_sum = [None] * LEV
    aod_sum = None
    for b2, hc, c in chains:
        bin_at = b2 * 6 + hc * 3 + c
        x = [grid_ref[0, hc, 2 * l + b2, c] for l in range(LEV)]
        flow = [flow_ref[BINS * l + bin_at] for l in range(LEV)]
        for step in range(STEPS):
            out = [flow[l] * x[l] for l in range(LEV)]
            x = [x[l] - out[l] if l == 0 else x[l] - out[l] + out[l - 1] for l in range(LEV)]
        coef = lidar_ref[bin_at]
        for l in range(LEV):
            hold_ref[BINS * l + bin_at] = x[l]
            lidar_sum[l] = x[l] * coef if lidar_sum[l] is None else lidar_sum[l] + x[l] * coef
            term = x[l] * aod_ref[BINS * l + bin_at]
            aod_sum = term if aod_sum is None else aod_sum + term

    for h in range(12):
        rows = turn([hold_ref[8 * h + j] for j in range(8)], 0, 1)
        for t in range(7):
            state_ref[t, 8 * h : 8 * h + 8] = rows[t]

    weight = [sums_ref[0, 8 * l : 8 * l + 8] for l in range(LEV)]
    lidar = [weight[l] * lidar_sum[l] - sums_ref[1, 8 * l : 8 * l + 8] for l in range(LEV)]
    aod = sum(weight[1:], weight[0]) * aod_sum
    for l in range(LEV):
        aod = aod - sums_ref[2, 8 * l : 8 * l + 8]
    for b2, hc, c in chains:
        bin_at = b2 * 6 + hc * 3 + c
        coef = lidar_ref[bin_at]
        flow = [flow_ref[BINS * l + bin_at] for l in range(LEV)]
        a = [lidar[l] * coef + aod * aod_ref[BINS * l + bin_at] for l in range(LEV)]
        for step in range(STEPS):
            a = [
                a[l] + flow[l] * ((a[l + 1] - a[l]) if l + 1 < LEV else -a[l]) for l in range(LEV)
            ]
        for l in range(LEV):
            adjoint_ref[0, hc, 2 * l + b2, c] = a[l]


def shape(*lengths, kind=f32):
    return jax.ShapeDtypeStruct(lengths, kind)


def whole(*lengths):
    return pl.BlockSpec(lengths, lambda *_: (0,) * len(lengths))


def cost(flops, size):
    return pl.CostEstimate(flops=flops, bytes_accessed=size, transcendentals=0)


def exchange(tiles, axis):
    return lax.all_to_all(tiles, axis, split_axis=0, concat_axis=0, tiled=True)


def observation_sums(counts, columns, levels, lidar_obs, aod_obs, weights):
    packed = pl.pallas_call(
        pack_kernel,
        out_shape=shape(DEVICES, 8, SLOT),
        compiler_params=params(),
        name="pack",
    )(counts, columns, levels, lidar_obs, aod_obs, weights)
    arrived = exchange(packed, ("wave", "band"))
    return pl.pallas_call(
        sums_kernel,
        grid=(16,),
        in_specs=[pl.BlockSpec((8, 8, SLOT), lambda i: (i, 0, 0))],
        out_specs=whole(3, 256, 128),
        out_shape=shape(3, 256, 128),
        scratch_shapes=[pltpu.VMEM((256, 768), f32)],
        compiler_params=params(dimension_semantics=("arbitrary",)),
        cost_estimate=cost(2 * 16384 * 256 * 768, 1 << 20),
        name="sums",
    )(arrived)


def body(
    control,
    spectral_scale,
    vertical_root,
    legendre,
    zonal_number,
    courant,
    lidar_coef,
    aod_coef,
    obs_count,
    obs_column,
    obs_level,
    lidar_obs,
    aod_obs,
    obs_weight,
):
    control = jnp.swapaxes(control, 0, 1)
    scale = jnp.swapaxes(spectral_scale, 0, 1)
    modes = pl.pallas_call(
        mix_kernel,
        out_shape=shape(24, 4, 8, 128),
        compiler_params=params(),
        cost_estimate=cost(6 * 448 * 192 * 192, 1 << 20),
        name="mix",
    )(control, scale, vertical_root)
    modes = exchange(modes.reshape(BANDS, 48, 128), "band")

    sums = observation_sums(obs_count, obs_column, obs_level, lidar_obs, aod_obs, obs_weight)
    high, low = pl.pallas_call(
        wave_table_kernel,
        out_shape=(shape(2 * MW, NLON, kind=bf16), shape(2 * MW, NLON, kind=bf16)),
        compiler_params=params(),
        cost_estimate=cost(20 * 448 * 1024, 2 << 20),
        name="wave_table",
    )(zonal_number.reshape(1, MW))

    legendre_cost = cost(6 * 28 * 448 * 256 * 48, 14 << 20)
    table_spec = pl.BlockSpec((4, NLAT, NT), lambda g: (g, 0, 0))
    in_order = params(dimension_semantics=("arbitrary",))
    legendre_scratch = [pltpu.VMEM((8, 48, NT), f32), pltpu.VMEM((NLAT, 512), bf16)]
    spec = pl.pallas_call(
        legendre_kernel,
        grid=(GROUPS,),
        in_specs=[whole(BANDS, 48, 128), table_spec],
        out_specs=pl.BlockSpec((WAVES, 24, 128), lambda g: (0, g, 0)),
        out_shape=shape(WAVES, 24 * GROUPS, 128),
        scratch_shapes=legendre_scratch,
        compiler_params=in_order,
        cost_estimate=legendre_cost,
        name="legendre",
    )(modes, legendre)
    spec = exchange(spec, "wave").reshape(WAVES, GROUPS, 3, 8, 128)

    wave_spec = pl.BlockSpec((2 * MW, 256), lambda i: (0, i))
    tile_spec = pl.BlockSpec((2, BANDS, 3, 8, 128), lambda i: (i, 0, 0, 0, 0))
    wave_cost = cost(6 * 384 * 448 * 1024, 4 << 20)
    grid = pl.pallas_call(
        synthesis_kernel,
        grid=(4,),
        in_specs=[whole(WAVES, GROUPS, 3, 8, 128), wave_spec, wave_spec],
        out_specs=tile_spec,
        out_shape=shape(WAVES, BANDS, 3, 8, 128),
        scratch_shapes=[pltpu.VMEM((768, 2 * MW), bf16)],
        compiler_params=in_order,
        cost_estimate=wave_cost,
        name="synthesis",
    )(spec, high, low)
    grid = exchange(grid.reshape(DEVICES, 24, 128), ("wave", "band"))

    block = pl.BlockSpec((1, 2, BANDS, 3, 8, 128), lambda q: (q, 0, 0, 0, 0, 0))
    field = pl.BlockSpec((7, CH, 128), lambda q: (q, 0, 0))
    scalars = pl.BlockSpec(memory_space=pltpu.SMEM)
    state, adjoint = pl.pallas_call(
        grid_kernel,
        grid=(4,),
        in_specs=[block, field, pl.BlockSpec((3, 64, 128), lambda q: (0, q, 0)), scalars, scalars],
        out_specs=(field, block),
        out_shape=(shape(28, CH, 128), shape(4, 2, BANDS, 3, 8, 128)),
        scratch_shapes=[pltpu.VMEM((CH, 8, 128), f32), pltpu.VMEM((CH, 8, 128), f32)],
        compiler_params=in_order,
        cost_estimate=cost(40 * 28 * 96 * 128, 6 << 20),
        name="grid_steps",
    )(grid.reshape(4, 2, BANDS, 3, 8, 128), courant, sums, lidar_coef, aod_coef)
    adjoint = exchange(adjoint.reshape(DEVICES, 24, 128), ("wave", "band"))

    spec = pl.pallas_call(
        analysis_kernel,
        grid=(4,),
        in_specs=[tile_spec, wave_spec, wave_spec],
        out_specs=whole(WAVES, GROUPS, 3, 8, 128),
        out_shape=shape(WAVES, GROUPS, 3, 8, 128),
        scratch_shapes=[pltpu.VMEM((3, 2 * MW, 128), f32)],
        compiler_params=in_order,
        cost_estimate=wave_cost,
        name="analysis",
    )(adjoint.reshape(WAVES, BANDS, 3, 8, 128), high, low)
    spec = exchange(spec.reshape(WAVES, 24 * GROUPS, 128), "wave")

    modes = pl.pallas_call(
        legendre_adjoint_kernel,
        grid=(GROUPS,),
        in_specs=[pl.BlockSpec((WAVES, 24, 128), lambda g: (0, g, 0)), table_spec],
        out_specs=whole(BANDS, 48, 128),
        out_shape=shape(BANDS, 48, 128),
        scratch_shapes=legendre_scratch,
        compiler_params=in_order,
        cost_estimate=legendre_cost,
        name="legendre_adjoint",
    )(spec, legendre)
    modes = exchange(modes, "band").reshape(24, 4, 8, 128)

    gradient = pl.pallas_call(
        unmix_kernel,
        out_shape=shape(28, 16, 192),
        compiler_params=params(),
        cost_estimate=cost(6 * 448 * 192 * 192, 1 << 20),
        name="unmix",
    )(modes, control, scale, vertical_root)
    return jnp.swapaxes(gradient, 0, 1), state


def solution(mesh):
    both = ("wave", "band")
    placed = (
        P("band", "wave", None),
        P("band", "wave", None),
        P(),
        P("wave", None, None),
        P(),
        P("band", None, "wave"),
        P(),
        P(),
        P(both, None),
        P(both, None),
        P(both, None),
        P(both, None),
        P(both, None),
        P(both, None),
    )
    return jax.shard_map(
        body,
        mesh=mesh,
        in_specs=placed,
        out_specs=(P("band", "wave", None), P("band", None, "wave")),
        check_vma=False,
    )
```

time: 692 us -> 180 us (0.26)
  local copies, waits for them, and re-layouts: 338 us -> 7.78 us
  other arithmetic: 142 us -> 0 us
  Pallas kernels: 0 us -> 55.4 us
  matrix products: 51 us -> 0 us
  starting transfers between devices: 32 us -> 13.9 us
  waiting for transfers between devices: 42.4 us -> 28 us
    gather x2 -> x0, local copies, waits for them, and re-layouts: 186 us -> none  [body(): profile = tracer[lat_index, :, lon_index]]
    unnamed x4 -> x0, other arithmetic: 90.2 us -> none
    pallas_call x0 -> x10, Pallas kernels: none -> 55.4 us  [the longest x1 12.3 us: observation_sums(): pl.pallas_call(sums_kernel, grid=(16,), in_specs=[pl.BlockSpec((8, 8, SLO...]
    dot_general x8 -> x0, matrix products: 51 us -> none  [the longest x1 13.5 us: body(): jnp.einsum('mln,nmc->mlc', legendre, all_modes, precision=highest)]
    unnamed x73 -> x40, local copies, waits for them, and re-layouts: 57.3 us -> 7.78 us
    all_to_all x16 -> x0, local copies, waits for them, and re-layouts: 36.8 us -> none  [the longest x2 7.78 us: body(): lax.all_to_all(spectral_adj, 'band', split_axis=2, concat_axis=1, tiled=T...]
    reshape x7 -> x0, local copies, waits for them, and re-layouts: 20.2 us -> none  [the longest x1 6.54 us: departures(): layered = profile.reshape(-1, LEV, BINS)]
    all_to_all x6 -> x3, starting transfers between devices: 32 us -> 13.9 us  [exchange(): return lax.all_to_all(tiles, axis, split_axis=0, concat_axis=0, tiled=True)]
  transfers between devices with their start and end apart: 6 -> 3, of which waited for: 5 -> 3; matrix products, arithmetic and copies ran while one was open for 5% -> 0% of each run, Pallas kernels for 0% -> 11%
where the time goes in v1:
time: 180 us; the launch traced here: 179 us
  blocking collectives  73.5 us (41%)
  Pallas kernels  55.4 us (31%)
  waiting for transfers between devices  28 us (16%)
  starting transfers between devices  13.9 us (8%)
  local copies, waits for them, and re-layouts  7.78 us (4%)
    all_to_all x4, blocking collectives, exchange(): return lax.all_to_all(tiles, axis, split_axis=0, concat_axis=0, tiled=True)  73.5 us
    all_to_all x3, waiting for transfers between devices, exchange(): return lax.all_to_all(tiles, axis, split_axis=0, concat_axis=0, tiled=True)  28 us
    all_to_all x3, starting transfers between devices, exchange(): return lax.all_to_all(tiles, axis, split_axis=0, concat_axis=0, tiled=True)  13.9 us
    pallas_call x1, Pallas kernels, observation_sums(): pl.pallas_call(sums_kernel, grid=(16,), in_specs=[pl.BlockSpec((8, 8, SLO...  12.3 us
    pallas_call x1, Pallas kernels, body(): pl.pallas_call(legendre_kernel, grid=(GROUPS,), in_specs=[whole(BANDS, 48...  11.7 us
    pallas_call x1, Pallas kernels, body(): pl.pallas_call(legendre_adjoint_kernel, grid=(GROUPS,), in_specs=[pl.Bloc...  10.6 us
    unnamed x40, local copies, waits for them, and re-layouts  7.78 us
    pallas_call x1, Pallas kernels, body(): pl.pallas_call(analysis_kernel, grid=(4,), in_specs=[tile_spec, wave_spec...  5.9 us
  transfers between devices with their start and end apart: 3, of which 3 were waited for; matrix products, arithmetic and copies ran while one was open for 0% of the time, Pallas kernels for 11%

profile of v1, /device:TPU:0, one launch (start us, length us, event | category | flops | bytes accessed | tf_op | source)
XLA Modules:
  0.0 179.4 jit_solution(974636765961168086)
XLA Ops:
  0.6 0.0 copy-start
  0.6 1.0 copy-done
  1.7 1.0 copy-done.2
  2.7 0.8 copy-done.9
  3.5 1.2 mix.1
  4.6 17.8 %all_to_all.35.modes_ref = f32[16,48,128]{2,1,0:T(8,128)S(1)} all-to-all(f32[16,48,128]{2,1,0:T(8,128)S(1)} %bitcast.22), channel_id=1, replica_groups=mesh['wave'=8,'band'=16] {'band'}, dimensions={0} | all-to-all | bytes 786432 | tf_op jit(solution)/shard_map/all_to_all | solution.py:364
  22.4 0.0 copy-start.15
  22.4 0.0 copy-start.16
  22.4 11.7 %legendre.1 = f32[8,168,128]{2,1,0:T(8,128)} custom-call(f32[16,48,128]{2,1,0:T(8,128)S(1)} %all_to_all.35.modes_ref, f32[28,448,256]{2,1,0:T(8,128)} %table_ref.3), custom_call_target="tpu_custom_call" | custom-call | flops 924844032 | bytes 14680064 | tf_op jit(solution)/shard_map/legendre/pallas_call | solution.py:428
  34.1 4.4 %all-to-all-start.1 = ((f32[8,168,128]{2,1,0:T(8,128)}), f32[8,168,128]{2,1,0:T(8,128)S(1)}, u32[]{:S(2)}, u32[]{:S(2)}) async-start(f32[8,168,128]{2,1,0:T(8,128)} %legendre.1), calls=%async_computation.1 | async-start | bytes 1376256 | tf_op jit(solution)/shard_map/all_to_all | solution.py:364
  38.6 1.1 pack.1
  39.7 11.0 %all-to-all-done.1 = f32[8,168,128]{2,1,0:T(8,128)S(1)} async-done(((f32[8,168,128]{2,1,0:T(8,128)}), f32[8,168,128]{2,1,0:T(8,128)S(1)}, u32[]{:S(2)}, u32[]{:S(2)}) %all-to-all-start.1) | async-done | bytes 688160 | tf_op jit(solution)/shard_map/all_to_all | solution.py:364
  50.6 4.9 %all-to-all-start.3 = ((f32[128,8,128]{2,1,0:T(8,128)}), f32[128,8,128]{2,1,0:T(8,128)S(1)}, u32[]{:S(2)}, u32[]{:S(2)}) async-start(f32[128,8,128]{2,1,0:T(8,128)} %pack.1), calls=%async_computation.3 | async-start | bytes 1048576 | tf_op jit(solution)/shard_map/all_to_all | solution.py:364
  55.5 3.5 %wave_table.1 = (bf16[448,1024]{1,0:T(8,128)(2,1)S(1)}, bf16[448,1024]{1,0:T(8,128)(2,1)S(1)}) custom-call(s32[1,224]{1,0:T(1,128)S(1)} %bitcast.23), custom_call_target="tpu_custom_call" | custom-call | flops 9175040 | bytes 2097152 | tf_op jit(solution)/shard_map/wave_table/pallas_call | solution.py:416
  59.0 3.4 %synthesis.1 = f32[8,16,3,8,128]{4,3,2,1,0:T(8,128)} custom-call(f32[8,7,3,8,128]{4,3,2,1,0:T(8,128)S(1)} %bitcast.14, bf16[448,1024]{1,0:T(8,128)(2,1)S(1)} %get-tuple-element.6.high_ref, bf16[448,1024]{1,0:T(8,128)(2,1)S(1)} %get-tuple-element.7.low_ref), custom_call_target="tpu_custom_call" | custom-call | flops 1056964608 | bytes 4194304 | tf_op jit(solution)/shard_map/synthesis/pallas_call | solution.py:444
  62.4 6.7 %all-to-all-done.3.obs_ref = f32[128,8,128]{2,1,0:T(8,128)S(1)} async-done(((f32[128,8,128]{2,1,0:T(8,128)}), f32[128,8,128]{2,1,0:T(8,128)S(1)}, u32[]{:S(2)}, u32[]{:S(2)}) %all-to-all-start.3) | async-done | bytes 524320 | tf_op jit(solution)/shard_map/all_to_all | solution.py:364
  69.1 0.8 copy-done.5
  69.9 4.6 %all-to-all-start.2 = ((f32[128,24,128]{2,1,0:T(8,128)}), f32[128,24,128]{2,1,0:T(8,128)S(1)}, u32[]{:S(2)}, u32[]{:S(2)}) async-start(f32[128,24,128]{2,1,0:T(8,128)} %bitcast.5), calls=%async_computation.2 | async-start | bytes 3145728 | tf_op jit(solution)/shard_map/all_to_all | solution.py:364
  74.6 1.0 copy-done.6
  75.6 12.3 %sums.1.sums_ref = f32[3,256,128]{2,1,0:T(8,128)S(1)} custom-call(f32[128,8,128]{2,1,0:T(8,128)S(1)} %copy-done.6), custom_call_target="tpu_custom_call" | custom-call | flops 6442450944 | bytes 1048576 | tf_op jit(solution)/shard_map/sums/pallas_call | solution.py:375
  87.9 0.0 copy-start.7
  87.9 0.7 copy-done.7
  88.7 10.4 %all-to-all-done.2 = f32[128,24,128]{2,1,0:T(8,128)S(1)} async-done(((f32[128,24,128]{2,1,0:T(8,128)}), f32[128,24,128]{2,1,0:T(8,128)S(1)}, u32[]{:S(2)}, u32[]{:S(2)}) %all-to-all-start.2) | async-done | bytes 1572896 | tf_op jit(solution)/shard_map/all_to_all | solution.py:364
  99.0 1.3 copy-done.4
  100.4 1.0 copy-done.8
  101.3 3.8 %grid_steps.1 = (f32[28,96,128]{2,1,0:T(8,128)}, f32[4,2,16,3,8,128]{5,4,3,2,1,0:T(8,128)S(1)}) custom-call(f32[4,2,16,3,8,128]{5,4,3,2,1,0:T(8,128)S(1)} %bitcast.12, f32[28,96,128]{2,1,0:T(8,128)S(1)} %copy-done.4, f32[3,256,128]{2,1,0:T(8,128)S(1)} %copy-done.8, f32[12]{0:T(128)S(1)} %copy-done.17, f32[96]{0:T(128)S(1)} %copy-done.18), custom_call_target="tpu_custom_call" | custom-call | flops 13762560 | bytes 6291456 | tf_op jit(solution)/shard_map/grid_steps/pallas_call | solution.py:460
  105.2 28.6 %all_to_all.36 = f32[128,24,128]{2,1,0:T(8,128)S(1)} all-to-all(f32[128,24,128]{2,1,0:T(8,128)S(1)} %bitcast.20), channel_id=1, replica_groups=mesh['wave'=8,'band'=16] {'wave','band'}, dimensions={0} | all-to-all | bytes 3145728 | tf_op jit(solution)/shard_map/all_to_all | solution.py:364
  133.8 5.9 %analysis.1 = f32[8,7,3,8,128]{4,3,2,1,0:T(8,128)S(1)} custom-call(f32[8,16,3,8,128]{4,3,2,1,0:T(8,128)S(1)} %bitcast.13, bf16[448,1024]{1,0:T(8,128)(2,1)S(1)} %get-tuple-element.6.high_ref, bf16[448,1024]{1,0:T(8,128)(2,1)S(1)} %get-tuple-element.7.low_ref), custom_call_target="tpu_custom_call" | custom-call | flops 1056964608 | bytes 4194304 | tf_op jit(solution)/shard_map/analysis/pallas_call | solution.py:473
  139.7 14.6 %all_to_all.37.spec_ref = f32[8,168,128]{2,1,0:T(8,128)S(1)} all-to-all(f32[8,168,128]{2,1,0:T(8,128)S(1)} %bitcast.15), channel_id=1, replica_groups=mesh['wave'=8,'band'=16] {'wave'}, dimensions={0} | all-to-all | bytes 1376256 | tf_op jit(solution)/shard_map/all_to_all | solution.py:364
  154.3 10.6 %legendre_adjoint.1 = f32[16,48,128]{2,1,0:T(8,128)S(1)} custom-call(f32[8,168,128]{2,1,0:T(8,128)S(1)} %all_to_all.37.spec_ref, f32[28,448,256]{2,1,0:T(8,128)} %table_ref.3), custom_call_target="tpu_custom_call" | custom-call | flops 924844032 | bytes 14680064 | tf_op jit(solution)/shard_map/legendre_adjoint/pallas_call | solution.py:486
  165.0 12.5 %all_to_all.38 = f32[16,48,128]{2,1,0:T(8,128)S(1)} all-to-all(f32[16,48,128]{2,1,0:T(8,128)S(1)} %legendre_adjoint.1), channel_id=1, replica_groups=mesh['wave'=8,'band'=16] {'band'}, dimensions={0} | all-to-all | bytes 786432 | tf_op jit(solution)/shard_map/all_to_all | solution.py:364
  177.4 2.0 %unmix.1 = f32[28,16,192]{2,1,0:T(8,128)} custom-call(f32[24,4,8,128]{3,2,1,0:T(8,128)S(1)} %bitcast.21, f32[28,16,192]{2,1,0:T(8,128)S(1)} %bitcast.17, f32[28,16,192]{2,1,0:T(8,128)S(1)} %bitcast.19, f32[96,96]{1,0:T(8,128)S(1)} %copy-done.10), custom_call_target="tpu_custom_call" | custom-call | flops 99090432 | bytes 1048576 | tf_op jit(solution)/shard_map/unmix/pallas_call | solution.py:499
  (28 shorter events, 0.1 us)
Async XLA Ops:
  0.6 1.0 copy-start
  1.7 1.0 copy-start.2
  2.7 0.8 copy-start.9
  22.4 16.1 %copy-start.11 = (s32[128,128]{1,0:T(8,128)S(1)}, s32[128,128]{1,0:T(8,128)}, u32[]{:S(2)}) copy-start(s32[128,128]{1,0:T(8,128)} %column_ref.1) | copy-start | bytes 196612
  22.4 16.1 %copy-start.12 = (s32[128,128]{1,0:T(8,128)S(1)}, s32[128,128]{1,0:T(8,128)}, u32[]{:S(2)}) copy-start(s32[128,128]{1,0:T(8,128)} %level_ref.1) | copy-start | bytes 196612
  22.4 16.1 %copy-start.13 = (f32[128,128]{1,0:T(8,128)S(1)}, f32[128,128]{1,0:T(8,128)}, u32[]{:S(2)}) copy-start(f32[128,128]{1,0:T(8,128)} %lidar_ref.2) | copy-start | bytes 196612
  22.4 16.2 %copy-start.14 = (f32[128,128]{1,0:T(8,128)S(1)}, f32[128,128]{1,0:T(8,128)}, u32[]{:S(2)}) copy-start(f32[128,128]{1,0:T(8,128)} %aod_ref.2) | copy-start | bytes 196612
  22.4 16.2 %copy-start.15 = (f32[128,128]{1,0:T(8,128)S(1)}, f32[128,128]{1,0:T(8,128)}, u32[]{:S(2)}) copy-start(f32[128,128]{1,0:T(8,128)} %weight_ref.1) | copy-start | bytes 196612
  22.4 16.2 %copy-start.16 = (s32[1,128]{1,0:T(1,128)S(1)}, s32[1,128]{1,0:T(1,128)}, u32[]{:S(2)}) copy-start(s32[1,128]{1,0:T(1,128)} %count_ref.1) | copy-start | bytes 1540
  34.1 21.4 %copy-start.19 = (s32[224]{0:T(256)S(1)}, s32[224]{0:T(256)}, u32[]{:S(2)}) copy-start(s32[224]{0:T(256)} %param.18) | copy-start | bytes 2692
  34.1 16.5 %all-to-all-start.1 = ((f32[8,168,128]{2,1,0:T(8,128)}), f32[8,168,128]{2,1,0:T(8,128)S(1)}, u32[]{:S(2)}, u32[]{:S(2)}) async-start(f32[8,168,128]{2,1,0:T(8,128)} %legendre.1), calls=%async_computation.1 | async-start | bytes 1376256 | tf_op jit(solution)/shard_map/all_to_all | solution.py:364
  50.6 18.5 %all-to-all-start.3 = ((f32[128,8,128]{2,1,0:T(8,128)}), f32[128,8,128]{2,1,0:T(8,128)S(1)}, u32[]{:S(2)}, u32[]{:S(2)}) async-start(f32[128,8,128]{2,1,0:T(8,128)} %pack.1), calls=%async_computation.3 | async-start | bytes 1048576 | tf_op jit(solution)/shard_map/all_to_all | solution.py:364
  69.1 0.8 copy-start.5
  69.9 29.1 %all-to-all-start.2 = ((f32[128,24,128]{2,1,0:T(8,128)}), f32[128,24,128]{2,1,0:T(8,128)S(1)}, u32[]{:S(2)}, u32[]{:S(2)}) async-start(f32[128,24,128]{2,1,0:T(8,128)} %bitcast.5), calls=%async_computation.2 | async-start | bytes 3145728 | tf_op jit(solution)/shard_map/all_to_all | solution.py:364
  74.5 1.0 copy-start.6
  75.6 23.4 %copy-start.17 = (f32[12]{0:T(128)S(1)}, f32[12]{0:T(128)}, u32[]{:S(2)}) copy-start(f32[12]{0:T(128)} %lidar_ref.3) | copy-start | bytes 148
  75.6 23.4 %copy-start.18 = (f32[96]{0:T(128)S(1)}, f32[96]{0:T(128)}, u32[]{:S(2)}) copy-start(f32[96]{0:T(128)} %aod_ref.3) | copy-start | bytes 1156
  87.9 0.7 copy-start.7
  99.0 1.3 copy-start.4
  100.4 1.0 copy-start.8
  154.3 23.1 %copy-start.1 = (f32[16,28,192]{2,0,1:T(8,128)S(1)}, f32[16,28,192]{2,0,1:T(8,128)}, u32[]{:S(2)}) copy-start(f32[16,28,192]{2,0,1:T(8,128)} %param.14) | copy-start | bytes 1032196
  154.3 23.1 %copy-start.3 = (f32[16,28,192]{2,0,1:T(8,128)S(1)}, f32[16,28,192]{2,0,1:T(8,128)}, u32[]{:S(2)}) copy-start(f32[16,28,192]{2,0,1:T(8,128)} %param.15) | copy-start | bytes 1032196
  154.3 23.1 %copy-start.10 = (f32[96,96]{1,0:T(8,128)S(1)}, f32[96,96]{1,0:T(8,128)}, u32[]{:S(2)}) copy-start(f32[96,96]{1,0:T(8,128)} %root_ref.3) | copy-start | bytes 110596

commit v2 on v1

--- a/solution.py
+++ b/solution.py
@@ -24,7 +24,7 @@
 f32 = jnp.float32
 bf16 = jnp.bfloat16
 highest = lax.Precision.HIGHEST
-LIMIT = 48 << 20
+LIMIT = 24 << 20
 
 
 def params(**kw):
@@ -75,7 +75,46 @@
     return jnp.where(same, wide, 0.0)
 
 
-def mix_kernel(control_ref, scale_ref, root_ref, out_ref):
+def mix_kernel(
+    control_hbm,
+    scale_hbm,
+    root_hbm,
+    column_hbm,
+    level_hbm,
+    lidar_hbm,
+    aod_hbm,
+    weight_hbm,
+    count_hbm,
+    out_ref,
+    control_ref,
+    scale_ref,
+    root_ref,
+    index_ref,
+    value_ref,
+    count_ref,
+    obs_ref,
+    sem,
+):
+    copies = [
+        pltpu.make_async_copy(source, target, sem.at[k])
+        for k, (source, target) in enumerate(
+            (
+                (root_hbm, root_ref),
+                (control_hbm, control_ref),
+                (scale_hbm, scale_ref),
+                (column_hbm, index_ref.at[0]),
+                (level_hbm, index_ref.at[1]),
+                (lidar_hbm, value_ref.at[0]),
+                (aod_hbm, value_ref.at[1]),
+                (weight_hbm, value_ref.at[2]),
+                (count_hbm, count_ref),
+            )
+        )
+    ]
+    for copy in copies:
+        copy.start()
+    for copy in copies[:3]:
+        copy.wait()
     root = doubled_root(root_ref[...])
     rh, rl = split(root)
     tiles = []
@@ -87,36 +126,72 @@
         y = jnp.concatenate([y, jnp.zeros((16, 2 * CH), f32)], axis=0)
         tiles.append(y.T.reshape(24, 8, 128))
     for j, z in enumerate(turn(tiles, 1, 2)):
-        out_ref[:, j] = z
-
-
-def legendre_kernel(modes_ref, table_ref, out_ref, x_ref, order_ref):
-    g = pl.program_id(0)
-
-    @pl.when(g == 0)
-    def _():
+        for h in range(24):
+            c = 4 * h + j
+            out_ref[c // 6, 8 * (c % 6) : 8 * (c % 6) + 8] = z[h]
+
+    for copy in copies[3:]:
+        copy.wait()
+    counts = jnp.broadcast_to(count_ref[...].astype(f32), (DEVICES, DEVICES)).T
+    live = iota((DEVICES, SLOT), 1).astype(f32) < counts
+    weight = jnp.where(live, value_ref[2], 0.0)
+    obs_ref[0] = index_ref[0].astype(f32)
+    obs_ref[1] = index_ref[1].astype(f32)
+    obs_ref[2] = weight
+    obs_ref[3] = weight * value_ref[0]
+    obs_ref[4] = weight * value_ref[1]
+    for band in range(BANDS):
+        for k in range(5):
+            rows = obs_ref[k, pl.ds(band, WAVES, stride=BANDS), :]
+            out_ref[band, 48 + 8 * k : 56 + 8 * k] = rows
+
+
+def table_copies(table_hbm, table_ref, sem):
+    copies = [
+        pltpu.make_async_copy(table_hbm.at[m], table_ref.at[m], sem.at[m])
+        for m in range(4 * GROUPS)
+    ]
+    for copy in copies:
+        copy.start()
+    return copies
+
+
+def legendre_kernel(modes_ref, table_hbm, out_ref, acc_ref, table_ref, sem):
+    copies = table_copies(table_hbm, table_ref, sem)
+    x = [[None] * 12 for g in range(8)]
+    for half in range(2):
+        for c in range(6):
+            got = [modes_ref[8 * half + s, 8 * c : 8 * c + 8] for s in range(8)]
+            for g, z in enumerate(turn(got, 1, 16)):
+                x[g][6 * half + c] = z
+    for k in range(5):
         for half in range(2):
-            for c in range(6):
-                got = [modes_ref[8 * half + s, 8 * c : 8 * c + 8] for s in range(8)]
-                for k, z in enumerate(turn(got, 1, 16)):
-                    x_ref[k, 8 * c : 8 * c + 8, 128 * half : 128 * half + 128] = z
-        order_ref[...] = lat_order()
-
-    x = x_ref[g]
+            got = [modes_ref[8 * half + s, 48 + 8 * k : 56 + 8 * k] for s in range(8)]
+            at = 168 + 16 * k + 8 * half
+            for w, z in enumerate(turn(got, 0, 1)):
+                out_ref[w, at : at + 8] = z
+
     slot = (iota((48, NT), 0) % 8) // 2
-    acc = None
-    for m4 in range(4):
-        xh, xl = split(jnp.where(slot == m4, x, 0.0))
-        th, tl = split(table_ref[m4])
-        both = mm_nt(jnp.concatenate([xh, xl], axis=0), th)
-        part = both[:48] + both[48:] + mm_nt(xh, tl)
-        acc = part if acc is None else acc + part
-    ah, al = split(acc)
-    both = mm(jnp.concatenate([ah, al], axis=0), order_ref[...])
-    out = both[:48] + both[48:]
+    for g in range(GROUPS):
+        halves = [jnp.concatenate(x[g][6 * h : 6 * h + 6], axis=0) for h in range(2)]
+        mine = jnp.concatenate(halves, axis=1)
+        acc = None
+        for m4 in range(4):
+            xh, xl = split(jnp.where(slot == m4, mine, 0.0))
+            copies[4 * g + m4].wait()
+            th, tl = split(table_ref[4 * g + m4])
+            both = mm_nt(jnp.concatenate([xh, xl], axis=0), th)
+            part = both[:48] + both[48:] + mm_nt(xh, tl)
+            acc = part if acc is None else acc + part
+        for hc in range(2):
+            at = 168 * hc + 24 * g
+            acc_ref[at : at + 24] = acc[24 * hc : 24 * hc + 24]
+    ah, al = split(acc_ref[...])
+    order = lat_order()
+    out = mm(ah, order) + mm(al, order)
     for q in range(4):
         for hc in range(2):
-            out_ref[2 * q + hc] = out[24 * hc : 24 * hc + 24, 128 * q : 128 * q + 128]
+            out_ref[2 * q + hc, :168] = out[168 * hc : 168 * hc + 168, 128 * q : 128 * q + 128]
 
 
 def lat_order():
@@ -160,8 +235,9 @@
 def synthesis_kernel(spec_ref, high_ref, low_ref, out_ref, lhs_ref):
     @pl.when(pl.program_id(0) == 0)
     def _():
+        rows = spec_ref[:, :168].reshape(WAVES, GROUPS, 3, 8, 128)
         for c in range(3):
-            s = spec_ref[:, :, c].reshape(2 * MW, 128).T
+            s = rows[:, :, c].reshape(2 * MW, 128).T
             sh, sl = split(s)
             lhs_ref[128 * c : 128 * c + 128] = sh
             lhs_ref[384 + 128 * c : 512 + 128 * c] = sl
@@ -176,63 +252,57 @@
 
 def analysis_kernel(grid_ref, high_ref, low_ref, out_ref, acc_ref):
     i = pl.program_id(0)
+    tiles = []
     for c in range(3):
-        rows = jnp.concatenate(
-            [grid_ref[w, :, c].reshape(128, 128) for w in range(2)], axis=1
-        )
-        gh, gl = split(rows)
-        high = high_ref[...]
-        part = mm_nt(high, gh) + mm_nt(high, gl) + mm_nt(low_ref[...], gh)
-
-        @pl.when(i == 0)
-        def _():
-            acc_ref[c] = part
-
-        @pl.when((i > 0) & (i < 3))
-        def _():
-            acc_ref[c] += part
-
-        @pl.when(i == 3)
-        def _():
-            out_ref[:, :, c] = (acc_ref[c] + part).reshape(WAVES, GROUPS, 8, 128)
-
-
-def legendre_adjoint_kernel(spec_ref, table_ref, out_ref, x_ref, order_ref):
-    g = pl.program_id(0)
-
-    @pl.when(g == 0)
+        parts = [grid_ref[w, :, c].reshape(128, 128) for w in range(2)]
+        tiles.append(jnp.concatenate(parts, axis=1))
+    gh, gl = split(jnp.concatenate(tiles, axis=0))
+    both = mm_nt(high_ref[...], jnp.concatenate([gh, gl], axis=0))
+    part = both[:, :384] + both[:, 384:] + mm_nt(low_ref[...], gh)
+
+    @pl.when(i == 0)
     def _():
-        order_ref[...] = lat_order()
-        x_ref[GROUPS] = jnp.zeros((48, NT), f32)
-
-    parts = []
+        acc_ref[...] = part
+
+    @pl.when((i > 0) & (i < 3))
+    def _():
+        acc_ref[...] += part
+
+    @pl.when(i == 3)
+    def _():
+        total = acc_ref[...] + part
+        for c in range(3):
+            rows = total[:, 128 * c : 128 * c + 128]
+            out_ref[:, :, c] = rows.reshape(WAVES, GROUPS, 8, 128)
+
+
+def legendre_adjoint_kernel(spec_ref, table_hbm, out_ref, acc_ref, table_ref, sem):
+    copies = table_copies(table_hbm, table_ref, sem)
+    order = lat_order()
     for hc in range(2):
-        cols = [spec_ref[2 * q + hc].reshape(24, 128) for q in range(4)]
-        parts.append(jnp.concatenate(cols, axis=1))
-    s = jnp.concatenate(parts, axis=0)
-    sh, sl = split(s)
-    both = mm_nt(jnp.concatenate([sh, sl], axis=0), order_ref[...])
-    x = both[:48] + both[48:]
+        s = jnp.concatenate([spec_ref[2 * q + hc] for q in range(4)], axis=1)
+        sh, sl = split(s)
+        acc_ref[168 * hc : 168 * hc + 168] = mm_nt(sh, order) + mm_nt(sl, order)
     slot = (iota((48, NLAT), 0) % 8) // 2
-    acc = None
-    for m4 in range(4):
-        xh, xl = split(jnp.where(slot == m4, x, 0.0))
-        th, tl = split(table_ref[m4])
-        both = mm(jnp.concatenate([xh, xl], axis=0), th)
-        part = both[:48] + both[48:] + mm(xh, tl)
-        acc = part if acc is None else acc + part
-    x_ref[g] = acc
-
-    @pl.when(g == GROUPS - 1)
-    def _():
-        for half in range(2):
-            for c in range(6):
-                got = [
-                    x_ref[k, 8 * c : 8 * c + 8, 128 * half : 128 * half + 128]
-                    for k in range(8)
-                ]
-                for s, z in enumerate(turn(got, 1, 16)):
-                    out_ref[8 * half + s, 8 * c : 8 * c + 8] = z
+    x = []
+    for g in range(GROUPS):
+        rows = [acc_ref[168 * hc + 24 * g : 168 * hc + 24 * g + 24] for hc in range(2)]
+        mine = jnp.concatenate(rows, axis=0)
+        acc = None
+        for m4 in range(4):
+            xh, xl = split(jnp.where(slot == m4, mine, 0.0))
+            copies[4 * g + m4].wait()
+            th, tl = split(table_ref[4 * g + m4])
+            both = mm(jnp.concatenate([xh, xl], axis=0), th)
+            part = both[:48] + both[48:] + mm(xh, tl)
+            acc = part if acc is None else acc + part
+        x.append(acc)
+    x.append(jnp.zeros((48, NT), f32))
+    for half in range(2):
+        for c in range(6):
+            got = [v[8 * c : 8 * c + 8, 128 * half : 128 * half + 128] for v in x]
+            for s, z in enumerate(turn(got, 1, 16)):
+                out_ref[8 * half + s, 8 * c : 8 * c + 8] = z
 
 
 def unmix_kernel(modes_ref, control_ref, scale_ref, root_ref, out_ref):
@@ -249,40 +319,30 @@
             out_ref[m] = control_ref[m] + z[16 * g : 16 * g + 16]
 
 
-def pack_kernel(count_ref, column_ref, level_ref, lidar_ref, aod_ref, weight_ref, out_ref):
-    counts = jnp.broadcast_to(count_ref[...].astype(f32), (DEVICES, DEVICES)).T
-    live = iota((DEVICES, SLOT), 1).astype(f32) < counts
-    weight = jnp.where(live, weight_ref[...], 0.0)
-    out_ref[:, 0, :] = column_ref[...].astype(f32)
-    out_ref[:, 1, :] = level_ref[...].astype(f32)
-    out_ref[:, 2, :] = weight
-    out_ref[:, 3, :] = weight * lidar_ref[...]
-    out_ref[:, 4, :] = weight * aod_ref[...]
-    for k in range(5, 8):
-        out_ref[:, k, :] = jnp.zeros((DEVICES, SLOT), f32)
-
-
 def sums_kernel(obs_ref, out_ref, acc_ref):
     i = pl.program_id(0)
-    count = obs_ref.shape[0]
-
-    def line(k):
-        return jnp.concatenate([obs_ref[s, k : k + 1, :] for s in range(count)], axis=1)
-
-    wide = count * SLOT
-    column = line(0).astype(jnp.int32)
-    level = line(1).astype(jnp.int32)
-    lat = column // 128
-    lon = column % 128
-    q = (lat >= 7).astype(jnp.int32) + (lat >= 14).astype(jnp.int32) + (lat >= 21).astype(jnp.int32)
-    row = q * 64 + level * 8 + (lat - 7 * q)
-    rows = jnp.where(iota((256, wide), 0) == row, 1.0, 0.0).astype(bf16)
-    cols = jnp.where(iota((128, wide), 0) == lon, 1.0, 0.0).astype(bf16)
-    values = []
-    for k in range(2, 5):
-        for v in split(line(k)):
-            values.append(cols * v)
-    part = mm_nt(rows, jnp.concatenate(values, axis=0))
+    part = None
+    for half in range(2):
+
+        def line(k):
+            at = 168 + 16 * k + 8 * half
+            rows = obs_ref[0, at : at + 8]
+            return jnp.concatenate([rows[s : s + 1] for s in range(8)], axis=1)
+
+        column = line(0).astype(jnp.int32)
+        level = line(1).astype(jnp.int32)
+        lat = column // 128
+        lon = column % 128
+        q = sum((lat >= 7 * k).astype(jnp.int32) for k in range(1, 4))
+        row = q * 64 + level * 8 + (lat - 7 * q)
+        rows = jnp.where(iota((256, 1024), 0) == row, 1.0, 0.0).astype(bf16)
+        cols = jnp.where(iota((128, 1024), 0) == lon, 1.0, 0.0).astype(bf16)
+        values = []
+        for k in range(2, 5):
+            for v in split(line(k)):
+                values.append(cols * v)
+        new = mm_nt(rows, jnp.concatenate(values, axis=0))
+        part = new if part is None else part + new
 
     @pl.when(i == 0)
     def _():
@@ -292,12 +352,11 @@
     def _():
         acc_ref[...] += part
 
-    @pl.when(i == pl.num_programs(0) - 1)
+    @pl.when(i == WAVES - 1)
     def _():
         for k in range(3):
-            out_ref[k] = (
-                acc_ref[:, 256 * k : 256 * k + 128] + acc_ref[:, 256 * k + 128 : 256 * k + 256]
-            )
+            first = acc_ref[:, 256 * k : 256 * k + 128]
+            out_ref[k] = first + acc_ref[:, 256 * k + 128 : 256 * k + 256]
 
 
 def grid_kernel(
@@ -356,33 +415,16 @@
     return pl.BlockSpec(lengths, lambda *_: (0,) * len(lengths))
 
 
+def in_hbm(x):
+    return pltpu.with_memory_space_constraint(x, pltpu.HBM)
+
+
 def cost(flops, size):
     return pl.CostEstimate(flops=flops, bytes_accessed=size, transcendentals=0)
 
 
 def exchange(tiles, axis):
     return lax.all_to_all(tiles, axis, split_axis=0, concat_axis=0, tiled=True)
-
-
-def observation_sums(counts, columns, levels, lidar_obs, aod_obs, weights):
-    packed = pl.pallas_call(
-        pack_kernel,
-        out_shape=shape(DEVICES, 8, SLOT),
-        compiler_params=params(),
-        name="pack",
-    )(counts, columns, levels, lidar_obs, aod_obs, weights)
-    arrived = exchange(packed, ("wave", "band"))
-    return pl.pallas_call(
-        sums_kernel,
-        grid=(16,),
-        in_specs=[pl.BlockSpec((8, 8, SLOT), lambda i: (i, 0, 0))],
-        out_specs=whole(3, 256, 128),
-        out_shape=shape(3, 256, 128),
-        scratch_shapes=[pltpu.VMEM((256, 768), f32)],
-        compiler_params=params(dimension_semantics=("arbitrary",)),
-        cost_estimate=cost(2 * 16384 * 256 * 768, 1 << 20),
-        name="sums",
-    )(arrived)
 
 
 def body(
@@ -403,16 +445,43 @@
 ):
     control = jnp.swapaxes(control, 0, 1)
     scale = jnp.swapaxes(spectral_scale, 0, 1)
+    hbm = pl.BlockSpec(memory_space=pltpu.HBM)
     modes = pl.pallas_call(
         mix_kernel,
-        out_shape=shape(24, 4, 8, 128),
+        in_specs=[hbm] * 9,
+        out_specs=whole(BANDS, 88, 128),
+        out_shape=shape(BANDS, 88, 128),
+        scratch_shapes=[
+            pltpu.VMEM((28, 16, 192), f32),
+            pltpu.VMEM((28, 16, 192), f32),
+            pltpu.VMEM((CH, CH), f32),
+            pltpu.VMEM((2, DEVICES, SLOT), jnp.int32),
+            pltpu.VMEM((3, DEVICES, SLOT), f32),
+            pltpu.VMEM((1, DEVICES), jnp.int32),
+            pltpu.VMEM((5, DEVICES, SLOT), f32),
+            pltpu.SemaphoreType.DMA((9,)),
+        ],
         compiler_params=params(),
         cost_estimate=cost(6 * 448 * 192 * 192, 1 << 20),
         name="mix",
-    )(control, scale, vertical_root)
-    modes = exchange(modes.reshape(BANDS, 48, 128), "band")
-
-    sums = observation_sums(obs_count, obs_column, obs_level, lidar_obs, aod_obs, obs_weight)
+    )(
+        *(
+            in_hbm(x)
+            for x in (
+                control,
+                scale,
+                vertical_root,
+                obs_column,
+                obs_level,
+                lidar_obs,
+                aod_obs,
+                obs_weight,
+                obs_count,
+            )
+        )
+    )
+    modes = exchange(modes, "band")
+
     high, low = pl.pallas_call(
         wave_table_kernel,
         out_shape=(shape(2 * MW, NLON, kind=bf16), shape(2 * MW, NLON, kind=bf16)),
@@ -422,21 +491,34 @@
     )(zonal_number.reshape(1, MW))
 
     legendre_cost = cost(6 * 28 * 448 * 256 * 48, 14 << 20)
-    table_spec = pl.BlockSpec((4, NLAT, NT), lambda g: (g, 0, 0))
     in_order = params(dimension_semantics=("arbitrary",))
-    legendre_scratch = [pltpu.VMEM((8, 48, NT), f32), pltpu.VMEM((NLAT, 512), bf16)]
+    legendre_scratch = [
+        pltpu.VMEM((336, NLAT), f32),
+        pltpu.VMEM((28, NLAT, NT), f32),
+        pltpu.SemaphoreType.DMA((28,)),
+    ]
     spec = pl.pallas_call(
         legendre_kernel,
-        grid=(GROUPS,),
-        in_specs=[whole(BANDS, 48, 128), table_spec],
-        out_specs=pl.BlockSpec((WAVES, 24, 128), lambda g: (0, g, 0)),
-        out_shape=shape(WAVES, 24 * GROUPS, 128),
+        in_specs=[whole(BANDS, 88, 128), hbm],
+        out_specs=whole(WAVES, 248, 128),
+        out_shape=shape(WAVES, 248, 128),
         scratch_shapes=legendre_scratch,
-        compiler_params=in_order,
+        compiler_params=params(),
         cost_estimate=legendre_cost,
         name="legendre",
-    )(modes, legendre)
-    spec = exchange(spec, "wave").reshape(WAVES, GROUPS, 3, 8, 128)
+    )(modes, in_hbm(legendre))
+    spec = exchange(spec, "wave")
+    sums = pl.pallas_call(
+        sums_kernel,
+        grid=(WAVES,),
+        in_specs=[pl.BlockSpec((1, 248, 128), lambda i: (i, 0, 0))],
+        out_specs=whole(3, 256, 128),
+        out_shape=shape(3, 256, 128),
+        scratch_shapes=[pltpu.VMEM((256, 768), f32)],
+        compiler_params=in_order,
+        cost_estimate=cost(2 * 16384 * 256 * 768, 1 << 20),
+        name="sums",
+    )(spec)
 
     wave_spec = pl.BlockSpec((2 * MW, 256), lambda i: (0, i))
     tile_spec = pl.BlockSpec((2, BANDS, 3, 8, 128), lambda i: (i, 0, 0, 0, 0))
@@ -444,7 +526,7 @@
     grid = pl.pallas_call(
         synthesis_kernel,
         grid=(4,),
-        in_specs=[whole(WAVES, GROUPS, 3, 8, 128), wave_spec, wave_spec],
+        in_specs=[whole(WAVES, 248, 128), wave_spec, wave_spec],
         out_specs=tile_spec,
         out_shape=shape(WAVES, BANDS, 3, 8, 128),
         scratch_shapes=[pltpu.VMEM((768, 2 * MW), bf16)],
@@ -467,7 +549,7 @@
         compiler_params=in_order,
         cost_estimate=cost(40 * 28 * 96 * 128, 6 << 20),
         name="grid_steps",
-    )(grid.reshape(4, 2, BANDS, 3, 8, 128), courant, sums, lidar_coef, aod_coef)
+    )(grid.reshape(4, 2, BANDS, 3, 8, 128), in_hbm(courant), in_hbm(sums), lidar_coef, aod_coef)
     adjoint = exchange(adjoint.reshape(DEVICES, 24, 128), ("wave", "band"))
 
     spec = pl.pallas_call(
@@ -476,7 +558,7 @@
         in_specs=[tile_spec, wave_spec, wave_spec],
         out_specs=whole(WAVES, GROUPS, 3, 8, 128),
         out_shape=shape(WAVES, GROUPS, 3, 8, 128),
-        scratch_shapes=[pltpu.VMEM((3, 2 * MW, 128), f32)],
+        scratch_shapes=[pltpu.VMEM((2 * MW, 384), f32)],
         compiler_params=in_order,
         cost_estimate=wave_cost,
         name="analysis",
@@ -485,15 +567,14 @@
 
     modes = pl.pallas_call(
         legendre_adjoint_kernel,
-        grid=(GROUPS,),
-        in_specs=[pl.BlockSpec((WAVES, 24, 128), lambda g: (0, g, 0)), table_spec],
+        in_specs=[whole(WAVES, 168, 128), hbm],
         out_specs=whole(BANDS, 48, 128),
         out_shape=shape(BANDS, 48, 128),
         scratch_shapes=legendre_scratch,
-        compiler_params=in_order,
+        compiler_params=params(),
         cost_estimate=legendre_cost,
         name="legendre_adjoint",
-    )(spec, legendre)
+    )(spec, in_hbm(legendre))
     modes = exchange(modes, "band").reshape(24, 4, 8, 128)
 
     gradient = pl.pallas_call(

time: 180 us -> 161 us (0.89)
  Pallas kernels: 55.4 us -> 46.1 us
  local copies, waits for them, and re-layouts: 7.78 us -> 0.78 us
  starting transfers between devices: 13.9 us -> 9.13 us
  blocking collectives: 73.5 us -> 77.1 us
    unnamed x40 -> x18, local copies, waits for them, and re-layouts: 7.78 us -> 0.78 us
    pallas_call x6 -> x5, Pallas kernels: 40.3 us -> 33.5 us  [the longest x1 10.9 us: body(): pl.pallas_call(legendre_kernel, in_specs=[whole(BANDS, 88, 128), hbm], ou...]
    all_to_all x3 -> x2, starting transfers between devices: 13.9 us -> 9.13 us  [exchange(): return lax.all_to_all(tiles, axis, split_axis=0, concat_axis=0, tiled=True)]
    all_to_all x4, blocking collectives: 73.5 us -> 77.1 us  [exchange(): return lax.all_to_all(tiles, axis, split_axis=0, concat_axis=0, tiled=True)]
    pallas_call x1, Pallas kernels: 5.9 us -> 2.57 us  [body(): pl.pallas_call(analysis_kernel, grid=(4,), in_specs=[tile_spec, wave_spec...]
    all_to_all x3 -> x2, waiting for transfers between devices: 28 us -> 26.3 us  [exchange(): return lax.all_to_all(tiles, axis, split_axis=0, concat_axis=0, tiled=True)]
  transfers between devices with their start and end apart: 3 -> 2, of which waited for: 3 -> 2; matrix products, arithmetic and copies ran while one was open for 0% -> 0% of each run, Pallas kernels for 11% -> 8%
where the time goes in v2:
time: 161 us; the launch traced here: 160 us
  blocking collectives  77.1 us (48%)
  Pallas kernels  46.1 us (29%)
  waiting for transfers between devices  26.3 us (16%)
  starting transfers between devices  9.13 us (6%)
    all_to_all x4, blocking collectives, exchange(): return lax.all_to_all(tiles, axis, split_axis=0, concat_axis=0, tiled=True)  77.1 us
    all_to_all x2, waiting for transfers between devices, exchange(): return lax.all_to_all(tiles, axis, split_axis=0, concat_axis=0, tiled=True)  26.3 us
    pallas_call x1, Pallas kernels, body(): pl.pallas_call(legendre_kernel, in_specs=[whole(BANDS, 88, 128), hbm], ou...  10.9 us
    pallas_call x1, Pallas kernels, body(): pl.pallas_call(sums_kernel, grid=(WAVES,), in_specs=[pl.BlockSpec((1, 248...  9.53 us
    all_to_all x2, starting transfers between devices, exchange(): return lax.all_to_all(tiles, axis, split_axis=0, concat_axis=0, tiled=True)  9.13 us
    pallas_call x1, Pallas kernels, body(): pl.pallas_call(legendre_adjoint_kernel, in_specs=[whole(WAVES, 168, 128),...  6.95 us
    pallas_call x1, Pallas kernels, body(): pl.pallas_call(grid_kernel, grid=(4,), in_specs=[block, field, pl.BlockSp...  4.63 us
    pallas_call x1, Pallas kernels, body(): pl.pallas_call(wave_table_kernel, out_shape=(shape(2 * MW, NLON, kind=bf1...  3.48 us
  transfers between devices with their start and end apart: 2, of which 2 were waited for; matrix products, arithmetic and copies ran while one was open for 0% of the time, Pallas kernels for 8%

profile of v2, /device:TPU:0, one launch (start us, length us, event | category | flops | bytes accessed | tf_op | source)
XLA Modules:
  0.0 160.1 jit_solution(12887221925574961686)
XLA Ops:
  0.6 2.6 %mix.1 = f32[16,88,128]{2,1,0:T(8,128)S(1)} custom-call(f32[28,16,192]{2,1,0:T(8,128)} %bitcast.13, f32[28,16,192]{2,1,0:T(8,128)} %bitcast.15, f32[96,96]{1,0:T(8,128)} %root_ref.1, s32[128,128]{1,0:T(8,128)} %column_hbm.1, s32[128,128]{1,0:T(8,128)} %level_hbm.1, f32[128,128]{1,0:T(8,128)} %lidar_hbm.1, f32[128,128]{1,0:T(8,128)} %aod_hbm.1, ...), custom_call_target="tpu_custom_call" | custom-call | flops 99090432 | bytes 1048576 | tf_op jit(solution)/shard_map/mix/pallas_call | solution.py:449
  3.3 21.4 %all_to_all.30.modes_ref = f32[16,88,128]{2,1,0:T(8,128)S(1)} all-to-all(f32[16,88,128]{2,1,0:T(8,128)S(1)} %mix.1), channel_id=1, replica_groups=mesh['wave'=8,'band'=16] {'band'}, dimensions={0} | all-to-all | bytes 1441792 | tf_op jit(solution)/shard_map/all_to_all | solution.py:427
  24.6 10.9 %legendre.1 = f32[8,248,128]{2,1,0:T(8,128)} custom-call(f32[16,88,128]{2,1,0:T(8,128)S(1)} %all_to_all.30.modes_ref, f32[28,448,256]{2,1,0:T(8,128)} %table_hbm.3), custom_call_target="tpu_custom_call" | custom-call | flops 924844032 | bytes 14680064 | tf_op jit(solution)/shard_map/legendre/pallas_call | solution.py:500
  35.6 0.0 copy-start.8
  35.6 4.3 %all-to-all-start.1 = ((f32[8,248,128]{2,1,0:T(8,128)}), f32[8,248,128]{2,1,0:T(8,128)S(1)}, u32[]{:S(2)}, u32[]{:S(2)}) async-start(f32[8,248,128]{2,1,0:T(8,128)} %legendre.1), calls=%async_computation.1 | async-start | bytes 2031616 | tf_op jit(solution)/shard_map/all_to_all | solution.py:427
  39.9 0.0 copy-done.8
  39.9 3.5 %wave_table.1 = (bf16[448,1024]{1,0:T(8,128)(2,1)S(1)}, bf16[448,1024]{1,0:T(8,128)(2,1)S(1)}) custom-call(s32[1,224]{1,0:T(1,128)S(1)} %bitcast.19), custom_call_target="tpu_custom_call" | custom-call | flops 9175040 | bytes 2097152 | tf_op jit(solution)/shard_map/wave_table/pallas_call | solution.py:485
  43.4 0.0 copy-start
  43.4 12.1 %all-to-all-done.1.spec_ref.obs_ref = f32[8,248,128]{2,1,0:T(8,128)S(1)} async-done(((f32[8,248,128]{2,1,0:T(8,128)}), f32[8,248,128]{2,1,0:T(8,128)S(1)}, u32[]{:S(2)}, u32[]{:S(2)}) %all-to-all-start.1) | async-done | bytes 1015840 | tf_op jit(solution)/shard_map/all_to_all | solution.py:427
  55.5 3.4 %synthesis.1 = f32[8,16,3,8,128]{4,3,2,1,0:T(8,128)} custom-call(f32[8,248,128]{2,1,0:T(8,128)S(1)} %all-to-all-done.1.spec_ref.obs_ref, bf16[448,1024]{1,0:T(8,128)(2,1)S(1)} %get-tuple-element.6.high_ref, bf16[448,1024]{1,0:T(8,128)(2,1)S(1)} %get-tuple-element.7.low_ref), custom_call_target="tpu_custom_call" | custom-call | flops 1056964608 | bytes 4194304 | tf_op jit(solution)/shard_map/synthesis/pallas_call | solution.py:526
  58.9 0.0 copy-done
  58.9 4.8 %all-to-all-start.2 = ((f32[128,24,128]{2,1,0:T(8,128)}), f32[128,24,128]{2,1,0:T(8,128)S(1)}, u32[]{:S(2)}, u32[]{:S(2)}) async-start(f32[128,24,128]{2,1,0:T(8,128)} %bitcast.3), calls=%async_computation.2 | async-start | bytes 3145728 | tf_op jit(solution)/shard_map/all_to_all | solution.py:427
  63.8 0.0 copy-start.6
  63.8 0.0 copy-start.7
  63.8 9.5 %sums.1.sums_ref = f32[3,256,128]{2,1,0:T(8,128)S(1)} custom-call(f32[8,248,128]{2,1,0:T(8,128)S(1)} %all-to-all-done.1.spec_ref.obs_ref), custom_call_target="tpu_custom_call" | custom-call | flops 6442450944 | bytes 1048576 | tf_op jit(solution)/shard_map/sums/pallas_call | solution.py:511
  73.3 0.0 copy-start.4
  73.3 0.7 copy-done.4
  74.1 14.2 %all-to-all-done.2 = f32[128,24,128]{2,1,0:T(8,128)S(1)} async-done(((f32[128,24,128]{2,1,0:T(8,128)}), f32[128,24,128]{2,1,0:T(8,128)S(1)}, u32[]{:S(2)}, u32[]{:S(2)}) %all-to-all-start.2) | async-done | bytes 1572896 | tf_op jit(solution)/shard_map/all_to_all | solution.py:427
  88.2 0.0 copy-done.6
  88.2 0.0 copy-done.7
  88.2 4.6 %grid_steps.1 = (f32[28,96,128]{2,1,0:T(8,128)}, f32[4,2,16,3,8,128]{5,4,3,2,1,0:T(8,128)S(1)}) custom-call(f32[4,2,16,3,8,128]{5,4,3,2,1,0:T(8,128)S(1)} %bitcast.10, f32[28,96,128]{2,1,0:T(8,128)} %courant_ref.1, f32[3,256,128]{2,1,0:T(8,128)} %copy-done.4, f32[12]{0:T(128)S(1)} %copy-done.6, f32[96]{0:T(128)S(1)} %copy-done.7), custom_call_target="tpu_custom_call" | custom-call | flops 13762560 | bytes 6291456 | tf_op jit(solution)/shard_map/grid_steps/pallas_call | solution.py:542
  92.9 0.0 copy-start.1
  92.9 28.6 %all_to_all.31 = f32[128,24,128]{2,1,0:T(8,128)S(1)} all-to-all(f32[128,24,128]{2,1,0:T(8,128)S(1)} %bitcast.17), channel_id=1, replica_groups=mesh['wave'=8,'band'=16] {'wave','band'}, dimensions={0} | all-to-all | bytes 3145728 | tf_op jit(solution)/shard_map/all_to_all | solution.py:427
  121.5 0.0 copy-done.1
  121.5 2.6 %analysis.1 = f32[8,7,3,8,128]{4,3,2,1,0:T(8,128)S(1)} custom-call(f32[8,16,3,8,128]{4,3,2,1,0:T(8,128)S(1)} %bitcast.11, bf16[448,1024]{1,0:T(8,128)(2,1)S(1)} %get-tuple-element.6.high_ref, bf16[448,1024]{1,0:T(8,128)(2,1)S(1)} %copy-done.1), custom_call_target="tpu_custom_call" | custom-call | flops 1056964608 | bytes 4194304 | tf_op jit(solution)/shard_map/analysis/pallas_call | solution.py:555
  124.1 14.6 %all_to_all.32.spec_ref = f32[8,168,128]{2,1,0:T(8,128)S(1)} all-to-all(f32[8,168,128]{2,1,0:T(8,128)S(1)} %bitcast.12), channel_id=1, replica_groups=mesh['wave'=8,'band'=16] {'wave'}, dimensions={0} | all-to-all | bytes 1376256 | tf_op jit(solution)/shard_map/all_to_all | solution.py:427
  138.7 7.0 %legendre_adjoint.1 = f32[16,48,128]{2,1,0:T(8,128)S(1)} custom-call(f32[8,168,128]{2,1,0:T(8,128)S(1)} %all_to_all.32.spec_ref, f32[28,448,256]{2,1,0:T(8,128)} %table_hbm.3), custom_call_target="tpu_custom_call" | custom-call | flops 924844032 | bytes 14680064 | tf_op jit(solution)/shard_map/legendre_adjoint/pallas_call | solution.py:568
  145.7 12.5 %all_to_all.33 = f32[16,48,128]{2,1,0:T(8,128)S(1)} all-to-all(f32[16,48,128]{2,1,0:T(8,128)S(1)} %legendre_adjoint.1), channel_id=1, replica_groups=mesh['wave'=8,'band'=16] {'band'}, dimensions={0} | all-to-all | bytes 786432 | tf_op jit(solution)/shard_map/all_to_all | solution.py:427
  158.1 0.0 copy-done.2
  158.1 0.0 copy-done.3
  158.1 0.0 copy-done.5
  158.1 2.0 %unmix.1 = f32[28,16,192]{2,1,0:T(8,128)} custom-call(f32[24,4,8,128]{3,2,1,0:T(8,128)S(1)} %bitcast.18, f32[28,16,192]{2,1,0:T(8,128)S(1)} %bitcast.14, f32[28,16,192]{2,1,0:T(8,128)S(1)} %bitcast.16, f32[96,96]{1,0:T(8,128)S(1)} %copy-done.5), custom_call_target="tpu_custom_call" | custom-call | flops 99090432 | bytes 1048576 | tf_op jit(solution)/shard_map/unmix/pallas_call | solution.py:580
  (3 shorter events, 0.0 us)
Async XLA Ops:
  35.6 4.3 %copy-start.8 = (s32[224]{0:T(256)S(1)}, s32[224]{0:T(256)}, u32[]{:S(2)}) copy-start(s32[224]{0:T(256)} %param.18) | copy-start | bytes 2692
  35.6 19.9 %all-to-all-start.1 = ((f32[8,248,128]{2,1,0:T(8,128)}), f32[8,248,128]{2,1,0:T(8,128)S(1)}, u32[]{:S(2)}, u32[]{:S(2)}) async-start(f32[8,248,128]{2,1,0:T(8,128)} %legendre.1), calls=%async_computation.1 | async-start | bytes 2031616 | tf_op jit(solution)/shard_map/all_to_all | solution.py:427
  43.4 15.6 %copy-start = (bf16[448,1024]{1,0:T(8,128)(2,1)}, bf16[448,1024]{1,0:T(8,128)(2,1)S(1)}, u32[]{:S(2)}) copy-start(bf16[448,1024]{1,0:T(8,128)(2,1)S(1)} %get-tuple-element.7.low_ref) | copy-start | bytes 2752516
  58.9 29.3 %all-to-all-start.2 = ((f32[128,24,128]{2,1,0:T(8,128)}), f32[128,24,128]{2,1,0:T(8,128)S(1)}, u32[]{:S(2)}, u32[]{:S(2)}) async-start(f32[128,24,128]{2,1,0:T(8,128)} %bitcast.3), calls=%async_computation.2 | async-start | bytes 3145728 | tf_op jit(solution)/shard_map/all_to_all | solution.py:427
  63.8 24.5 %copy-start.6 = (f32[12]{0:T(128)S(1)}, f32[12]{0:T(128)}, u32[]{:S(2)}) copy-start(f32[12]{0:T(128)} %lidar_ref.1) | copy-start | bytes 148
  63.8 24.5 %copy-start.7 = (f32[96]{0:T(128)S(1)}, f32[96]{0:T(128)}, u32[]{:S(2)}) copy-start(f32[96]{0:T(128)} %aod_ref.1) | copy-start | bytes 1156
  73.3 0.7 copy-start.4
  92.9 28.6 %copy-start.1 = (bf16[448,1024]{1,0:T(8,128)(2,1)S(1)}, bf16[448,1024]{1,0:T(8,128)(2,1)}, u32[]{:S(2)}) copy-start(bf16[448,1024]{1,0:T(8,128)(2,1)} %copy-done) | copy-start | bytes 2752516
  138.7 19.4 %copy-start.2 = (f32[16,28,192]{2,0,1:T(8,128)S(1)}, f32[16,28,192]{2,0,1:T(8,128)}, u32[]{:S(2)}) copy-start(f32[16,28,192]{2,0,1:T(8,128)} %param.14) | copy-start | bytes 1032196
  138.7 19.4 %copy-start.3 = (f32[16,28,192]{2,0,1:T(8,128)S(1)}, f32[16,28,192]{2,0,1:T(8,128)}, u32[]{:S(2)}) copy-start(f32[16,28,192]{2,0,1:T(8,128)} %param.15) | copy-start | bytes 1032196
  138.7 19.4 %copy-start.5 = (f32[96,96]{1,0:T(8,128)S(1)}, f32[96,96]{1,0:T(8,128)}, u32[]{:S(2)}) copy-start(f32[96,96]{1,0:T(8,128)} %root_ref.1) | copy-start | bytes 110596

commit v3 on v2

--- a/solution.py
+++ b/solution.py
@@ -20,6 +20,7 @@
 NLON = 1024
 NLAT = 448
 NT = 256
+TILE = 21
 FACTOR = MW ** (-0.5)
 f32 = jnp.float32
 bf16 = jnp.bfloat16
@@ -147,23 +148,23 @@
 
 
 def table_copies(table_hbm, table_ref, sem):
-    copies = [
-        pltpu.make_async_copy(table_hbm.at[m], table_ref.at[m], sem.at[m])
-        for m in range(4 * GROUPS)
-    ]
+    copies = []
+    for g in range(GROUPS):
+        at = pl.ds(4 * g, 4)
+        copies.append(pltpu.make_async_copy(table_hbm.at[at], table_ref.at[at], sem.at[g]))
     for copy in copies:
         copy.start()
     return copies
 
 
-def legendre_kernel(modes_ref, table_hbm, out_ref, acc_ref, table_ref, sem):
+def legendre_kernel(modes_ref, table_hbm, out_ref, x_ref, acc_ref, table_ref, sem):
     copies = table_copies(table_hbm, table_ref, sem)
-    x = [[None] * 12 for g in range(8)]
     for half in range(2):
         for c in range(6):
             got = [modes_ref[8 * half + s, 8 * c : 8 * c + 8] for s in range(8)]
             for g, z in enumerate(turn(got, 1, 16)):
-                x[g][6 * half + c] = z
+                if g < GROUPS:
+                    x_ref[g, 8 * c : 8 * c + 8, 128 * half : 128 * half + 128] = z
     for k in range(5):
         for half in range(2):
             got = [modes_ref[8 * half + s, 48 + 8 * k : 56 + 8 * k] for s in range(8)]
@@ -172,26 +173,30 @@
                 out_ref[w, at : at + 8] = z
 
     slot = (iota((48, NT), 0) % 8) // 2
+    order = lat_order()
     for g in range(GROUPS):
-        halves = [jnp.concatenate(x[g][6 * h : 6 * h + 6], axis=0) for h in range(2)]
-        mine = jnp.concatenate(halves, axis=1)
+        copies[g].wait()
+        x = x_ref[g]
         acc = None
         for m4 in range(4):
-            xh, xl = split(jnp.where(slot == m4, mine, 0.0))
-            copies[4 * g + m4].wait()
-            th, tl = split(table_ref[4 * g + m4])
-            both = mm_nt(jnp.concatenate([xh, xl], axis=0), th)
-            part = both[:48] + both[48:] + mm_nt(xh, tl)
+            xh, xl = split(jnp.where(slot == m4, x, 0.0))
+            both = jnp.concatenate(split(table_ref[4 * g + m4]), axis=0)
+            both = mm_nt(jnp.concatenate([xh, xl], axis=0), both)
+            part = both[:48, :NLAT] + (both[48:, :NLAT] + both[:48, NLAT:])
             acc = part if acc is None else acc + part
-        for hc in range(2):
-            at = 168 * hc + 24 * g
-            acc_ref[at : at + 24] = acc[24 * hc : 24 * hc + 24]
-    ah, al = split(acc_ref[...])
-    order = lat_order()
-    out = mm(ah, order) + mm(al, order)
-    for q in range(4):
-        for hc in range(2):
-            out_ref[2 * q + hc, :168] = out[168 * hc : 168 * hc + 168, 128 * q : 128 * q + 128]
+        acc_ref[g] = acc
+        for first, last in ((0, 5), (5, 7)):
+            if g + 1 == last:
+                rows = 48 * (last - first)
+                part = acc_ref[first:last].reshape(rows, NLAT)
+                both = mm(jnp.concatenate(split(part), axis=0), order)
+                out = both[:rows] + both[rows:]
+                for k in range(first, last):
+                    for q in range(4):
+                        for hc in range(2):
+                            at = 48 * (k - first) + 24 * hc
+                            tile = out[at : at + 24, 128 * q : 128 * q + 128]
+                            out_ref[2 * q + hc, 24 * k : 24 * k + 24] = tile
 
 
 def lat_order():
@@ -244,17 +249,26 @@
 
     both = mm(lhs_ref[...], high_ref[...])
     out = both[:384] + both[384:] + mm(lhs_ref[:384], low_ref[...])
-    for c in range(3):
-        for w in range(2):
-            tile = out[128 * c : 128 * c + 128, 128 * w : 128 * w + 128]
-            out_ref[w, :, c] = tile.reshape(BANDS, 8, 128)
+    for w in range(2):
+        for band in range(BANDS):
+            for c in range(3):
+                row = 128 * c + 8 * band
+                at = TILE * (BANDS * w + band) + 7 * c
+                out_ref[at : at + 7] = out[row : row + 7, 128 * w : 128 * w + 128]
 
 
 def analysis_kernel(grid_ref, high_ref, low_ref, out_ref, acc_ref):
     i = pl.program_id(0)
+    blank = jnp.zeros((1, 128), f32)
     tiles = []
     for c in range(3):
-        parts = [grid_ref[w, :, c].reshape(128, 128) for w in range(2)]
+        parts = []
+        for w in range(2):
+            rows = []
+            for band in range(BANDS):
+                at = TILE * (BANDS * w + band) + 7 * c
+                rows += [grid_ref[at : at + 7], blank]
+            parts.append(jnp.concatenate(rows, axis=0))
         tiles.append(jnp.concatenate(parts, axis=1))
     gh, gl = split(jnp.concatenate(tiles, axis=0))
     both = mm_nt(high_ref[...], jnp.concatenate([gh, gl], axis=0))
@@ -286,12 +300,12 @@
     slot = (iota((48, NLAT), 0) % 8) // 2
     x = []
     for g in range(GROUPS):
+        copies[g].wait()
         rows = [acc_ref[168 * hc + 24 * g : 168 * hc + 24 * g + 24] for hc in range(2)]
         mine = jnp.concatenate(rows, axis=0)
         acc = None
         for m4 in range(4):
             xh, xl = split(jnp.where(slot == m4, mine, 0.0))
-            copies[4 * g + m4].wait()
             th, tl = split(table_ref[4 * g + m4])
             both = mm(jnp.concatenate([xh, xl], axis=0), th)
             part = both[:48] + both[48:] + mm(xh, tl)
@@ -367,12 +381,19 @@
         for j, z in enumerate(turn(rows, 0, 1)):
             flow_ref[8 * h + j] = z
 
+    def tile_rows(l, b2, hc, c):
+        return pl.ds(TILE * (BANDS * hc + 2 * l + b2) + 7 * c, 7)
+
+    blank = jnp.zeros((1, 128), f32)
     chains = [(b2, hc, c) for b2 in range(2) for hc in range(2) for c in range(3)]
     lidar_sum = [None] * LEV
     aod_sum = None
     for b2, hc, c in chains:
         bin_at = b2 * 6 + hc * 3 + c
-        x = [grid_ref[0, hc, 2 * l + b2, c] for l in range(LEV)]
+        x = [
+            jnp.concatenate([grid_ref[tile_rows(l, b2, hc, c)], blank], axis=0)
+            for l in range(LEV)
+        ]
         flow = [flow_ref[BINS * l + bin_at] for l in range(LEV)]
         for step in range(STEPS):
             out = [flow[l] * x[l] for l in range(LEV)]
@@ -404,7 +425,7 @@
                 a[l] + flow[l] * ((a[l + 1] - a[l]) if l + 1 < LEV else -a[l]) for l in range(LEV)
             ]
         for l in range(LEV):
-            adjoint_ref[0, hc, 2 * l + b2, c] = a[l]
+            adjoint_ref[tile_rows(l, b2, hc, c)] = a[l][:7]
 
 
 def shape(*lengths, kind=f32):
@@ -425,6 +446,11 @@
 
 def exchange(tiles, axis):
     return lax.all_to_all(tiles, axis, split_axis=0, concat_axis=0, tiled=True)
+
+
+def exchange_tiles(tiles):
+    rows = tiles.reshape(DEVICES, 1, TILE * 128)
+    return exchange(rows, ("wave", "band")).reshape(DEVICES * TILE, 128)
 
 
 def body(
@@ -492,17 +518,17 @@
 
     legendre_cost = cost(6 * 28 * 448 * 256 * 48, 14 << 20)
     in_order = params(dimension_semantics=("arbitrary",))
-    legendre_scratch = [
-        pltpu.VMEM((336, NLAT), f32),
-        pltpu.VMEM((28, NLAT, NT), f32),
-        pltpu.SemaphoreType.DMA((28,)),
-    ]
+    table_scratch = [pltpu.VMEM((28, NLAT, NT), f32), pltpu.SemaphoreType.DMA((GROUPS,))]
     spec = pl.pallas_call(
         legendre_kernel,
         in_specs=[whole(BANDS, 88, 128), hbm],
         out_specs=whole(WAVES, 248, 128),
         out_shape=shape(WAVES, 248, 128),
-        scratch_shapes=legendre_scratch,
+        scratch_shapes=[
+            pltpu.VMEM((GROUPS, 48, NT), f32),
+            pltpu.VMEM((GROUPS, 48, NLAT), f32),
+            *table_scratch,
+        ],
         compiler_params=params(),
         cost_estimate=legendre_cost,
         name="legendre",
@@ -521,36 +547,36 @@
     )(spec)
 
     wave_spec = pl.BlockSpec((2 * MW, 256), lambda i: (0, i))
-    tile_spec = pl.BlockSpec((2, BANDS, 3, 8, 128), lambda i: (i, 0, 0, 0, 0))
+    tile_spec = pl.BlockSpec((2 * BANDS * TILE, 128), lambda i: (i, 0))
+    tiles = shape(DEVICES * TILE, 128)
     wave_cost = cost(6 * 384 * 448 * 1024, 4 << 20)
     grid = pl.pallas_call(
         synthesis_kernel,
         grid=(4,),
         in_specs=[whole(WAVES, 248, 128), wave_spec, wave_spec],
         out_specs=tile_spec,
-        out_shape=shape(WAVES, BANDS, 3, 8, 128),
+        out_shape=tiles,
         scratch_shapes=[pltpu.VMEM((768, 2 * MW), bf16)],
         compiler_params=in_order,
         cost_estimate=wave_cost,
         name="synthesis",
     )(spec, high, low)
-    grid = exchange(grid.reshape(DEVICES, 24, 128), ("wave", "band"))
-
-    block = pl.BlockSpec((1, 2, BANDS, 3, 8, 128), lambda q: (q, 0, 0, 0, 0, 0))
+    grid = exchange_tiles(grid)
+
     field = pl.BlockSpec((7, CH, 128), lambda q: (q, 0, 0))
     scalars = pl.BlockSpec(memory_space=pltpu.SMEM)
     state, adjoint = pl.pallas_call(
         grid_kernel,
         grid=(4,),
-        in_specs=[block, field, pl.BlockSpec((3, 64, 128), lambda q: (0, q, 0)), scalars, scalars],
-        out_specs=(field, block),
-        out_shape=(shape(28, CH, 128), shape(4, 2, BANDS, 3, 8, 128)),
+        in_specs=[tile_spec, field, pl.BlockSpec((3, 64, 128), lambda q: (0, q, 0)), scalars, scalars],
+        out_specs=(field, tile_spec),
+        out_shape=(shape(28, CH, 128), tiles),
         scratch_shapes=[pltpu.VMEM((CH, 8, 128), f32), pltpu.VMEM((CH, 8, 128), f32)],
         compiler_params=in_order,
         cost_estimate=cost(40 * 28 * 96 * 128, 6 << 20),
         name="grid_steps",
-    )(grid.reshape(4, 2, BANDS, 3, 8, 128), in_hbm(courant), in_hbm(sums), lidar_coef, aod_coef)
-    adjoint = exchange(adjoint.reshape(DEVICES, 24, 128), ("wave", "band"))
+    )(grid, in_hbm(courant), in_hbm(sums), lidar_coef, aod_coef)
+    adjoint = exchange_tiles(adjoint)
 
     spec = pl.pallas_call(
         analysis_kernel,
@@ -562,7 +588,7 @@
         compiler_params=in_order,
         cost_estimate=wave_cost,
         name="analysis",
-    )(adjoint.reshape(WAVES, BANDS, 3, 8, 128), high, low)
+    )(adjoint, high, low)
     spec = exchange(spec.reshape(WAVES, 24 * GROUPS, 128), "wave")
 
     modes = pl.pallas_call(
@@ -570,7 +596,7 @@
         in_specs=[whole(WAVES, 168, 128), hbm],
         out_specs=whole(BANDS, 48, 128),
         out_shape=shape(BANDS, 48, 128),
-        scratch_shapes=legendre_scratch,
+        scratch_shapes=[pltpu.VMEM((336, NLAT), f32), *table_scratch],
         compiler_params=params(),
         cost_estimate=legendre_cost,
         name="legendre_adjoint",

time: 161 us -> 154 us (0.957)
  Pallas kernels: 46.1 us -> 43.7 us
  blocking collectives: 77.1 us -> 75 us
  waiting for transfers between devices: 26.3 us -> 24.3 us
    all_to_all x4, blocking collectives: 77.1 us -> 75 us  [exchange(): return lax.all_to_all(tiles, axis, split_axis=0, concat_axis=0, tiled=True)]
    all_to_all x2, waiting for transfers between devices: 26.3 us -> 24.3 us  [exchange(): return lax.all_to_all(tiles, axis, split_axis=0, concat_axis=0, tiled=True)]
    pallas_call x1, Pallas kernels: 10.9 us -> 9.04 us  [body(): pl.pallas_call(legendre_kernel, in_specs=[whole(BANDS, 88, 128), hbm], ou...]
where the time goes in v3:
time: 154 us
  blocking collectives  75 us (49%)
  Pallas kernels  43.7 us (28%)
  waiting for transfers between devices  24.3 us (16%)
  starting transfers between devices  9.13 us (6%)
    all_to_all x4, blocking collectives, exchange(): return lax.all_to_all(tiles, axis, split_axis=0, concat_axis=0, tiled=True)  75 us
    all_to_all x2, waiting for transfers between devices, exchange(): return lax.all_to_all(tiles, axis, split_axis=0, concat_axis=0, tiled=True)  24.3 us
    pallas_call x1, Pallas kernels, body(): pl.pallas_call(sums_kernel, grid=(WAVES,), in_specs=[pl.BlockSpec((1, 248...  9.53 us
    all_to_all x2, starting transfers between devices, exchange(): return lax.all_to_all(tiles, axis, split_axis=0, concat_axis=0, tiled=True)  9.13 us
    pallas_call x1, Pallas kernels, body(): pl.pallas_call(legendre_kernel, in_specs=[whole(BANDS, 88, 128), hbm], ou...  9.04 us
    pallas_call x1, Pallas kernels, body(): pl.pallas_call(legendre_adjoint_kernel, in_specs=[whole(WAVES, 168, 128),...  6.51 us
    pallas_call x1, Pallas kernels, body(): pl.pallas_call(grid_kernel, grid=(4,), in_specs=[tile_spec, field, pl.Blo...  4.66 us
    pallas_call x1, Pallas kernels, body(): pl.pallas_call(wave_table_kernel, out_shape=(shape(2 * MW, NLON, kind=bf1...  3.48 us
  transfers between devices with their start and end apart: 2, of which 2 were waited for; matrix products, arithmetic and copies ran while one was open for 0% of the time, Pallas kernels for 8%

profile of v3, /device:TPU:0, one launch (start us, length us, event | category | flops | bytes accessed | tf_op | source)
XLA Modules:
  0.0 153.6 jit_solution(16741544311329294581)
XLA Ops:
  0.6 2.6 %mix.1 = f32[16,88,128]{2,1,0:T(8,128)S(1)} custom-call(f32[28,16,192]{2,1,0:T(8,128)} %bitcast.11, f32[28,16,192]{2,1,0:T(8,128)} %bitcast.13, f32[96,96]{1,0:T(8,128)} %root_ref.1, s32[128,128]{1,0:T(8,128)} %column_hbm.1, s32[128,128]{1,0:T(8,128)} %level_hbm.1, f32[128,128]{1,0:T(8,128)} %lidar_hbm.1, f32[128,128]{1,0:T(8,128)} %aod_hbm.1, ...), custom_call_target="tpu_custom_call" | custom-call | flops 99090432 | bytes 1048576 | tf_op jit(solution)/shard_map/mix/pallas_call | solution.py:475
  3.3 21.4 %all_to_all.30.modes_ref = f32[16,88,128]{2,1,0:T(8,128)S(1)} all-to-all(f32[16,88,128]{2,1,0:T(8,128)S(1)} %mix.1), channel_id=1, replica_groups=mesh['wave'=8,'band'=16] {'band'}, dimensions={0} | all-to-all | bytes 1441792 | tf_op jit(solution)/shard_map/all_to_all | solution.py:448
  24.6 9.0 %legendre.1 = f32[8,248,128]{2,1,0:T(8,128)} custom-call(f32[16,88,128]{2,1,0:T(8,128)S(1)} %all_to_all.30.modes_ref, f32[28,448,256]{2,1,0:T(8,128)} %table_hbm.3), custom_call_target="tpu_custom_call" | custom-call | flops 924844032 | bytes 14680064 | tf_op jit(solution)/shard_map/legendre/pallas_call | solution.py:522
  33.7 0.0 copy-start.8
  33.7 4.3 %all-to-all-start.1 = ((f32[8,248,128]{2,1,0:T(8,128)}), f32[8,248,128]{2,1,0:T(8,128)S(1)}, u32[]{:S(2)}, u32[]{:S(2)}) async-start(f32[8,248,128]{2,1,0:T(8,128)} %legendre.1), calls=%async_computation.1 | async-start | bytes 2031616 | tf_op jit(solution)/shard_map/all_to_all | solution.py:448
  38.0 0.0 copy-done.8
  38.0 3.5 %wave_table.1 = (bf16[448,1024]{1,0:T(8,128)(2,1)S(1)}, bf16[448,1024]{1,0:T(8,128)(2,1)S(1)}) custom-call(s32[1,224]{1,0:T(1,128)S(1)} %bitcast.19), custom_call_target="tpu_custom_call" | custom-call | flops 9175040 | bytes 2097152 | tf_op jit(solution)/shard_map/wave_table/pallas_call | solution.py:511
  41.5 0.0 copy-start.2
  41.5 12.1 %all-to-all-done.1.spec_ref.obs_ref = f32[8,248,128]{2,1,0:T(8,128)S(1)} async-done(((f32[8,248,128]{2,1,0:T(8,128)}), f32[8,248,128]{2,1,0:T(8,128)S(1)}, u32[]{:S(2)}, u32[]{:S(2)}) %all-to-all-start.1) | async-done | bytes 1015840 | tf_op jit(solution)/shard_map/all_to_all | solution.py:448
  53.6 3.4 %synthesis.1 = f32[2688,128]{1,0:T(8,128)} custom-call(f32[8,248,128]{2,1,0:T(8,128)S(1)} %all-to-all-done.1.spec_ref.obs_ref, bf16[448,1024]{1,0:T(8,128)(2,1)S(1)} %get-tuple-element.6.high_ref, bf16[448,1024]{1,0:T(8,128)(2,1)S(1)} %get-tuple-element.7.low_ref), custom_call_target="tpu_custom_call" | custom-call | flops 1056964608 | bytes 4194304 | tf_op jit(solution)/shard_map/synthesis/pallas_call | solution.py:553
  57.0 0.0 copy-done.2
  57.0 4.8 %all-to-all-start.2 = ((f32[128,1,2688]{2,1,0:T(1,128)}), f32[128,1,2688]{2,1,0:T(1,128)S(1)}, u32[]{:S(2)}, u32[]{:S(2)}) async-start(f32[128,1,2688]{2,1,0:T(1,128)} %bitcast.3), calls=%async_computation.2 | async-start | bytes 2752512 | tf_op jit(solution)/shard_map/all_to_all | solution.py:448
  61.8 0.0 copy-start.6
  61.8 0.0 copy-start.7
  61.9 9.5 %sums.1.sums_ref = f32[3,256,128]{2,1,0:T(8,128)S(1)} custom-call(f32[8,248,128]{2,1,0:T(8,128)S(1)} %all-to-all-done.1.spec_ref.obs_ref), custom_call_target="tpu_custom_call" | custom-call | flops 6442450944 | bytes 1048576 | tf_op jit(solution)/shard_map/sums/pallas_call | solution.py:537
  71.4 0.0 copy-start.4
  71.4 0.7 copy-done.4
  72.1 12.1 %all-to-all-done.2 = f32[128,1,2688]{2,1,0:T(1,128)S(1)} async-done(((f32[128,1,2688]{2,1,0:T(1,128)}), f32[128,1,2688]{2,1,0:T(1,128)S(1)}, u32[]{:S(2)}, u32[]{:S(2)}) %all-to-all-start.2) | async-done | bytes 1376288 | tf_op jit(solution)/shard_map/all_to_all | solution.py:448
  84.3 0.0 copy-done.6
  84.3 0.0 copy-done.7
  84.3 4.7 %grid_steps.1 = (f32[28,96,128]{2,1,0:T(8,128)}, f32[2688,128]{1,0:T(8,128)S(1)}) custom-call(f32[2688,128]{1,0:T(8,128)S(1)} %bitcast.10, f32[28,96,128]{2,1,0:T(8,128)} %courant_ref.1, f32[3,256,128]{2,1,0:T(8,128)} %copy-done.4, f32[12]{0:T(128)S(1)} %copy-done.6, f32[96]{0:T(128)S(1)} %copy-done.7), custom_call_target="tpu_custom_call" | custom-call | flops 13762560 | bytes 6291456 | tf_op jit(solution)/shard_map/grid_steps/pallas_call | solution.py:568
  88.9 0.0 copy-start.3
  88.9 26.6 %all_to_all.31 = f32[128,1,2688]{2,1,0:T(1,128)S(1)} all-to-all(f32[128,1,2688]{2,1,0:T(1,128)S(1)} %bitcast.16), channel_id=1, replica_groups=mesh['wave'=8,'band'=16] {'wave','band'}, dimensions={0} | all-to-all | bytes 2752512 | tf_op jit(solution)/shard_map/all_to_all | solution.py:448
  115.5 0.0 copy-done.3
  115.5 2.6 %analysis.1 = f32[8,7,3,8,128]{4,3,2,1,0:T(8,128)S(1)} custom-call(f32[2688,128]{1,0:T(8,128)S(1)} %bitcast.17, bf16[448,1024]{1,0:T(8,128)(2,1)S(1)} %get-tuple-element.6.high_ref, bf16[448,1024]{1,0:T(8,128)(2,1)S(1)} %copy-done.3), custom_call_target="tpu_custom_call" | custom-call | flops 1056964608 | bytes 4194304 | tf_op jit(solution)/shard_map/analysis/pallas_call | solution.py:581
  118.1 14.6 %all_to_all.32.spec_ref = f32[8,168,128]{2,1,0:T(8,128)S(1)} all-to-all(f32[8,168,128]{2,1,0:T(8,128)S(1)} %bitcast.18), channel_id=1, replica_groups=mesh['wave'=8,'band'=16] {'wave'}, dimensions={0} | all-to-all | bytes 1376256 | tf_op jit(solution)/shard_map/all_to_all | solution.py:448
  132.7 6.5 %legendre_adjoint.1 = f32[16,48,128]{2,1,0:T(8,128)S(1)} custom-call(f32[8,168,128]{2,1,0:T(8,128)S(1)} %all_to_all.32.spec_ref, f32[28,448,256]{2,1,0:T(8,128)} %table_hbm.3), custom_call_target="tpu_custom_call" | custom-call | flops 924844032 | bytes 14680064 | tf_op jit(solution)/shard_map/legendre_adjoint/pallas_call | solution.py:594
  139.2 12.5 %all_to_all.33 = f32[16,48,128]{2,1,0:T(8,128)S(1)} all-to-all(f32[16,48,128]{2,1,0:T(8,128)S(1)} %legendre_adjoint.1), channel_id=1, replica_groups=mesh['wave'=8,'band'=16] {'band'}, dimensions={0} | all-to-all | bytes 786432 | tf_op jit(solution)/shard_map/all_to_all | solution.py:448
  151.7 0.0 copy-done
  151.7 0.0 copy-done.1
  151.7 0.0 copy-done.5
  151.7 2.0 %unmix.1 = f32[28,16,192]{2,1,0:T(8,128)} custom-call(f32[24,4,8,128]{3,2,1,0:T(8,128)S(1)} %bitcast.15, f32[28,16,192]{2,1,0:T(8,128)S(1)} %bitcast.12, f32[28,16,192]{2,1,0:T(8,128)S(1)} %bitcast.14, f32[96,96]{1,0:T(8,128)S(1)} %copy-done.5), custom_call_target="tpu_custom_call" | custom-call | flops 99090432 | bytes 1048576 | tf_op jit(solution)/shard_map/unmix/pallas_call | solution.py:606
  (3 shorter events, 0.0 us)
Async XLA Ops:
  33.7 4.3 %copy-start.8 = (s32[224]{0:T(256)S(1)}, s32[224]{0:T(256)}, u32[]{:S(2)}) copy-start(s32[224]{0:T(256)} %param.18) | copy-start | bytes 2692
  33.7 19.9 %all-to-all-start.1 = ((f32[8,248,128]{2,1,0:T(8,128)}), f32[8,248,128]{2,1,0:T(8,128)S(1)}, u32[]{:S(2)}, u32[]{:S(2)}) async-start(f32[8,248,128]{2,1,0:T(8,128)} %legendre.1), calls=%async_computation.1 | async-start | bytes 2031616 | tf_op jit(solution)/shard_map/all_to_all | solution.py:448
  41.5 15.5 %copy-start.2 = (bf16[448,1024]{1,0:T(8,128)(2,1)}, bf16[448,1024]{1,0:T(8,128)(2,1)S(1)}, u32[]{:S(2)}) copy-start(bf16[448,1024]{1,0:T(8,128)(2,1)S(1)} %get-tuple-element.7.low_ref) | copy-start | bytes 2752516
  57.0 27.3 %all-to-all-start.2 = ((f32[128,1,2688]{2,1,0:T(1,128)}), f32[128,1,2688]{2,1,0:T(1,128)S(1)}, u32[]{:S(2)}, u32[]{:S(2)}) async-start(f32[128,1,2688]{2,1,0:T(1,128)} %bitcast.3), calls=%async_computation.2 | async-start | bytes 2752512 | tf_op jit(solution)/shard_map/all_to_all | solution.py:448
  61.8 22.5 %copy-start.6 = (f32[12]{0:T(128)S(1)}, f32[12]{0:T(128)}, u32[]{:S(2)}) copy-start(f32[12]{0:T(128)} %lidar_ref.1) | copy-start | bytes 148
  61.8 22.4 %copy-start.7 = (f32[96]{0:T(128)S(1)}, f32[96]{0:T(128)}, u32[]{:S(2)}) copy-start(f32[96]{0:T(128)} %aod_ref.1) | copy-start | bytes 1156
  71.4 0.7 copy-start.4
  88.9 26.6 %copy-start.3 = (bf16[448,1024]{1,0:T(8,128)(2,1)S(1)}, bf16[448,1024]{1,0:T(8,128)(2,1)}, u32[]{:S(2)}) copy-start(bf16[448,1024]{1,0:T(8,128)(2,1)} %copy-done.2) | copy-start | bytes 2752516
  132.7 19.0 %copy-start = (f32[16,28,192]{2,0,1:T(8,128)S(1)}, f32[16,28,192]{2,0,1:T(8,128)}, u32[]{:S(2)}) copy-start(f32[16,28,192]{2,0,1:T(8,128)} %param.14) | copy-start | bytes 1032196
  132.7 19.0 %copy-start.1 = (f32[16,28,192]{2,0,1:T(8,128)S(1)}, f32[16,28,192]{2,0,1:T(8,128)}, u32[]{:S(2)}) copy-start(f32[16,28,192]{2,0,1:T(8,128)} %param.15) | copy-start | bytes 1032196
  132.7 19.0 %copy-start.5 = (f32[96,96]{1,0:T(8,128)S(1)}, f32[96,96]{1,0:T(8,128)}, u32[]{:S(2)}) copy-start(f32[96,96]{1,0:T(8,128)} %root_ref.1) | copy-start | bytes 110596

commit v4 on v3

--- a/solution.py
+++ b/solution.py
@@ -21,6 +21,7 @@
 NLAT = 448
 NT = 256
 TILE = 21
+HEAD = 4
 FACTOR = MW ** (-0.5)
 f32 = jnp.float32
 bf16 = jnp.bfloat16
@@ -112,8 +113,23 @@
             )
         )
     ]
-    for copy in copies:
+    for copy in copies[3:] + copies[:3]:
         copy.start()
+    for copy in copies[3:]:
+        copy.wait()
+    counts = jnp.broadcast_to(count_ref[...].astype(f32), (DEVICES, DEVICES)).T
+    live = iota((DEVICES, SLOT), 1).astype(f32) < counts
+    weight = jnp.where(live, value_ref[2], 0.0)
+    obs_ref[0] = index_ref[0].astype(f32)
+    obs_ref[1] = index_ref[1].astype(f32)
+    obs_ref[2] = weight
+    obs_ref[3] = weight * value_ref[0]
+    obs_ref[4] = weight * value_ref[1]
+    for band in range(BANDS):
+        for k in range(5):
+            rows = obs_ref[k, pl.ds(band, WAVES, stride=BANDS), :]
+            out_ref[band, 48 + 8 * k : 56 + 8 * k] = rows
+
     for copy in copies[:3]:
         copy.wait()
     root = doubled_root(root_ref[...])
@@ -131,33 +147,36 @@
             c = 4 * h + j
             out_ref[c // 6, 8 * (c % 6) : 8 * (c % 6) + 8] = z[h]
 
-    for copy in copies[3:]:
-        copy.wait()
-    counts = jnp.broadcast_to(count_ref[...].astype(f32), (DEVICES, DEVICES)).T
-    live = iota((DEVICES, SLOT), 1).astype(f32) < counts
-    weight = jnp.where(live, value_ref[2], 0.0)
-    obs_ref[0] = index_ref[0].astype(f32)
-    obs_ref[1] = index_ref[1].astype(f32)
-    obs_ref[2] = weight
-    obs_ref[3] = weight * value_ref[0]
-    obs_ref[4] = weight * value_ref[1]
-    for band in range(BANDS):
-        for k in range(5):
-            rows = obs_ref[k, pl.ds(band, WAVES, stride=BANDS), :]
-            out_ref[band, 48 + 8 * k : 56 + 8 * k] = rows
+
+def head_kernel(table_hbm, out_ref, sem):
+    copy = pltpu.make_async_copy(table_hbm.at[pl.ds(0, HEAD)], out_ref, sem)
+    copy.start()
+    copy.wait()
 
 
 def table_copies(table_hbm, table_ref, sem):
-    copies = []
-    for g in range(GROUPS):
-        at = pl.ds(4 * g, 4)
-        copies.append(pltpu.make_async_copy(table_hbm.at[at], table_ref.at[at], sem.at[g]))
-    for copy in copies:
+    copies = {}
+    first = HEAD
+    while first < 4 * GROUPS:
+        count = 4 - first % 4
+        source = table_hbm.at[pl.ds(first, count)]
+        target = table_ref.at[pl.ds(first - HEAD, count)]
+        copies[first] = pltpu.make_async_copy(source, target, sem.at[len(copies)])
+        first += count
+    for copy in copies.values():
         copy.start()
     return copies
 
 
-def legendre_kernel(modes_ref, table_hbm, out_ref, x_ref, acc_ref, table_ref, sem):
+def table_slot(m, copies, head_ref, table_ref):
+    if m < HEAD:
+        return head_ref[m]
+    if m in copies:
+        copies[m].wait()
+    return table_ref[m - HEAD]
+
+
+def legendre_kernel(modes_ref, head_ref, table_hbm, out_ref, x_ref, acc_ref, table_ref, sem):
     copies = table_copies(table_hbm, table_ref, sem)
     for half in range(2):
         for c in range(6):
@@ -175,12 +194,11 @@
     slot = (iota((48, NT), 0) % 8) // 2
     order = lat_order()
     for g in range(GROUPS):
-        copies[g].wait()
         x = x_ref[g]
         acc = None
         for m4 in range(4):
             xh, xl = split(jnp.where(slot == m4, x, 0.0))
-            both = jnp.concatenate(split(table_ref[4 * g + m4]), axis=0)
+            both = jnp.concatenate(split(table_slot(4 * g + m4, copies, head_ref, table_ref)), axis=0)
             both = mm_nt(jnp.concatenate([xh, xl], axis=0), both)
             part = both[:48, :NLAT] + (both[48:, :NLAT] + both[:48, NLAT:])
             acc = part if acc is None else acc + part
@@ -238,59 +256,48 @@
 
 
 def synthesis_kernel(spec_ref, high_ref, low_ref, out_ref, lhs_ref):
-    @pl.when(pl.program_id(0) == 0)
-    def _():
-        rows = spec_ref[:, :168].reshape(WAVES, GROUPS, 3, 8, 128)
+    rows = spec_ref[:, :168].reshape(WAVES, GROUPS, 3, 8, 128)
+    for c in range(3):
+        high, low = split(rows[:, :, c].reshape(2 * MW, 128).T)
+        lhs_ref[128 * c : 128 * c + 128] = high
+        lhs_ref[384 + 128 * c : 512 + 128 * c] = low
+    for i in range(4):
+        lon = pl.ds(256 * i, 256)
+        both = mm(lhs_ref[...], high_ref[:, lon])
+        out = both[:384] + both[384:] + mm(lhs_ref[:384], low_ref[:, lon])
+        for w in range(2):
+            for band in range(BANDS):
+                for c in range(3):
+                    row = 128 * c + 8 * band
+                    at = TILE * (BANDS * (2 * i + w) + band) + 7 * c
+                    out_ref[at : at + 7] = out[row : row + 7, 128 * w : 128 * w + 128]
+
+
+def analysis_kernel(grid_ref, high_ref, low_ref, out_ref):
+    blank = jnp.zeros((1, 128), f32)
+    total = None
+    for i in range(4):
+        tiles = []
         for c in range(3):
-            s = rows[:, :, c].reshape(2 * MW, 128).T
-            sh, sl = split(s)
-            lhs_ref[128 * c : 128 * c + 128] = sh
-            lhs_ref[384 + 128 * c : 512 + 128 * c] = sl
-
-    both = mm(lhs_ref[...], high_ref[...])
-    out = both[:384] + both[384:] + mm(lhs_ref[:384], low_ref[...])
-    for w in range(2):
-        for band in range(BANDS):
-            for c in range(3):
-                row = 128 * c + 8 * band
-                at = TILE * (BANDS * w + band) + 7 * c
-                out_ref[at : at + 7] = out[row : row + 7, 128 * w : 128 * w + 128]
-
-
-def analysis_kernel(grid_ref, high_ref, low_ref, out_ref, acc_ref):
-    i = pl.program_id(0)
-    blank = jnp.zeros((1, 128), f32)
-    tiles = []
+            parts = []
+            for w in range(2):
+                rows = []
+                for band in range(BANDS):
+                    at = TILE * (BANDS * (2 * i + w) + band) + 7 * c
+                    rows += [grid_ref[at : at + 7], blank]
+                parts.append(jnp.concatenate(rows, axis=0))
+            tiles.append(jnp.concatenate(parts, axis=1))
+        gh, gl = split(jnp.concatenate(tiles, axis=0))
+        lon = pl.ds(256 * i, 256)
+        both = mm_nt(high_ref[:, lon], jnp.concatenate([gh, gl], axis=0))
+        part = both[:, :384] + both[:, 384:] + mm_nt(low_ref[:, lon], gh)
+        total = part if total is None else total + part
     for c in range(3):
-        parts = []
-        for w in range(2):
-            rows = []
-            for band in range(BANDS):
-                at = TILE * (BANDS * w + band) + 7 * c
-                rows += [grid_ref[at : at + 7], blank]
-            parts.append(jnp.concatenate(rows, axis=0))
-        tiles.append(jnp.concatenate(parts, axis=1))
-    gh, gl = split(jnp.concatenate(tiles, axis=0))
-    both = mm_nt(high_ref[...], jnp.concatenate([gh, gl], axis=0))
-    part = both[:, :384] + both[:, 384:] + mm_nt(low_ref[...], gh)
-
-    @pl.when(i == 0)
-    def _():
-        acc_ref[...] = part
-
-    @pl.when((i > 0) & (i < 3))
-    def _():
-        acc_ref[...] += part
-
-    @pl.when(i == 3)
-    def _():
-        total = acc_ref[...] + part
-        for c in range(3):
-            rows = total[:, 128 * c : 128 * c + 128]
-            out_ref[:, :, c] = rows.reshape(WAVES, GROUPS, 8, 128)
-
-
-def legendre_adjoint_kernel(spec_ref, table_hbm, out_ref, acc_ref, table_ref, sem):
+        rows = total[:, 128 * c : 128 * c + 128]
+        out_ref[:, :, c] = rows.reshape(WAVES, GROUPS, 8, 128)
+
+
+def legendre_adjoint_kernel(spec_ref, head_ref, table_hbm, out_ref, acc_ref, table_ref, sem):
     copies = table_copies(table_hbm, table_ref, sem)
     order = lat_order()
     for hc in range(2):
@@ -300,13 +307,12 @@
     slot = (iota((48, NLAT), 0) % 8) // 2
     x = []
     for g in range(GROUPS):
-        copies[g].wait()
         rows = [acc_ref[168 * hc + 24 * g : 168 * hc + 24 * g + 24] for hc in range(2)]
         mine = jnp.concatenate(rows, axis=0)
         acc = None
         for m4 in range(4):
             xh, xl = split(jnp.where(slot == m4, mine, 0.0))
-            th, tl = split(table_ref[4 * g + m4])
+            th, tl = split(table_slot(4 * g + m4, copies, head_ref, table_ref))
             both = mm(jnp.concatenate([xh, xl], axis=0), th)
             part = both[:48] + both[48:] + mm(xh, tl)
             acc = part if acc is None else acc + part
@@ -373,14 +379,21 @@
             out_ref[k] = first + acc_ref[:, 256 * k + 128 : 256 * k + 256]
 
 
-def grid_kernel(
-    grid_ref, courant_ref, sums_ref, lidar_ref, aod_ref, state_ref, adjoint_ref, flow_ref, hold_ref
-):
+def flow_kernel(courant_ref, out_ref):
     for h in range(12):
         rows = [courant_ref[min(t, 6), 8 * h : 8 * h + 8] for t in range(8)]
         for j, z in enumerate(turn(rows, 0, 1)):
-            flow_ref[8 * h + j] = z
-
+            out_ref[8 * h + j] = z
+
+
+def state_kernel(hold_ref, out_ref):
+    for h in range(12):
+        rows = turn([hold_ref[8 * h + j] for j in range(8)], 0, 1)
+        for t in range(7):
+            out_ref[t, 8 * h : 8 * h + 8] = rows[t]
+
+
+def grid_kernel(grid_ref, flow_ref, sums_ref, lidar_ref, aod_ref, hold_ref, adjoint_ref):
     def tile_rows(l, b2, hc, c):
         return pl.ds(TILE * (BANDS * hc + 2 * l + b2) + 7 * c, 7)
 
@@ -404,11 +417,6 @@
             lidar_sum[l] = x[l] * coef if lidar_sum[l] is None else lidar_sum[l] + x[l] * coef
             term = x[l] * aod_ref[BINS * l + bin_at]
             aod_sum = term if aod_sum is None else aod_sum + term
-
-    for h in range(12):
-        rows = turn([hold_ref[8 * h + j] for j in range(8)], 0, 1)
-        for t in range(7):
-            state_ref[t, 8 * h : 8 * h + 8] = rows[t]
 
     weight = [sums_ref[0, 8 * l : 8 * l + 8] for l in range(LEV)]
     lidar = [weight[l] * lidar_sum[l] - sums_ref[1, 8 * l : 8 * l + 8] for l in range(LEV)]
@@ -516,12 +524,25 @@
         name="wave_table",
     )(zonal_number.reshape(1, MW))
 
+
+    def head(table):
+        return pl.pallas_call(
+            head_kernel,
+            in_specs=[hbm],
+            out_specs=whole(HEAD, NLAT, NT),
+            out_shape=shape(HEAD, NLAT, NT),
+            scratch_shapes=[pltpu.SemaphoreType.DMA(())],
+            compiler_params=params(),
+            cost_estimate=cost(0, 8 * HEAD * NLAT * NT),
+            name="head",
+        )(in_hbm(table))
+
     legendre_cost = cost(6 * 28 * 448 * 256 * 48, 14 << 20)
     in_order = params(dimension_semantics=("arbitrary",))
-    table_scratch = [pltpu.VMEM((28, NLAT, NT), f32), pltpu.SemaphoreType.DMA((GROUPS,))]
+    table_scratch = [pltpu.VMEM((28 - HEAD, NLAT, NT), f32), pltpu.SemaphoreType.DMA((GROUPS,))]
     spec = pl.pallas_call(
         legendre_kernel,
-        in_specs=[whole(BANDS, 88, 128), hbm],
+        in_specs=[whole(BANDS, 88, 128), whole(HEAD, NLAT, NT), hbm],
         out_specs=whole(WAVES, 248, 128),
         out_shape=shape(WAVES, 248, 128),
         scratch_shapes=[
@@ -532,7 +553,7 @@
         compiler_params=params(),
         cost_estimate=legendre_cost,
         name="legendre",
-    )(modes, in_hbm(legendre))
+    )(modes, head(legendre), in_hbm(legendre))
     spec = exchange(spec, "wave")
     sums = pl.pallas_call(
         sums_kernel,
@@ -546,18 +567,14 @@
         name="sums",
     )(spec)
 
-    wave_spec = pl.BlockSpec((2 * MW, 256), lambda i: (0, i))
     tile_spec = pl.BlockSpec((2 * BANDS * TILE, 128), lambda i: (i, 0))
     tiles = shape(DEVICES * TILE, 128)
     wave_cost = cost(6 * 384 * 448 * 1024, 4 << 20)
     grid = pl.pallas_call(
         synthesis_kernel,
-        grid=(4,),
-        in_specs=[whole(WAVES, 248, 128), wave_spec, wave_spec],
-        out_specs=tile_spec,
         out_shape=tiles,
         scratch_shapes=[pltpu.VMEM((768, 2 * MW), bf16)],
-        compiler_params=in_order,
+        compiler_params=params(),
         cost_estimate=wave_cost,
         name="synthesis",
     )(spec, high, low)
@@ -565,42 +582,65 @@
 
     field = pl.BlockSpec((7, CH, 128), lambda q: (q, 0, 0))
     scalars = pl.BlockSpec(memory_space=pltpu.SMEM)
-    state, adjoint = pl.pallas_call(
+    turned = pl.BlockSpec((CH, 8, 128), lambda q: (q, 0, 0))
+    flow = pl.pallas_call(
+        flow_kernel,
+        grid=(4,),
+        in_specs=[field],
+        out_specs=turned,
+        out_shape=shape(4 * CH, 8, 128),
+        compiler_params=in_order,
+        cost_estimate=cost(6 * 28 * 96 * 128, 3 << 20),
+        name="flow",
+    )(in_hbm(courant))
+    hold, adjoint = pl.pallas_call(
         grid_kernel,
         grid=(4,),
-        in_specs=[tile_spec, field, pl.BlockSpec((3, 64, 128), lambda q: (0, q, 0)), scalars, scalars],
-        out_specs=(field, tile_spec),
-        out_shape=(shape(28, CH, 128), tiles),
-        scratch_shapes=[pltpu.VMEM((CH, 8, 128), f32), pltpu.VMEM((CH, 8, 128), f32)],
+        in_specs=[
+            tile_spec,
+            turned,
+            pl.BlockSpec((3, 64, 128), lambda q: (0, q, 0)),
+            scalars,
+            scalars,
+        ],
+        out_specs=(turned, tile_spec),
+        out_shape=(shape(4 * CH, 8, 128), tiles),
         compiler_params=in_order,
         cost_estimate=cost(40 * 28 * 96 * 128, 6 << 20),
         name="grid_steps",
-    )(grid, in_hbm(courant), in_hbm(sums), lidar_coef, aod_coef)
+    )(grid, flow, in_hbm(sums), lidar_coef, aod_coef)
+    state = pl.pallas_call(
+        state_kernel,
+        grid=(4,),
+        in_specs=[turned],
+        out_specs=field,
+        out_shape=shape(28, CH, 128),
+        compiler_params=in_order,
+        cost_estimate=cost(6 * 28 * 96 * 128, 3 << 20),
+        name="state",
+    )(hold)
     adjoint = exchange_tiles(adjoint)
 
     spec = pl.pallas_call(
         analysis_kernel,
-        grid=(4,),
-        in_specs=[tile_spec, wave_spec, wave_spec],
-        out_specs=whole(WAVES, GROUPS, 3, 8, 128),
         out_shape=shape(WAVES, GROUPS, 3, 8, 128),
-        scratch_shapes=[pltpu.VMEM((2 * MW, 384), f32)],
-        compiler_params=in_order,
+        compiler_params=params(),
         cost_estimate=wave_cost,
         name="analysis",
     )(adjoint, high, low)
+    again, spec = lax.optimization_barrier((legendre, spec))
     spec = exchange(spec.reshape(WAVES, 24 * GROUPS, 128), "wave")
 
     modes = pl.pallas_call(
         legendre_adjoint_kernel,
-        in_specs=[whole(WAVES, 168, 128), hbm],
+        in_specs=[whole(WAVES, 168, 128), whole(HEAD, NLAT, NT), hbm],
         out_specs=whole(BANDS, 48, 128),
         out_shape=shape(BANDS, 48, 128),
         scratch_shapes=[pltpu.VMEM((336, NLAT), f32), *table_scratch],
         compiler_params=params(),
         cost_estimate=legendre_cost,
         name="legendre_adjoint",
-    )(spec, in_hbm(legendre))
+    )(spec, head(again), in_hbm(legendre))
     modes = exchange(modes, "band").reshape(24, 4, 8, 128)
 
     gradient = pl.pallas_call(

time: 154 us -> 155 us (level)
  blocking collectives: 75 us -> 26.7 us
  waiting for transfers between devices: 24.3 us -> 51.1 us
  starting transfers between devices: 9.13 us -> 24.2 us
  Pallas kernels: 43.7 us -> 49.3 us
    all_to_all x4 -> x1, blocking collectives: 75 us -> 26.7 us  [exchange(): return lax.all_to_all(tiles, axis, split_axis=0, concat_axis=0, tiled=True)]
    all_to_all x2 -> x5, waiting for transfers between devices: 24.3 us -> 51.1 us  [exchange(): return lax.all_to_all(tiles, axis, split_axis=0, concat_axis=0, tiled=True)]
    all_to_all x2 -> x5, starting transfers between devices: 9.13 us -> 24.2 us  [exchange(): return lax.all_to_all(tiles, axis, split_axis=0, concat_axis=0, tiled=True)]
    pallas_call x4 -> x8, Pallas kernels: 19.6 us -> 24.6 us  [the longest x1 9.33 us: body(): pl.pallas_call(legendre_kernel, in_specs=[whole(BANDS, 88, 128), whole(HE...]
  transfers between devices with their start and end apart: 2 -> 5, of which waited for: 2 -> 5; matrix products, arithmetic and copies ran while one was open for 0% -> 0% of each run, Pallas kernels for 8% -> 13%
where the time goes in v4:
time: 155 us; the launch traced here: 154 us
  waiting for transfers between devices  51.1 us (33%)
  Pallas kernels  49.3 us (32%)
  blocking collectives  26.7 us (17%)
  starting transfers between devices  24.2 us (16%)
  local copies, waits for them, and re-layouts  2.2 us (1%)
    all_to_all x5, waiting for transfers between devices, exchange(): return lax.all_to_all(tiles, axis, split_axis=0, concat_axis=0, tiled=True)  51.1 us
    all_to_all x1, blocking collectives, exchange(): return lax.all_to_all(tiles, axis, split_axis=0, concat_axis=0, tiled=True)  26.7 us
    all_to_all x5, starting transfers between devices, exchange(): return lax.all_to_all(tiles, axis, split_axis=0, concat_axis=0, tiled=True)  24.2 us
    pallas_call x1, Pallas kernels, body(): pl.pallas_call(sums_kernel, grid=(WAVES,), in_specs=[pl.BlockSpec((1, 248...  9.53 us
    pallas_call x1, Pallas kernels, body(): pl.pallas_call(legendre_kernel, in_specs=[whole(BANDS, 88, 128), whole(HE...  9.33 us
    pallas_call x1, Pallas kernels, body(): pl.pallas_call(legendre_adjoint_kernel, in_specs=[whole(WAVES, 168, 128),...  6.33 us
    pallas_call x1, Pallas kernels, body(): pl.pallas_call(wave_table_kernel, out_shape=(shape(2 * MW, NLON, kind=bf1...  3.48 us
    pallas_call x1, Pallas kernels, body(): pl.pallas_call(mix_kernel, in_specs=[hbm] * 9, out_specs=whole(BANDS, 88,...  3.46 us
  transfers between devices with their start and end apart: 5, of which 5 were waited for; matrix products, arithmetic and copies ran while one was open for 0% of the time, Pallas kernels for 13%

profile of v4, /device:TPU:0, one launch (start us, length us, event | category | flops | bytes accessed | tf_op | source)
XLA Modules:
  0.0 154.4 jit_solution(13000871756922720933)
XLA Ops:
  0.6 3.5 %mix.1 = f32[16,88,128]{2,1,0:T(8,128)} custom-call(f32[28,16,192]{2,1,0:T(8,128)} %bitcast.11, f32[28,16,192]{2,1,0:T(8,128)} %bitcast.13, f32[96,96]{1,0:T(8,128)} %root_ref.1, s32[128,128]{1,0:T(8,128)} %column_hbm.1, s32[128,128]{1,0:T(8,128)} %level_hbm.1, f32[128,128]{1,0:T(8,128)} %lidar_hbm.1, f32[128,128]{1,0:T(8,128)} %aod_hbm.1, ...), custom_call_target="tpu_custom_call" | custom-call | flops 99090432 | bytes 1048576 | tf_op jit(solution)/shard_map/mix/pallas_call | solution.py:483
  4.1 8.1 %all-to-all-start = ((f32[16,88,128]{2,1,0:T(8,128)}), f32[16,88,128]{2,1,0:T(8,128)S(1)}, u32[]{:S(2)}, u32[]{:S(2)}) async-start(f32[16,88,128]{2,1,0:T(8,128)} %mix.1), calls=%async_computation | async-start | bytes 1441792 | tf_op jit(solution)/shard_map/all_to_all | solution.py:456
  12.3 1.5 head.2.head_ref
  13.8 12.1 %all-to-all-done.modes_ref = f32[16,88,128]{2,1,0:T(8,128)S(1)} async-done(((f32[16,88,128]{2,1,0:T(8,128)}), f32[16,88,128]{2,1,0:T(8,128)S(1)}, u32[]{:S(2)}, u32[]{:S(2)}) %all-to-all-start) | async-done | bytes 720928 | tf_op jit(solution)/shard_map/all_to_all | solution.py:456
  25.9 9.3 %legendre.1 = f32[8,248,128]{2,1,0:T(8,128)} custom-call(f32[16,88,128]{2,1,0:T(8,128)S(1)} %all-to-all-done.modes_ref, f32[4,448,256]{2,1,0:T(8,128)S(1)} %head.2.head_ref, f32[28,448,256]{2,1,0:T(8,128)} %table_hbm.6), custom_call_target="tpu_custom_call" | custom-call | flops 924844032 | bytes 14680064 | tf_op jit(solution)/shard_map/legendre/pallas_call | solution.py:543
  35.2 0.0 copy-start.14
  35.2 4.3 %all-to-all-start.1 = ((f32[8,248,128]{2,1,0:T(8,128)}), f32[8,248,128]{2,1,0:T(8,128)S(1)}, u32[]{:S(2)}, u32[]{:S(2)}) async-start(f32[8,248,128]{2,1,0:T(8,128)} %legendre.1), calls=%async_computation.1 | async-start | bytes 2031616 | tf_op jit(solution)/shard_map/all_to_all | solution.py:456
  39.5 3.5 %wave_table.1 = (bf16[448,1024]{1,0:T(8,128)(2,1)S(1)}, bf16[448,1024]{1,0:T(8,128)(2,1)S(1)}) custom-call(s32[1,224]{1,0:T(1,128)S(1)} %bitcast.18), custom_call_target="tpu_custom_call" | custom-call | flops 9175040 | bytes 2097152 | tf_op jit(solution)/shard_map/wave_table/pallas_call | solution.py:519
  43.0 0.0 copy-start.6
  43.0 0.0 copy-start.8
  43.0 12.1 %all-to-all-done.1.spec_ref.obs_ref = f32[8,248,128]{2,1,0:T(8,128)S(1)} async-done(((f32[8,248,128]{2,1,0:T(8,128)}), f32[8,248,128]{2,1,0:T(8,128)S(1)}, u32[]{:S(2)}, u32[]{:S(2)}) %all-to-all-start.1) | async-done | bytes 1015840 | tf_op jit(solution)/shard_map/all_to_all | solution.py:456
  55.1 2.5 %synthesis.1 = f32[2688,128]{1,0:T(8,128)} custom-call(f32[8,248,128]{2,1,0:T(8,128)S(1)} %all-to-all-done.1.spec_ref.obs_ref, bf16[448,1024]{1,0:T(8,128)(2,1)S(1)} %get-tuple-element.8.high_ref, bf16[448,1024]{1,0:T(8,128)(2,1)S(1)} %get-tuple-element.9.low_ref), custom_call_target="tpu_custom_call" | custom-call | flops 1056964608 | bytes 4194304 | tf_op jit(solution)/shard_map/synthesis/pallas_call | solution.py:573
  57.7 4.6 %all-to-all-start.2 = ((f32[128,1,2688]{2,1,0:T(1,128)}), f32[128,1,2688]{2,1,0:T(1,128)S(1)}, u32[]{:S(2)}, u32[]{:S(2)}) async-start(f32[128,1,2688]{2,1,0:T(1,128)} %bitcast.3), calls=%async_computation.2 | async-start | bytes 2752512 | tf_op jit(solution)/shard_map/all_to_all | solution.py:456
  62.3 2.4 %flow.1.flow_ref = f32[384,8,128]{2,1,0:T(8,128)S(1)} custom-call(f32[28,96,128]{2,1,0:T(8,128)} %courant_ref.1), custom_call_target="tpu_custom_call" | custom-call | flops 2064384 | bytes 3145728 | tf_op jit(solution)/shard_map/flow/pallas_call | solution.py:586
  64.7 0.0 copy-start.12
  64.7 0.0 copy-start.13
  64.7 9.5 %sums.1.sums_ref = f32[3,256,128]{2,1,0:T(8,128)S(1)} custom-call(f32[8,248,128]{2,1,0:T(8,128)S(1)} %copy-done.1), custom_call_target="tpu_custom_call" | custom-call | flops 6442450944 | bytes 1048576 | tf_op jit(solution)/shard_map/sums/pallas_call | solution.py:558
  74.3 0.0 copy-start.10
  74.3 0.7 copy-done.10
  75.0 9.7 %all-to-all-done.2 = f32[128,1,2688]{2,1,0:T(1,128)S(1)} async-done(((f32[128,1,2688]{2,1,0:T(1,128)}), f32[128,1,2688]{2,1,0:T(1,128)S(1)}, u32[]{:S(2)}, u32[]{:S(2)}) %all-to-all-start.2) | async-done | bytes 1376288 | tf_op jit(solution)/shard_map/all_to_all | solution.py:456
  84.8 3.3 %grid_steps.1 = (f32[384,8,128]{2,1,0:T(8,128)S(1)}, f32[2688,128]{1,0:T(8,128)S(1)}) custom-call(f32[2688,128]{1,0:T(8,128)S(1)} %bitcast.10, f32[384,8,128]{2,1,0:T(8,128)S(1)} %flow.1.flow_ref, f32[3,256,128]{2,1,0:T(8,128)} %copy-done.10, f32[12]{0:T(128)S(1)} %copy-done.12, f32[96]{0:T(128)S(1)} %copy-done.13), custom_call_target="tpu_custom_call" | custom-call | flops 13762560 | bytes 6291456 | tf_op jit(solution)/shard_map/grid_steps/pallas_call | solution.py:596
  88.1 26.7 %all_to_all.30 = f32[128,1,2688]{2,1,0:T(1,128)S(1)} all-to-all(f32[128,1,2688]{2,1,0:T(1,128)S(1)} %bitcast.16), channel_id=1, replica_groups=mesh['wave'=8,'band'=16] {'wave','band'}, dimensions={0} | all-to-all | bytes 2752512 | tf_op jit(solution)/shard_map/all_to_all | solution.py:456
  114.8 2.3 %analysis.1 = f32[8,7,3,8,128]{4,3,2,1,0:T(8,128)} custom-call(f32[2688,128]{1,0:T(8,128)S(1)} %bitcast.17, bf16[448,1024]{1,0:T(8,128)(2,1)S(1)} %copy-done.7, bf16[448,1024]{1,0:T(8,128)(2,1)S(1)} %copy-done.9), custom_call_target="tpu_custom_call" | custom-call | flops 1056964608 | bytes 4194304 | tf_op jit(solution)/shard_map/analysis/pallas_call | solution.py:624
  117.1 3.5 %all-to-all-start.4 = ((f32[8,168,128]{2,1,0:T(8,128)}), f32[8,168,128]{2,1,0:T(8,128)S(1)}, u32[]{:S(2)}, u32[]{:S(2)}) async-start(f32[8,168,128]{2,1,0:T(8,128)} %bitcast.7), calls=%async_computation.4 | async-start | bytes 1376256 | tf_op jit(solution)/shard_map/all_to_all | solution.py:456
  120.7 1.5 head.3.head_ref
  122.2 10.5 %all-to-all-done.4.spec_ref = f32[8,168,128]{2,1,0:T(8,128)S(1)} async-done(((f32[8,168,128]{2,1,0:T(8,128)}), f32[8,168,128]{2,1,0:T(8,128)S(1)}, u32[]{:S(2)}, u32[]{:S(2)}) %all-to-all-start.4) | async-done | bytes 688160 | tf_op jit(solution)/shard_map/all_to_all | solution.py:456
  132.7 6.3 %legendre_adjoint.1 = f32[16,48,128]{2,1,0:T(8,128)} custom-call(f32[8,168,128]{2,1,0:T(8,128)S(1)} %all-to-all-done.4.spec_ref, f32[4,448,256]{2,1,0:T(8,128)S(1)} %head.3.head_ref, f32[28,448,256]{2,1,0:T(8,128)} %table_hbm.6), custom_call_target="tpu_custom_call" | custom-call | flops 924844032 | bytes 14680064 | tf_op jit(solution)/shard_map/legendre_adjoint/pallas_call | solution.py:634
  139.0 3.6 %all-to-all-start.5 = ((f32[16,48,128]{2,1,0:T(8,128)}), f32[16,48,128]{2,1,0:T(8,128)S(1)}, u32[]{:S(2)}, u32[]{:S(2)}) async-start(f32[16,48,128]{2,1,0:T(8,128)} %legendre_adjoint.1), calls=%async_computation.5 | async-start | bytes 786432 | tf_op jit(solution)/shard_map/all_to_all | solution.py:456
  142.6 1.4 copy-done.5
  144.0 1.7 %state.1 = f32[28,96,128]{2,1,0:T(8,128)} custom-call(f32[384,8,128]{2,1,0:T(8,128)S(1)} %copy-done.5), custom_call_target="tpu_custom_call" | custom-call | flops 2064384 | bytes 3145728 | tf_op jit(solution)/shard_map/state/pallas_call | solution.py:612
  145.8 6.7 %all-to-all-done.5 = f32[16,48,128]{2,1,0:T(8,128)S(1)} async-done(((f32[16,48,128]{2,1,0:T(8,128)}), f32[16,48,128]{2,1,0:T(8,128)S(1)}, u32[]{:S(2)}, u32[]{:S(2)}) %all-to-all-start.5) | async-done | bytes 393248 | tf_op jit(solution)/shard_map/all_to_all | solution.py:456
  152.5 2.0 %unmix.1 = f32[28,16,192]{2,1,0:T(8,128)} custom-call(f32[24,4,8,128]{3,2,1,0:T(8,128)S(1)} %bitcast.15, f32[28,16,192]{2,1,0:T(8,128)S(1)} %bitcast.12, f32[28,16,192]{2,1,0:T(8,128)S(1)} %bitcast.14, f32[96,96]{1,0:T(8,128)S(1)} %copy-done.11), custom_call_target="tpu_custom_call" | custom-call | flops 99090432 | bytes 1048576 | tf_op jit(solution)/shard_map/unmix/pallas_call | solution.py:646
  (22 shorter events, 0.0 us)
Async XLA Ops:
  4.1 21.7 %all-to-all-start = ((f32[16,88,128]{2,1,0:T(8,128)}), f32[16,88,128]{2,1,0:T(8,128)S(1)}, u32[]{:S(2)}, u32[]{:S(2)}) async-start(f32[16,88,128]{2,1,0:T(8,128)} %mix.1), calls=%async_computation | async-start | bytes 1441792 | tf_op jit(solution)/shard_map/all_to_all | solution.py:456
  35.2 4.3 %copy-start.14 = (s32[224]{0:T(256)S(1)}, s32[224]{0:T(256)}, u32[]{:S(2)}) copy-start(s32[224]{0:T(256)} %param.18) | copy-start | bytes 2692
  35.2 19.9 %all-to-all-start.1 = ((f32[8,248,128]{2,1,0:T(8,128)}), f32[8,248,128]{2,1,0:T(8,128)S(1)}, u32[]{:S(2)}, u32[]{:S(2)}) async-start(f32[8,248,128]{2,1,0:T(8,128)} %legendre.1), calls=%async_computation.1 | async-start | bytes 2031616 | tf_op jit(solution)/shard_map/all_to_all | solution.py:456
  43.0 14.6 %copy-start.6 = (bf16[448,1024]{1,0:T(8,128)(2,1)}, bf16[448,1024]{1,0:T(8,128)(2,1)S(1)}, u32[]{:S(2)}) copy-start(bf16[448,1024]{1,0:T(8,128)(2,1)S(1)} %get-tuple-element.8.high_ref) | copy-start | bytes 2752516
  43.0 14.6 %copy-start.8 = (bf16[448,1024]{1,0:T(8,128)(2,1)}, bf16[448,1024]{1,0:T(8,128)(2,1)S(1)}, u32[]{:S(2)}) copy-start(bf16[448,1024]{1,0:T(8,128)(2,1)S(1)} %get-tuple-element.9.low_ref) | copy-start | bytes 2752516
  55.1 2.5 %copy-start = (f32[8,248,128]{2,1,0:T(8,128)}, f32[8,248,128]{2,1,0:T(8,128)S(1)}, u32[]{:S(2)}) copy-start(f32[8,248,128]{2,1,0:T(8,128)S(1)} %all-to-all-done.1.spec_ref.obs_ref) | copy-start | bytes 3047428
  57.7 27.1 %all-to-all-start.2 = ((f32[128,1,2688]{2,1,0:T(1,128)}), f32[128,1,2688]{2,1,0:T(1,128)S(1)}, u32[]{:S(2)}, u32[]{:S(2)}) async-start(f32[128,1,2688]{2,1,0:T(1,128)} %bitcast.3), calls=%async_computation.2 | async-start | bytes 2752512 | tf_op jit(solution)/shard_map/all_to_all | solution.py:456
  62.3 2.4 %copy-start.1 = (f32[8,248,128]{2,1,0:T(8,128)S(1)}, f32[8,248,128]{2,1,0:T(8,128)}, u32[]{:S(2)}) copy-start(f32[8,248,128]{2,1,0:T(8,128)} %copy-done) | copy-start | bytes 3047428
  64.7 20.1 %copy-start.12 = (f32[12]{0:T(128)S(1)}, f32[12]{0:T(128)}, u32[]{:S(2)}) copy-start(f32[12]{0:T(128)} %lidar_ref.1) | copy-start | bytes 148
  64.7 20.0 %copy-start.13 = (f32[96]{0:T(128)S(1)}, f32[96]{0:T(128)}, u32[]{:S(2)}) copy-start(f32[96]{0:T(128)} %aod_ref.1) | copy-start | bytes 1156
  74.3 0.7 copy-start.10
  88.0 26.7 %copy-start.4 = (f32[384,8,128]{2,1,0:T(8,128)}, f32[384,8,128]{2,1,0:T(8,128)S(1)}, u32[]{:S(2)}) copy-start(f32[384,8,128]{2,1,0:T(8,128)S(1)} %get-tuple-element.13.hold_ref) | copy-start | bytes 4718596
  88.1 26.7 %copy-start.7 = (bf16[448,1024]{1,0:T(8,128)(2,1)S(1)}, bf16[448,1024]{1,0:T(8,128)(2,1)}, u32[]{:S(2)}) copy-start(bf16[448,1024]{1,0:T(8,128)(2,1)} %copy-done.6) | copy-start | bytes 2752516
  88.1 26.7 %copy-start.9 = (bf16[448,1024]{1,0:T(8,128)(2,1)S(1)}, bf16[448,1024]{1,0:T(8,128)(2,1)}, u32[]{:S(2)}) copy-start(bf16[448,1024]{1,0:T(8,128)(2,1)} %copy-done.8) | copy-start | bytes 2752516
  117.1 15.6 %all-to-all-start.4 = ((f32[8,168,128]{2,1,0:T(8,128)}), f32[8,168,128]{2,1,0:T(8,128)S(1)}, u32[]{:S(2)}, u32[]{:S(2)}) async-start(f32[8,168,128]{2,1,0:T(8,128)} %bitcast.7), calls=%async_computation.4 | async-start | bytes 1376256 | tf_op jit(solution)/shard_map/all_to_all | solution.py:456
  139.0 13.4 %all-to-all-start.5 = ((f32[16,48,128]{2,1,0:T(8,128)}), f32[16,48,128]{2,1,0:T(8,128)S(1)}, u32[]{:S(2)}, u32[]{:S(2)}) async-start(f32[16,48,128]{2,1,0:T(8,128)} %legendre_adjoint.1), calls=%async_computation.5 | async-start | bytes 786432 | tf_op jit(solution)/shard_map/all_to_all | solution.py:456
  142.6 1.4 copy-start.5
  144.0 8.4 %copy-start.2 = (f32[16,28,192]{2,0,1:T(8,128)S(1)}, f32[16,28,192]{2,0,1:T(8,128)}, u32[]{:S(2)}) copy-start(f32[16,28,192]{2,0,1:T(8,128)} %param.14) | copy-start | bytes 1032196
  144.0 8.4 %copy-start.3 = (f32[16,28,192]{2,0,1:T(8,128)S(1)}, f32[16,28,192]{2,0,1:T(8,128)}, u32[]{:S(2)}) copy-start(f32[16,28,192]{2,0,1:T(8,128)} %param.15) | copy-start | bytes 1032196
  144.0 8.4 %copy-start.11 = (f32[96,96]{1,0:T(8,128)S(1)}, f32[96,96]{1,0:T(8,128)}, u32[]{:S(2)}) copy-start(f32[96,96]{1,0:T(8,128)} %root_ref.1) | copy-start | bytes 110596

commit v5 on v4

--- a/solution.py
+++ b/solution.py
@@ -21,7 +21,6 @@
 NLAT = 448
 NT = 256
 TILE = 21
-HEAD = 4
 FACTOR = MW ** (-0.5)
 f32 = jnp.float32
 bf16 = jnp.bfloat16
@@ -148,35 +147,17 @@
             out_ref[c // 6, 8 * (c % 6) : 8 * (c % 6) + 8] = z[h]
 
 
-def head_kernel(table_hbm, out_ref, sem):
-    copy = pltpu.make_async_copy(table_hbm.at[pl.ds(0, HEAD)], out_ref, sem)
-    copy.start()
-    copy.wait()
-
-
 def table_copies(table_hbm, table_ref, sem):
-    copies = {}
-    first = HEAD
-    while first < 4 * GROUPS:
-        count = 4 - first % 4
-        source = table_hbm.at[pl.ds(first, count)]
-        target = table_ref.at[pl.ds(first - HEAD, count)]
-        copies[first] = pltpu.make_async_copy(source, target, sem.at[len(copies)])
-        first += count
-    for copy in copies.values():
+    copies = []
+    for g in range(GROUPS):
+        at = pl.ds(4 * g, 4)
+        copies.append(pltpu.make_async_copy(table_hbm.at[at], table_ref.at[at], sem.at[g]))
+    for copy in copies:
         copy.start()
     return copies
 
 
-def table_slot(m, copies, head_ref, table_ref):
-    if m < HEAD:
-        return head_ref[m]
-    if m in copies:
-        copies[m].wait()
-    return table_ref[m - HEAD]
-
-
-def legendre_kernel(modes_ref, head_ref, table_hbm, out_ref, x_ref, acc_ref, table_ref, sem):
+def legendre_kernel(modes_ref, table_hbm, out_ref, x_ref, acc_ref, table_ref, sem):
     copies = table_copies(table_hbm, table_ref, sem)
     for half in range(2):
         for c in range(6):
@@ -194,11 +175,12 @@
     slot = (iota((48, NT), 0) % 8) // 2
     order = lat_order()
     for g in range(GROUPS):
+        copies[g].wait()
         x = x_ref[g]
         acc = None
         for m4 in range(4):
             xh, xl = split(jnp.where(slot == m4, x, 0.0))
-            both = jnp.concatenate(split(table_slot(4 * g + m4, copies, head_ref, table_ref)), axis=0)
+            both = jnp.concatenate(split(table_ref[4 * g + m4]), axis=0)
             both = mm_nt(jnp.concatenate([xh, xl], axis=0), both)
             part = both[:48, :NLAT] + (both[48:, :NLAT] + both[:48, NLAT:])
             acc = part if acc is None else acc + part
@@ -297,7 +279,7 @@
         out_ref[:, :, c] = rows.reshape(WAVES, GROUPS, 8, 128)
 
 
-def legendre_adjoint_kernel(spec_ref, head_ref, table_hbm, out_ref, acc_ref, table_ref, sem):
+def legendre_adjoint_kernel(spec_ref, table_hbm, out_ref, acc_ref, table_ref, sem):
     copies = table_copies(table_hbm, table_ref, sem)
     order = lat_order()
     for hc in range(2):
@@ -307,12 +289,13 @@
     slot = (iota((48, NLAT), 0) % 8) // 2
     x = []
     for g in range(GROUPS):
+        copies[g].wait()
         rows = [acc_ref[168 * hc + 24 * g : 168 * hc + 24 * g + 24] for hc in range(2)]
         mine = jnp.concatenate(rows, axis=0)
         acc = None
         for m4 in range(4):
             xh, xl = split(jnp.where(slot == m4, mine, 0.0))
-            th, tl = split(table_slot(4 * g + m4, copies, head_ref, table_ref))
+            th, tl = split(table_ref[4 * g + m4])
             both = mm(jnp.concatenate([xh, xl], axis=0), th)
             part = both[:48] + both[48:] + mm(xh, tl)
             acc = part if acc is None else acc + part
@@ -386,14 +369,9 @@
             out_ref[8 * h + j] = z
 
 
-def state_kernel(hold_ref, out_ref):
-    for h in range(12):
-        rows = turn([hold_ref[8 * h + j] for j in range(8)], 0, 1)
-        for t in range(7):
-            out_ref[t, 8 * h : 8 * h + 8] = rows[t]
-
-
-def grid_kernel(grid_ref, flow_ref, sums_ref, lidar_ref, aod_ref, hold_ref, adjoint_ref):
+def grid_kernel(
+    grid_ref, flow_ref, sums_ref, lidar_ref, aod_ref, state_ref, adjoint_ref, hold_ref
+):
     def tile_rows(l, b2, hc, c):
         return pl.ds(TILE * (BANDS * hc + 2 * l + b2) + 7 * c, 7)
 
@@ -417,6 +395,11 @@
             lidar_sum[l] = x[l] * coef if lidar_sum[l] is None else lidar_sum[l] + x[l] * coef
             term = x[l] * aod_ref[BINS * l + bin_at]
             aod_sum = term if aod_sum is None else aod_sum + term
+
+    for h in range(12):
+        rows = turn([hold_ref[8 * h + j] for j in range(8)], 0, 1)
+        for t in range(7):
+            state_ref[t, 8 * h : 8 * h + 8] = rows[t]
 
     weight = [sums_ref[0, 8 * l : 8 * l + 8] for l in range(LEV)]
     lidar = [weight[l] * lidar_sum[l] - sums_ref[1, 8 * l : 8 * l + 8] for l in range(LEV)]
@@ -523,26 +506,12 @@
         cost_estimate=cost(20 * 448 * 1024, 2 << 20),
         name="wave_table",
     )(zonal_number.reshape(1, MW))
-
-
-    def head(table):
-        return pl.pallas_call(
-            head_kernel,
-            in_specs=[hbm],
-            out_specs=whole(HEAD, NLAT, NT),
-            out_shape=shape(HEAD, NLAT, NT),
-            scratch_shapes=[pltpu.SemaphoreType.DMA(())],
-            compiler_params=params(),
-            cost_estimate=cost(0, 8 * HEAD * NLAT * NT),
-            name="head",
-        )(in_hbm(table))
-
     legendre_cost = cost(6 * 28 * 448 * 256 * 48, 14 << 20)
     in_order = params(dimension_semantics=("arbitrary",))
-    table_scratch = [pltpu.VMEM((28 - HEAD, NLAT, NT), f32), pltpu.SemaphoreType.DMA((GROUPS,))]
+    table_scratch = [pltpu.VMEM((28, NLAT, NT), f32), pltpu.SemaphoreType.DMA((GROUPS,))]
     spec = pl.pallas_call(
         legendre_kernel,
-        in_specs=[whole(BANDS, 88, 128), whole(HEAD, NLAT, NT), hbm],
+        in_specs=[whole(BANDS, 88, 128), hbm],
         out_specs=whole(WAVES, 248, 128),
         out_shape=shape(WAVES, 248, 128),
         scratch_shapes=[
@@ -553,7 +522,7 @@
         compiler_params=params(),
         cost_estimate=legendre_cost,
         name="legendre",
-    )(modes, head(legendre), in_hbm(legendre))
+    )(modes, in_hbm(legendre))
     spec = exchange(spec, "wave")
     sums = pl.pallas_call(
         sums_kernel,
@@ -593,7 +562,7 @@
         cost_estimate=cost(6 * 28 * 96 * 128, 3 << 20),
         name="flow",
     )(in_hbm(courant))
-    hold, adjoint = pl.pallas_call(
+    state, adjoint = pl.pallas_call(
         grid_kernel,
         grid=(4,),
         in_specs=[
@@ -603,22 +572,13 @@
             scalars,
             scalars,
         ],
-        out_specs=(turned, tile_spec),
-        out_shape=(shape(4 * CH, 8, 128), tiles),
+        out_specs=(field, tile_spec),
+        out_shape=(shape(28, CH, 128), tiles),
+        scratch_shapes=[pltpu.VMEM((CH, 8, 128), f32)],
         compiler_params=in_order,
         cost_estimate=cost(40 * 28 * 96 * 128, 6 << 20),
         name="grid_steps",
     )(grid, flow, in_hbm(sums), lidar_coef, aod_coef)
-    state = pl.pallas_call(
-        state_kernel,
-        grid=(4,),
-        in_specs=[turned],
-        out_specs=field,
-        out_shape=shape(28, CH, 128),
-        compiler_params=in_order,
-        cost_estimate=cost(6 * 28 * 96 * 128, 3 << 20),
-        name="state",
-    )(hold)
     adjoint = exchange_tiles(adjoint)
 
     spec = pl.pallas_call(
@@ -628,19 +588,18 @@
         cost_estimate=wave_cost,
         name="analysis",
     )(adjoint, high, low)
-    again, spec = lax.optimization_barrier((legendre, spec))
     spec = exchange(spec.reshape(WAVES, 24 * GROUPS, 128), "wave")
 
     modes = pl.pallas_call(
         legendre_adjoint_kernel,
-        in_specs=[whole(WAVES, 168, 128), whole(HEAD, NLAT, NT), hbm],
+        in_specs=[whole(WAVES, 168, 128), hbm],
         out_specs=whole(BANDS, 48, 128),
         out_shape=shape(BANDS, 48, 128),
         scratch_shapes=[pltpu.VMEM((336, NLAT), f32), *table_scratch],
         compiler_params=params(),
         cost_estimate=legendre_cost,
         name="legendre_adjoint",
-    )(spec, head(again), in_hbm(legendre))
+    )(spec, in_hbm(legendre))
     modes = exchange(modes, "band").reshape(24, 4, 8, 128)
 
     gradient = pl.pallas_call(

time: 155 us -> 152 us (0.981)
  blocking collectives: 26.7 us -> 75.2 us
  waiting for transfers between devices: 51.1 us -> 21.8 us
  starting transfers between devices: 24.2 us -> 9.13 us
  Pallas kernels: 49.3 us -> 43.6 us
    all_to_all x1 -> x4, blocking collectives: 26.7 us -> 75.2 us  [exchange(): return lax.all_to_all(tiles, axis, split_axis=0, concat_axis=0, tiled=True)]
    all_to_all x5 -> x2, waiting for transfers between devices: 51.1 us -> 21.8 us  [exchange(): return lax.all_to_all(tiles, axis, split_axis=0, concat_axis=0, tiled=True)]
    all_to_all x5 -> x2, starting transfers between devices: 24.2 us -> 9.13 us  [exchange(): return lax.all_to_all(tiles, axis, split_axis=0, concat_axis=0, tiled=True)]
    pallas_call x4 -> x1, Pallas kernels: 14.1 us -> 9.04 us  [body(): pl.pallas_call(legendre_kernel, in_specs=[whole(BANDS, 88, 128), hbm], ou...]
  transfers between devices with their start and end apart: 5 -> 2, of which waited for: 5 -> 2; matrix products, arithmetic and copies ran while one was open for 0% -> 0% of each run, Pallas kernels for 13% -> 10%
where the time goes in v5:
time: 152 us; the launch traced here: 151 us
  blocking collectives  75.2 us (49%)
  Pallas kernels  43.6 us (29%)
  waiting for transfers between devices  21.8 us (14%)
  starting transfers between devices  9.13 us (6%)
    all_to_all x4, blocking collectives, exchange(): return lax.all_to_all(tiles, axis, split_axis=0, concat_axis=0, tiled=True)  75.2 us
    all_to_all x2, waiting for transfers between devices, exchange(): return lax.all_to_all(tiles, axis, split_axis=0, concat_axis=0, tiled=True)  21.8 us
    pallas_call x1, Pallas kernels, body(): pl.pallas_call(sums_kernel, grid=(WAVES,), in_specs=[pl.BlockSpec((1, 248...  9.53 us
    all_to_all x2, starting transfers between devices, exchange(): return lax.all_to_all(tiles, axis, split_axis=0, concat_axis=0, tiled=True)  9.13 us
    pallas_call x1, Pallas kernels, body(): pl.pallas_call(legendre_kernel, in_specs=[whole(BANDS, 88, 128), hbm], ou...  9.04 us
    pallas_call x1, Pallas kernels, body(): pl.pallas_call(legendre_adjoint_kernel, in_specs=[whole(WAVES, 168, 128),...  6.51 us
    pallas_call x1, Pallas kernels, body(): pl.pallas_call(grid_kernel, grid=(4,), in_specs=[tile_spec, turned, pl.Bl...  4.22 us
    pallas_call x1, Pallas kernels, body(): pl.pallas_call(wave_table_kernel, out_shape=(shape(2 * MW, NLON, kind=bf1...  3.48 us
  transfers between devices with their start and end apart: 2, of which 2 were waited for; matrix products, arithmetic and copies ran while one was open for 0% of the time, Pallas kernels for 10%

profile of v5, /device:TPU:0, one launch (start us, length us, event | category | flops | bytes accessed | tf_op | source)
XLA Modules:
  0.0 151.3 jit_solution(13426827256251548363)
XLA Ops:
  0.6 2.6 %mix.1 = f32[16,88,128]{2,1,0:T(8,128)S(1)} custom-call(f32[28,16,192]{2,1,0:T(8,128)} %bitcast.11, f32[28,16,192]{2,1,0:T(8,128)} %bitcast.13, f32[96,96]{1,0:T(8,128)} %root_ref.1, s32[128,128]{1,0:T(8,128)} %column_hbm.1, s32[128,128]{1,0:T(8,128)} %level_hbm.1, f32[128,128]{1,0:T(8,128)} %lidar_hbm.1, f32[128,128]{1,0:T(8,128)} %aod_hbm.1, ...), custom_call_target="tpu_custom_call" | custom-call | flops 99090432 | bytes 1048576 | tf_op jit(solution)/shard_map/mix/pallas_call | solution.py:466
  3.2 21.4 %all_to_all.30.modes_ref = f32[16,88,128]{2,1,0:T(8,128)S(1)} all-to-all(f32[16,88,128]{2,1,0:T(8,128)S(1)} %mix.1), channel_id=1, replica_groups=mesh['wave'=8,'band'=16] {'band'}, dimensions={0} | all-to-all | bytes 1441792 | tf_op jit(solution)/shard_map/all_to_all | solution.py:439
  24.6 9.0 %legendre.1 = f32[8,248,128]{2,1,0:T(8,128)} custom-call(f32[16,88,128]{2,1,0:T(8,128)S(1)} %all_to_all.30.modes_ref, f32[28,448,256]{2,1,0:T(8,128)} %table_hbm.3), custom_call_target="tpu_custom_call" | custom-call | flops 924844032 | bytes 14680064 | tf_op jit(solution)/shard_map/legendre/pallas_call | solution.py:512
  33.7 0.0 copy-start.12
  33.7 4.3 %all-to-all-start.1 = ((f32[8,248,128]{2,1,0:T(8,128)}), f32[8,248,128]{2,1,0:T(8,128)S(1)}, u32[]{:S(2)}, u32[]{:S(2)}) async-start(f32[8,248,128]{2,1,0:T(8,128)} %legendre.1), calls=%async_computation.1 | async-start | bytes 2031616 | tf_op jit(solution)/shard_map/all_to_all | solution.py:439
  38.0 0.0 copy-done.12
  38.0 3.5 %wave_table.1 = (bf16[448,1024]{1,0:T(8,128)(2,1)S(1)}, bf16[448,1024]{1,0:T(8,128)(2,1)S(1)}) custom-call(s32[1,224]{1,0:T(1,128)S(1)} %bitcast.19), custom_call_target="tpu_custom_call" | custom-call | flops 9175040 | bytes 2097152 | tf_op jit(solution)/shard_map/wave_table/pallas_call | solution.py:502
  41.5 0.0 copy-start.4
  41.5 0.0 copy-start.6
  41.5 12.1 %all-to-all-done.1.spec_ref.obs_ref = f32[8,248,128]{2,1,0:T(8,128)S(1)} async-done(((f32[8,248,128]{2,1,0:T(8,128)}), f32[8,248,128]{2,1,0:T(8,128)S(1)}, u32[]{:S(2)}, u32[]{:S(2)}) %all-to-all-start.1) | async-done | bytes 1015840 | tf_op jit(solution)/shard_map/all_to_all | solution.py:439
  53.6 2.5 %synthesis.1 = f32[2688,128]{1,0:T(8,128)} custom-call(f32[8,248,128]{2,1,0:T(8,128)S(1)} %all-to-all-done.1.spec_ref.obs_ref, bf16[448,1024]{1,0:T(8,128)(2,1)S(1)} %get-tuple-element.6.high_ref, bf16[448,1024]{1,0:T(8,128)(2,1)S(1)} %get-tuple-element.7.low_ref), custom_call_target="tpu_custom_call" | custom-call | flops 1056964608 | bytes 4194304 | tf_op jit(solution)/shard_map/synthesis/pallas_call | solution.py:542
  56.1 0.0 copy-done.4
  56.1 0.0 copy-done.6
  56.1 0.0 copy-done
  56.1 4.8 %all-to-all-start.2 = ((f32[128,1,2688]{2,1,0:T(1,128)}), f32[128,1,2688]{2,1,0:T(1,128)S(1)}, u32[]{:S(2)}, u32[]{:S(2)}) async-start(f32[128,1,2688]{2,1,0:T(1,128)} %bitcast.3), calls=%async_computation.2 | async-start | bytes 2752512 | tf_op jit(solution)/shard_map/all_to_all | solution.py:439
  60.9 0.0 copy-start.1
  61.0 2.4 %flow.1.flow_ref = f32[384,8,128]{2,1,0:T(8,128)S(1)} custom-call(f32[28,96,128]{2,1,0:T(8,128)} %courant_ref.1), custom_call_target="tpu_custom_call" | custom-call | flops 2064384 | bytes 3145728 | tf_op jit(solution)/shard_map/flow/pallas_call | solution.py:555
  63.3 0.0 copy-done.1
  63.3 0.0 copy-start.10
  63.4 0.0 copy-start.11
  63.4 9.5 %sums.1.sums_ref = f32[3,256,128]{2,1,0:T(8,128)S(1)} custom-call(f32[8,248,128]{2,1,0:T(8,128)S(1)} %copy-done.1), custom_call_target="tpu_custom_call" | custom-call | flops 6442450944 | bytes 1048576 | tf_op jit(solution)/shard_map/sums/pallas_call | solution.py:527
  72.9 0.0 copy-start.8
  72.9 0.7 copy-done.8
  73.7 9.7 %all-to-all-done.2 = f32[128,1,2688]{2,1,0:T(1,128)S(1)} async-done(((f32[128,1,2688]{2,1,0:T(1,128)}), f32[128,1,2688]{2,1,0:T(1,128)S(1)}, u32[]{:S(2)}, u32[]{:S(2)}) %all-to-all-start.2) | async-done | bytes 1376288 | tf_op jit(solution)/shard_map/all_to_all | solution.py:439
  83.4 4.2 %grid_steps.1 = (f32[28,96,128]{2,1,0:T(8,128)}, f32[2688,128]{1,0:T(8,128)S(1)}) custom-call(f32[2688,128]{1,0:T(8,128)S(1)} %bitcast.10, f32[384,8,128]{2,1,0:T(8,128)S(1)} %flow.1.flow_ref, f32[3,256,128]{2,1,0:T(8,128)} %copy-done.8, f32[12]{0:T(128)S(1)} %copy-done.10, f32[96]{0:T(128)S(1)} %copy-done.11), custom_call_target="tpu_custom_call" | custom-call | flops 13762560 | bytes 6291456 | tf_op jit(solution)/shard_map/grid_steps/pallas_call | solution.py:565
  87.6 26.6 %all_to_all.31 = f32[128,1,2688]{2,1,0:T(1,128)S(1)} all-to-all(f32[128,1,2688]{2,1,0:T(1,128)S(1)} %bitcast.16), channel_id=1, replica_groups=mesh['wave'=8,'band'=16] {'wave','band'}, dimensions={0} | all-to-all | bytes 2752512 | tf_op jit(solution)/shard_map/all_to_all | solution.py:439
  114.2 1.4 analysis.1
  115.6 14.8 %all_to_all.32.spec_ref = f32[8,168,128]{2,1,0:T(8,128)S(1)} all-to-all(f32[8,168,128]{2,1,0:T(8,128)S(1)} %bitcast.18), channel_id=1, replica_groups=mesh['wave'=8,'band'=16] {'wave'}, dimensions={0} | all-to-all | bytes 1376256 | tf_op jit(solution)/shard_map/all_to_all | solution.py:439
  130.4 6.5 %legendre_adjoint.1 = f32[16,48,128]{2,1,0:T(8,128)S(1)} custom-call(f32[8,168,128]{2,1,0:T(8,128)S(1)} %all_to_all.32.spec_ref, f32[28,448,256]{2,1,0:T(8,128)} %table_hbm.3), custom_call_target="tpu_custom_call" | custom-call | flops 924844032 | bytes 14680064 | tf_op jit(solution)/shard_map/legendre_adjoint/pallas_call | solution.py:593
  136.9 12.5 %all_to_all.33 = f32[16,48,128]{2,1,0:T(8,128)S(1)} all-to-all(f32[16,48,128]{2,1,0:T(8,128)S(1)} %legendre_adjoint.1), channel_id=1, replica_groups=mesh['wave'=8,'band'=16] {'band'}, dimensions={0} | all-to-all | bytes 786432 | tf_op jit(solution)/shard_map/all_to_all | solution.py:439
  149.4 0.0 copy-done.9
  149.4 2.0 %unmix.1 = f32[28,16,192]{2,1,0:T(8,128)} custom-call(f32[24,4,8,128]{3,2,1,0:T(8,128)S(1)} %bitcast.15, f32[28,16,192]{2,1,0:T(8,128)S(1)} %bitcast.12, f32[28,16,192]{2,1,0:T(8,128)S(1)} %bitcast.14, f32[96,96]{1,0:T(8,128)S(1)} %copy-done.9), custom_call_target="tpu_custom_call" | custom-call | flops 99090432 | bytes 1048576 | tf_op jit(solution)/shard_map/unmix/pallas_call | solution.py:605
  (12 shorter events, 0.0 us)
Async XLA Ops:
  33.7 4.3 %copy-start.12 = (s32[224]{0:T(256)S(1)}, s32[224]{0:T(256)}, u32[]{:S(2)}) copy-start(s32[224]{0:T(256)} %param.18) | copy-start | bytes 2692
  33.7 19.9 %all-to-all-start.1 = ((f32[8,248,128]{2,1,0:T(8,128)}), f32[8,248,128]{2,1,0:T(8,128)S(1)}, u32[]{:S(2)}, u32[]{:S(2)}) async-start(f32[8,248,128]{2,1,0:T(8,128)} %legendre.1), calls=%async_computation.1 | async-start | bytes 2031616 | tf_op jit(solution)/shard_map/all_to_all | solution.py:439
  41.5 14.6 %copy-start.4 = (bf16[448,1024]{1,0:T(8,128)(2,1)}, bf16[448,1024]{1,0:T(8,128)(2,1)S(1)}, u32[]{:S(2)}) copy-start(bf16[448,1024]{1,0:T(8,128)(2,1)S(1)} %get-tuple-element.6.high_ref) | copy-start | bytes 2752516
  41.5 14.6 %copy-start.6 = (bf16[448,1024]{1,0:T(8,128)(2,1)}, bf16[448,1024]{1,0:T(8,128)(2,1)S(1)}, u32[]{:S(2)}) copy-start(bf16[448,1024]{1,0:T(8,128)(2,1)S(1)} %get-tuple-element.7.low_ref) | copy-start | bytes 2752516
  53.6 2.5 %copy-start = (f32[8,248,128]{2,1,0:T(8,128)}, f32[8,248,128]{2,1,0:T(8,128)S(1)}, u32[]{:S(2)}) copy-start(f32[8,248,128]{2,1,0:T(8,128)S(1)} %all-to-all-done.1.spec_ref.obs_ref) | copy-start | bytes 3047428
  56.1 27.3 %all-to-all-start.2 = ((f32[128,1,2688]{2,1,0:T(1,128)}), f32[128,1,2688]{2,1,0:T(1,128)S(1)}, u32[]{:S(2)}, u32[]{:S(2)}) async-start(f32[128,1,2688]{2,1,0:T(1,128)} %bitcast.3), calls=%async_computation.2 | async-start | bytes 2752512 | tf_op jit(solution)/shard_map/all_to_all | solution.py:439
  60.9 2.4 %copy-start.1 = (f32[8,248,128]{2,1,0:T(8,128)S(1)}, f32[8,248,128]{2,1,0:T(8,128)}, u32[]{:S(2)}) copy-start(f32[8,248,128]{2,1,0:T(8,128)} %copy-done) | copy-start | bytes 3047428
  63.3 20.1 %copy-start.10 = (f32[12]{0:T(128)S(1)}, f32[12]{0:T(128)}, u32[]{:S(2)}) copy-start(f32[12]{0:T(128)} %lidar_ref.1) | copy-start | bytes 148
  63.4 20.0 %copy-start.11 = (f32[96]{0:T(128)S(1)}, f32[96]{0:T(128)}, u32[]{:S(2)}) copy-start(f32[96]{0:T(128)} %aod_ref.1) | copy-start | bytes 1156
  72.9 0.7 copy-start.8
  87.6 26.6 %copy-start.5 = (bf16[448,1024]{1,0:T(8,128)(2,1)S(1)}, bf16[448,1024]{1,0:T(8,128)(2,1)}, u32[]{:S(2)}) copy-start(bf16[448,1024]{1,0:T(8,128)(2,1)} %copy-done.4) | copy-start | bytes 2752516
  87.6 26.6 %copy-start.7 = (bf16[448,1024]{1,0:T(8,128)(2,1)S(1)}, bf16[448,1024]{1,0:T(8,128)(2,1)}, u32[]{:S(2)}) copy-start(bf16[448,1024]{1,0:T(8,128)(2,1)} %copy-done.6) | copy-start | bytes 2752516
  130.4 19.0 %copy-start.2 = (f32[16,28,192]{2,0,1:T(8,128)S(1)}, f32[16,28,192]{2,0,1:T(8,128)}, u32[]{:S(2)}) copy-start(f32[16,28,192]{2,0,1:T(8,128)} %param.14) | copy-start | bytes 1032196
  130.4 19.0 %copy-start.3 = (f32[16,28,192]{2,0,1:T(8,128)S(1)}, f32[16,28,192]{2,0,1:T(8,128)}, u32[]{:S(2)}) copy-start(f32[16,28,192]{2,0,1:T(8,128)} %param.15) | copy-start | bytes 1032196
  130.4 19.0 %copy-start.9 = (f32[96,96]{1,0:T(8,128)S(1)}, f32[96,96]{1,0:T(8,128)}, u32[]{:S(2)}) copy-start(f32[96,96]{1,0:T(8,128)} %root_ref.1) | copy-start | bytes 110596

commit v6 on v5

--- a/solution.py
+++ b/solution.py
@@ -76,63 +76,20 @@
     return jnp.where(same, wide, 0.0)
 
 
-def mix_kernel(
-    control_hbm,
-    scale_hbm,
-    root_hbm,
-    column_hbm,
-    level_hbm,
-    lidar_hbm,
-    aod_hbm,
-    weight_hbm,
-    count_hbm,
-    out_ref,
-    control_ref,
-    scale_ref,
-    root_ref,
-    index_ref,
-    value_ref,
-    count_ref,
-    obs_ref,
-    sem,
-):
+def mix_kernel(control_hbm, scale_hbm, root_hbm, out_ref, control_ref, scale_ref, root_ref, sem):
     copies = [
         pltpu.make_async_copy(source, target, sem.at[k])
         for k, (source, target) in enumerate(
-            (
-                (root_hbm, root_ref),
-                (control_hbm, control_ref),
-                (scale_hbm, scale_ref),
-                (column_hbm, index_ref.at[0]),
-                (level_hbm, index_ref.at[1]),
-                (lidar_hbm, value_ref.at[0]),
-                (aod_hbm, value_ref.at[1]),
-                (weight_hbm, value_ref.at[2]),
-                (count_hbm, count_ref),
-            )
+            ((root_hbm, root_ref), (control_hbm, control_ref), (scale_hbm, scale_ref))
         )
     ]
-    for copy in copies[3:] + copies[:3]:
+    for copy in copies:
         copy.start()
-    for copy in copies[3:]:
-        copy.wait()
-    counts = jnp.broadcast_to(count_ref[...].astype(f32), (DEVICES, DEVICES)).T
-    live = iota((DEVICES, SLOT), 1).astype(f32) < counts
-    weight = jnp.where(live, value_ref[2], 0.0)
-    obs_ref[0] = index_ref[0].astype(f32)
-    obs_ref[1] = index_ref[1].astype(f32)
-    obs_ref[2] = weight
-    obs_ref[3] = weight * value_ref[0]
-    obs_ref[4] = weight * value_ref[1]
-    for band in range(BANDS):
-        for k in range(5):
-            rows = obs_ref[k, pl.ds(band, WAVES, stride=BANDS), :]
-            out_ref[band, 48 + 8 * k : 56 + 8 * k] = rows
-
-    for copy in copies[:3]:
-        copy.wait()
+    copies[0].wait()
     root = doubled_root(root_ref[...])
     rh, rl = split(root)
+    copies[1].wait()
+    copies[2].wait()
     tiles = []
     for m4 in range(4):
         x = jnp.concatenate([control_ref[4 * g + m4] for g in range(GROUPS)], axis=0)
@@ -147,6 +104,46 @@
             out_ref[c // 6, 8 * (c % 6) : 8 * (c % 6) + 8] = z[h]
 
 
+def pack_kernel(count_ref, column_ref, level_ref, lidar_ref, aod_ref, weight_ref, out_ref):
+    me = lax.axis_index("wave")
+    counts = jnp.broadcast_to(count_ref[...].astype(f32), (DEVICES, DEVICES)).T
+    for wave in range(WAVES):
+        at = pl.ds(BANDS * wave, BANDS)
+        live = iota((BANDS, SLOT), 1).astype(f32) < counts[BANDS * wave : BANDS * wave + BANDS]
+        weight = jnp.where(live, weight_ref[at, :], 0.0)
+        tile = (
+            column_ref[at, :].astype(f32),
+            level_ref[at, :].astype(f32),
+            weight,
+            weight * lidar_ref[at, :],
+            weight * aod_ref[at, :],
+        )
+        s = (wave - me + WAVES) % WAVES
+        for k in range(5):
+            out_ref[s, BANDS * k : BANDS * k + BANDS] = tile[k]
+
+
+def to_y_kernel(*refs):
+    out_ref = refs[-1]
+    me = lax.axis_index("band") // 4
+    for y in range(4):
+        s = (y - me + 4) % 4
+        for k in range(5):
+            rows = [ref[16 * k + 4 * y : 16 * k + 4 * y + 4] for ref in refs[:-1]]
+            out_ref[s, 32 * k : 32 * k + 32] = jnp.concatenate(rows, axis=0)
+
+
+def to_z_kernel(*refs):
+    out_ref = refs[-1]
+    me = lax.axis_index("band") % 4
+    for z in range(4):
+        s = (z - me + 4) % 4
+        for k in range(5):
+            for i, ref in enumerate(refs[:-1]):
+                at = 32 * k + 8 * i
+                out_ref[s, at : at + 8] = ref[pl.ds(32 * k + z, 8, stride=4), :]
+
+
 def table_copies(table_hbm, table_ref, sem):
     copies = []
     for g in range(GROUPS):
@@ -165,13 +162,6 @@
             for g, z in enumerate(turn(got, 1, 16)):
                 if g < GROUPS:
                     x_ref[g, 8 * c : 8 * c + 8, 128 * half : 128 * half + 128] = z
-    for k in range(5):
-        for half in range(2):
-            got = [modes_ref[8 * half + s, 48 + 8 * k : 56 + 8 * k] for s in range(8)]
-            at = 168 + 16 * k + 8 * half
-            for w, z in enumerate(turn(got, 0, 1)):
-                out_ref[w, at : at + 8] = z
-
     slot = (iota((48, NT), 0) % 8) // 2
     order = lat_order()
     for g in range(GROUPS):
@@ -238,7 +228,7 @@
 
 
 def synthesis_kernel(spec_ref, high_ref, low_ref, out_ref, lhs_ref):
-    rows = spec_ref[:, :168].reshape(WAVES, GROUPS, 3, 8, 128)
+    rows = spec_ref[...].reshape(WAVES, GROUPS, 3, 8, 128)
     for c in range(3):
         high, low = split(rows[:, :, c].reshape(2 * MW, 128).T)
         lhs_ref[128 * c : 128 * c + 128] = high
@@ -322,44 +312,34 @@
             out_ref[m] = control_ref[m] + z[16 * g : 16 * g + 16]
 
 
-def sums_kernel(obs_ref, out_ref, acc_ref):
-    i = pl.program_id(0)
-    part = None
-    for half in range(2):
-
-        def line(k):
-            at = 168 + 16 * k + 8 * half
-            rows = obs_ref[0, at : at + 8]
-            return jnp.concatenate([rows[s : s + 1] for s in range(8)], axis=1)
-
-        column = line(0).astype(jnp.int32)
-        level = line(1).astype(jnp.int32)
-        lat = column // 128
-        lon = column % 128
-        q = sum((lat >= 7 * k).astype(jnp.int32) for k in range(1, 4))
-        row = q * 64 + level * 8 + (lat - 7 * q)
-        rows = jnp.where(iota((256, 1024), 0) == row, 1.0, 0.0).astype(bf16)
-        cols = jnp.where(iota((128, 1024), 0) == lon, 1.0, 0.0).astype(bf16)
-        values = []
-        for k in range(2, 5):
-            for v in split(line(k)):
-                values.append(cols * v)
-        new = mm_nt(rows, jnp.concatenate(values, axis=0))
-        part = new if part is None else part + new
-
-    @pl.when(i == 0)
-    def _():
-        acc_ref[...] = part
-
-    @pl.when(i > 0)
-    def _():
-        acc_ref[...] += part
-
-    @pl.when(i == WAVES - 1)
-    def _():
-        for k in range(3):
-            first = acc_ref[:, 256 * k : 256 * k + 128]
-            out_ref[k] = first + acc_ref[:, 256 * k + 128 : 256 * k + 256]
+def sums_kernel(*refs):
+    out_ref, acc_ref = refs[-2:]
+    acc_ref[...] = jnp.zeros_like(acc_ref)
+    for ref in refs[:-2]:
+
+        @pl.loop(0, 4)
+        def _(i):
+            def line(k):
+                rows = ref[pl.ds(pl.multiple_of(32 * k + 8 * i, 8), 8), :]
+                return jnp.concatenate([rows[s : s + 1] for s in range(8)], axis=1)
+
+            column = line(0).astype(jnp.int32)
+            level = line(1).astype(jnp.int32)
+            lat = column // 128
+            lon = column % 128
+            q = sum((lat >= 7 * k).astype(jnp.int32) for k in range(1, 4))
+            row = q * 64 + level * 8 + (lat - 7 * q)
+            rows = jnp.where(iota((256, 1024), 0) == row, 1.0, 0.0).astype(bf16)
+            cols = jnp.where(iota((128, 1024), 0) == lon, 1.0, 0.0).astype(bf16)
+            values = []
+            for k in range(2, 5):
+                for v in split(line(k)):
+                    values.append(cols * v)
+            acc_ref[...] += mm_nt(rows, jnp.concatenate(values, axis=0))
+
+    for k in range(3):
+        first = acc_ref[:, 256 * k : 256 * k + 128]
+        out_ref[k] = first + acc_ref[:, 256 * k + 128 : 256 * k + 256]
 
 
 def flow_kernel(courant_ref, out_ref):
@@ -437,6 +417,45 @@
 
 def exchange(tiles, axis):
     return lax.all_to_all(tiles, axis, split_axis=0, concat_axis=0, tiled=True)
+
+
+def shifted(tiles, axis, places):
+    count = lax.axis_size(axis)
+    got = [tiles[0]]
+    for s in range(1, tiles.shape[0]):
+        got.append(lax.ppermute(tiles[s], axis, [(i, places(i, s)) for i in range(count)]))
+    return got
+
+
+def packed(*arrays):
+    return pl.pallas_call(
+        pack_kernel,
+        out_shape=shape(WAVES, 5 * BANDS, SLOT),
+        compiler_params=params(),
+        cost_estimate=cost(10 * 16384, 1 << 20),
+        name="pack",
+    )(*arrays)
+
+
+def regrouped(kernel, got, name):
+    return pl.pallas_call(
+        kernel,
+        out_shape=shape(4, 160, SLOT),
+        compiler_params=params(),
+        cost_estimate=cost(0, 1 << 20),
+        name=name,
+    )(*got)
+
+
+def summed(got):
+    return pl.pallas_call(
+        sums_kernel,
+        out_shape=shape(3, 256, 128),
+        scratch_shapes=[pltpu.VMEM((256, 768), f32)],
+        compiler_params=params(),
+        cost_estimate=cost(2 * 16384 * 256 * 768, 1 << 20),
+        name="sums",
+    )(*got)
 
 
 def exchange_tiles(tiles):
@@ -465,39 +484,25 @@
     hbm = pl.BlockSpec(memory_space=pltpu.HBM)
     modes = pl.pallas_call(
         mix_kernel,
-        in_specs=[hbm] * 9,
-        out_specs=whole(BANDS, 88, 128),
-        out_shape=shape(BANDS, 88, 128),
+        in_specs=[hbm] * 3,
+        out_specs=whole(BANDS, 48, 128),
+        out_shape=shape(BANDS, 48, 128),
         scratch_shapes=[
             pltpu.VMEM((28, 16, 192), f32),
             pltpu.VMEM((28, 16, 192), f32),
             pltpu.VMEM((CH, CH), f32),
-            pltpu.VMEM((2, DEVICES, SLOT), jnp.int32),
-            pltpu.VMEM((3, DEVICES, SLOT), f32),
-            pltpu.VMEM((1, DEVICES), jnp.int32),
-            pltpu.VMEM((5, DEVICES, SLOT), f32),
-            pltpu.SemaphoreType.DMA((9,)),
+            pltpu.SemaphoreType.DMA((3,)),
         ],
         compiler_params=params(),
         cost_estimate=cost(6 * 448 * 192 * 192, 1 << 20),
         name="mix",
-    )(
-        *(
-            in_hbm(x)
-            for x in (
-                control,
-                scale,
-                vertical_root,
-                obs_column,
-                obs_level,
-                lidar_obs,
-                aod_obs,
-                obs_weight,
-                obs_count,
-            )
-        )
-    )
-    modes = exchange(modes, "band")
+    )(in_hbm(control), in_hbm(scale), in_hbm(vertical_root))
+    modes, obs_weight = lax.optimization_barrier((modes, obs_weight))
+    obs = packed(obs_count, obs_column, obs_level, lidar_obs, aod_obs, obs_weight)
+    obs = shifted(obs, "wave", lambda i, s: (i + s) % WAVES)
+    modes, obs = lax.optimization_barrier((exchange(modes, "band"), obs))
+    obs = regrouped(to_y_kernel, obs, "to_y")
+    obs = shifted(obs, "band", lambda i, s: (i + 4 * s) % BANDS)
 
     high, low = pl.pallas_call(
         wave_table_kernel,
@@ -511,9 +516,9 @@
     table_scratch = [pltpu.VMEM((28, NLAT, NT), f32), pltpu.SemaphoreType.DMA((GROUPS,))]
     spec = pl.pallas_call(
         legendre_kernel,
-        in_specs=[whole(BANDS, 88, 128), hbm],
-        out_specs=whole(WAVES, 248, 128),
-        out_shape=shape(WAVES, 248, 128),
+        in_specs=[whole(BANDS, 48, 128), hbm],
+        out_specs=whole(WAVES, 168, 128),
+        out_shape=shape(WAVES, 168, 128),
         scratch_shapes=[
             pltpu.VMEM((GROUPS, 48, NT), f32),
             pltpu.VMEM((GROUPS, 48, NLAT), f32),
@@ -523,19 +528,10 @@
         cost_estimate=legendre_cost,
         name="legendre",
     )(modes, in_hbm(legendre))
-    spec = exchange(spec, "wave")
-    sums = pl.pallas_call(
-        sums_kernel,
-        grid=(WAVES,),
-        in_specs=[pl.BlockSpec((1, 248, 128), lambda i: (i, 0, 0))],
-        out_specs=whole(3, 256, 128),
-        out_shape=shape(3, 256, 128),
-        scratch_shapes=[pltpu.VMEM((256, 768), f32)],
-        compiler_params=in_order,
-        cost_estimate=cost(2 * 16384 * 256 * 768, 1 << 20),
-        name="sums",
-    )(spec)
-
+    spec, obs = lax.optimization_barrier((exchange(spec, "wave"), obs))
+    obs = regrouped(to_z_kernel, obs, "to_z")
+    obs = shifted(obs, "band", lambda i, s: i // 4 * 4 + (i + s) % 4)
+    sums = summed(obs)
     tile_spec = pl.BlockSpec((2 * BANDS * TILE, 128), lambda i: (i, 0))
     tiles = shape(DEVICES * TILE, 128)
     wave_cost = cost(6 * 384 * 448 * 1024, 4 << 20)

time: 152 us -> 165 us (1.086)
  starting transfers between devices: 9.13 us -> 36.9 us
  blocking collectives: 75.2 us -> 56.5 us
  waiting for transfers between devices: 21.8 us -> 23.7 us
    ppermute x0 -> x13, waiting for transfers between devices: none -> 22.7 us  [shifted(): lax.ppermute(tiles[s], axis, [(i, places(i, s)) for i in range(count)])]
    all_to_all x2 -> x3, waiting for transfers between devices: 21.8 us -> 0.99 us  [exchange(): return lax.all_to_all(tiles, axis, split_axis=0, concat_axis=0, tiled=True)]
    all_to_all x4 -> x3, blocking collectives: 75.2 us -> 56.5 us  [exchange(): return lax.all_to_all(tiles, axis, split_axis=0, concat_axis=0, tiled=True)]
    ppermute x0 -> x13, starting transfers between devices: none -> 16.9 us  [shifted(): lax.ppermute(tiles[s], axis, [(i, places(i, s)) for i in range(count)])]
    all_to_all x2 -> x3, starting transfers between devices: 9.13 us -> 20 us  [exchange(): return lax.all_to_all(tiles, axis, split_axis=0, concat_axis=0, tiled=True)]
    pallas_call x3 -> x6, Pallas kernels: 21.2 us -> 22.8 us  [the longest x1 10.9 us: summed(): pl.pallas_call(sums_kernel, out_shape=shape(3, 256, 128), scratch_shapes=...]
  transfers between devices with their start and end apart: 2 -> 16, of which waited for: 2 -> 9; matrix products, arithmetic and copies ran while one was open for 0% -> 0% of each run, Pallas kernels for 10% -> 10%
where the time goes in v6:
time: 165 us; the launch traced here: 164 us
  blocking collectives  56.5 us (34%)
  Pallas kernels  45.2 us (27%)
  starting transfers between devices  36.9 us (22%)
  waiting for transfers between devices  23.7 us (14%)
    all_to_all x3, blocking collectives, exchange(): return lax.all_to_all(tiles, axis, split_axis=0, concat_axis=0, tiled=True)  56.5 us
    ppermute x13, waiting for transfers between devices, shifted(): lax.ppermute(tiles[s], axis, [(i, places(i, s)) for i in range(count)])  22.7 us
    all_to_all x3, starting transfers between devices, exchange(): return lax.all_to_all(tiles, axis, split_axis=0, concat_axis=0, tiled=True)  20 us
    ppermute x13, starting transfers between devices, shifted(): lax.ppermute(tiles[s], axis, [(i, places(i, s)) for i in range(count)])  16.9 us
    pallas_call x1, Pallas kernels, summed(): pl.pallas_call(sums_kernel, out_shape=shape(3, 256, 128), scratch_shapes=...  10.9 us
    pallas_call x1, Pallas kernels, body(): pl.pallas_call(legendre_kernel, in_specs=[whole(BANDS, 48, 128), hbm], ou...  8.88 us
    pallas_call x1, Pallas kernels, body(): pl.pallas_call(legendre_adjoint_kernel, in_specs=[whole(WAVES, 168, 128),...  6.51 us
    pallas_call x1, Pallas kernels, body(): pl.pallas_call(grid_kernel, grid=(4,), in_specs=[tile_spec, turned, pl.Bl...  4.23 us
  transfers between devices with their start and end apart: 16, of which 9 were waited for; matrix products, arithmetic and copies ran while one was open for 0% of the time, Pallas kernels for 10%

profile of v6, /device:TPU:0, one launch (start us, length us, event | category | flops | bytes accessed | tf_op | source)
XLA Modules:
  0.0 164.1 jit_solution(5315884429180134732)
XLA Ops:
  0.7 2.8 %mix.1 = f32[16,48,128]{2,1,0:T(8,128)} custom-call(f32[28,16,192]{2,1,0:T(8,128)} %bitcast.43, f32[28,16,192]{2,1,0:T(8,128)} %bitcast.45, f32[96,96]{1,0:T(8,128)} %root_ref.1), custom_call_target="tpu_custom_call" | custom-call | flops 99090432 | bytes 1048576 | tf_op jit(solution)/shard_map/mix/pallas_call | solution.py:485
  3.5 8.1 %all-to-all-start = ((f32[16,48,128]{2,1,0:T(8,128)}), f32[16,48,128]{2,1,0:T(8,128)S(1)}, u32[]{:S(2)}, u32[]{:S(2)}) async-start(f32[16,48,128]{2,1,0:T(8,128)} %mix.1), calls=%async_computation | async-start | bytes 786432 | tf_op jit(solution)/shard_map/all_to_all | solution.py:419
  11.9 1.9 %collective-permute-start.6 = (f32[80,128]{1,0:T(8,128)S(1)}, f32[80,128]{1,0:T(8,128)S(1)}, u32[]{:S(2)}, u32[]{:S(2)}) collective-permute-start(f32[80,128]{1,0:T(8,128)S(1)} %get-tuple-element.50), channel_id=1, source_target_pairs={{0,112},{16,0},{32,16},{48,32},{64,48},{80,64},{96,80},{112,96},{1... | collective-permute-start | bytes 122888 | tf_op jit(solution)/shard_map/ppermute | solution.py:426
  13.8 0.9 collective-permute-start.5
  15.3 2.7 %collective-permute-start.3 = (f32[80,128]{1,0:T(8,128)S(1)}, f32[80,128]{1,0:T(8,128)S(1)}, u32[]{:S(2)}, u32[]{:S(2)}) collective-permute-start(f32[80,128]{1,0:T(8,128)S(1)} %get-tuple-element.53), channel_id=1, source_target_pairs={{0,64},{16,80},{32,96},{48,112},{64,0},{80,16},{96,32},{112,48},{1... | collective-permute-start | bytes 122888 | tf_op jit(solution)/shard_map/ppermute | solution.py:426
  18.5 1.1 collective-permute-start
  19.6 1.3 collective-permute-done.3.refs_4_
  20.9 2.1 %collective-permute-done.2.refs_3_ = f32[80,128]{1,0:T(8,128)S(1)} collective-permute-done((f32[80,128]{1,0:T(8,128)S(1)}, f32[80,128]{1,0:T(8,128)S(1)}, u32[]{:S(2)}, u32[]{:S(2)}) %collective-permute-start.2) | collective-permute-done | bytes 40992 | tf_op jit(solution)/shard_map/ppermute | solution.py:426
  23.0 0.9 collective-permute-done.1.refs_2_
  24.3 8.9 %legendre.1 = f32[8,168,128]{2,1,0:T(8,128)} custom-call(f32[16,48,128]{2,1,0:T(8,128)S(1)} %all-to-all-done.modes_ref, f32[28,448,256]{2,1,0:T(8,128)} %table_hbm.3), custom_call_target="tpu_custom_call" | custom-call | flops 924844032 | bytes 14680064 | tf_op jit(solution)/shard_map/legendre/pallas_call | solution.py:517
  33.2 3.6 %all-to-all-start.1 = ((f32[8,168,128]{2,1,0:T(8,128)}), f32[8,168,128]{2,1,0:T(8,128)S(1)}, u32[]{:S(2)}, u32[]{:S(2)}) async-start(f32[8,168,128]{2,1,0:T(8,128)} %legendre.1), calls=%async_computation.1 | async-start | bytes 1376256 | tf_op jit(solution)/shard_map/all_to_all | solution.py:419
  36.9 3.2 %collective-permute-start.9 = (f32[160,128]{1,0:T(8,128)S(1)}, f32[160,128]{1,0:T(8,128)S(1)}, u32[]{:S(2)}, u32[]{:S(2)}) collective-permute-start(f32[160,128]{1,0:T(8,128)S(1)} %get-tuple-element.46), channel_id=1, source_target_pairs={{0,12},{1,13},{2,14},{3,15},{4,0},{5,1},{6,2},{7,3},{8,4},{9,5},{1... | collective-permute-start | bytes 245768 | tf_op jit(solution)/shard_map/ppermute | solution.py:426
  40.9 0.9 collective-permute-start.7
  41.8 3.5 %wave_table.1 = (bf16[448,1024]{1,0:T(8,128)(2,1)S(1)}, bf16[448,1024]{1,0:T(8,128)(2,1)S(1)}) custom-call(s32[1,224]{1,0:T(1,128)S(1)} %bitcast.51), custom_call_target="tpu_custom_call" | custom-call | flops 9175040 | bytes 2097152 | tf_op jit(solution)/shard_map/wave_table/pallas_call | solution.py:507
  45.3 1.6 collective-permute-done.8.refs_2_
  46.9 1.0 collective-permute-done.7.refs_1_
  47.8 1.0 all-to-all-done.1.spec_ref
  48.8 2.5 %synthesis.1 = f32[2688,128]{1,0:T(8,128)} custom-call(f32[8,168,128]{2,1,0:T(8,128)S(1)} %all-to-all-done.1.spec_ref, bf16[448,1024]{1,0:T(8,128)(2,1)S(1)} %get-tuple-element.34.high_ref, bf16[448,1024]{1,0:T(8,128)(2,1)S(1)} %get-tuple-element.35.low_ref), custom_call_target="tpu_custom_call" | custom-call | flops 1056964608 | bytes 4194304 | tf_op jit(solution)/shard_map/synthesis/pallas_call | solution.py:538
  51.4 8.3 %all-to-all-start.2 = ((f32[128,1,2688]{2,1,0:T(1,128)}), f32[128,1,2688]{2,1,0:T(1,128)S(1)}, u32[]{:S(2)}, u32[]{:S(2)}) async-start(f32[128,1,2688]{2,1,0:T(1,128)} %bitcast.15), calls=%async_computation.2 | async-start | bytes 2752512 | tf_op jit(solution)/shard_map/all_to_all | solution.py:419
  59.8 2.9 %collective-permute-start.12 = (f32[160,128]{1,0:T(8,128)S(1)}, f32[160,128]{1,0:T(8,128)S(1)}, u32[]{:S(2)}, u32[]{:S(2)}) collective-permute-start(f32[160,128]{1,0:T(8,128)S(1)} %get-tuple-element.42), channel_id=1, source_target_pairs={{0,3},{1,0},{2,1},{3,2},{4,7},{5,4},{6,5},{7,6},{8,11},{9,8},{10,9... | collective-permute-start | bytes 245768 | tf_op jit(solution)/shard_map/ppermute | solution.py:426
  63.0 1.1 collective-permute-start.10
  64.1 2.3 %flow.1.flow_ref = f32[384,8,128]{2,1,0:T(8,128)S(1)} custom-call(f32[28,96,128]{2,1,0:T(8,128)} %courant_ref.1), custom_call_target="tpu_custom_call" | custom-call | flops 2064384 | bytes 3145728 | tf_op jit(solution)/shard_map/flow/pallas_call | solution.py:551
  66.4 13.1 %collective-permute-done.12.refs_3_ = f32[160,128]{1,0:T(8,128)S(1)} collective-permute-done((f32[160,128]{1,0:T(8,128)S(1)}, f32[160,128]{1,0:T(8,128)S(1)}, u32[]{:S(2)}, u32[]{:S(2)}) %collective-permute-start.12) | collective-permute-done | bytes 81952 | tf_op jit(solution)/shard_map/ppermute | solution.py:426
  79.5 2.3 %collective-permute-done.10.refs_1_ = f32[160,128]{1,0:T(8,128)S(1)} collective-permute-done((f32[160,128]{1,0:T(8,128)S(1)}, f32[160,128]{1,0:T(8,128)S(1)}, u32[]{:S(2)}, u32[]{:S(2)}) %collective-permute-start.10) | collective-permute-done | bytes 81952 | tf_op jit(solution)/shard_map/ppermute | solution.py:426
  81.8 10.9 %sums.1.sums_ref = f32[3,256,128]{2,1,0:T(8,128)S(1)} custom-call(f32[160,128]{1,0:T(8,128)S(1)} %get-tuple-element.45.refs_0_, f32[160,128]{1,0:T(8,128)S(1)} %collective-permute-done.10.refs_1_, f32[160,128]{1,0:T(8,128)S(1)} %collective-permute-done.11.refs_2_, f32[160,128]{1,0:T(8,128)S(1)} %collective-permute-done.12.refs_3_), custom_call_target="tpu_custom_call" | custom-call | flops 6442450944 | bytes 1048576 | tf_op jit(solution)/shard_map/sums/pallas_call | solution.py:451
  93.4 4.2 %grid_steps.1 = (f32[28,96,128]{2,1,0:T(8,128)}, f32[2688,128]{1,0:T(8,128)S(1)}) custom-call(f32[2688,128]{1,0:T(8,128)S(1)} %bitcast.42, f32[384,8,128]{2,1,0:T(8,128)S(1)} %flow.1.flow_ref, f32[3,256,128]{2,1,0:T(8,128)} %copy-done.2, f32[12]{0:T(128)S(1)} %copy-done.9, f32[96]{0:T(128)S(1)} %copy-done.10), custom_call_target="tpu_custom_call" | custom-call | flops 13762560 | bytes 6291456 | tf_op jit(solution)/shard_map/grid_steps/pallas_call | solution.py:561
  97.7 29.5 %all_to_all.30 = f32[128,1,2688]{2,1,0:T(1,128)S(1)} all-to-all(f32[128,1,2688]{2,1,0:T(1,128)S(1)} %bitcast.48), channel_id=1, replica_groups=mesh['wave'=8,'band'=16] {'wave','band'}, dimensions={0} | all-to-all | bytes 2752512 | tf_op jit(solution)/shard_map/all_to_all | solution.py:419
  127.2 1.4 analysis.1
  128.6 14.6 %all_to_all.31.spec_ref = f32[8,168,128]{2,1,0:T(8,128)S(1)} all-to-all(f32[8,168,128]{2,1,0:T(8,128)S(1)} %bitcast.50), channel_id=1, replica_groups=mesh['wave'=8,'band'=16] {'wave'}, dimensions={0} | all-to-all | bytes 1376256 | tf_op jit(solution)/shard_map/all_to_all | solution.py:419
  143.2 6.5 %legendre_adjoint.1 = f32[16,48,128]{2,1,0:T(8,128)S(1)} custom-call(f32[8,168,128]{2,1,0:T(8,128)S(1)} %all_to_all.31.spec_ref, f32[28,448,256]{2,1,0:T(8,128)} %table_hbm.3), custom_call_target="tpu_custom_call" | custom-call | flops 924844032 | bytes 14680064 | tf_op jit(solution)/shard_map/legendre_adjoint/pallas_call | solution.py:589
  149.7 12.5 %all_to_all.32 = f32[16,48,128]{2,1,0:T(8,128)S(1)} all-to-all(f32[16,48,128]{2,1,0:T(8,128)S(1)} %legendre_adjoint.1), channel_id=1, replica_groups=mesh['wave'=8,'band'=16] {'band'}, dimensions={0} | all-to-all | bytes 786432 | tf_op jit(solution)/shard_map/all_to_all | solution.py:419
  162.2 2.0 %unmix.1 = f32[28,16,192]{2,1,0:T(8,128)} custom-call(f32[24,4,8,128]{3,2,1,0:T(8,128)S(1)} %bitcast.47, f32[28,16,192]{2,1,0:T(8,128)S(1)} %bitcast.44, f32[28,16,192]{2,1,0:T(8,128)S(1)} %bitcast.46, f32[96,96]{1,0:T(8,128)S(1)} %copy-done.3), custom_call_target="tpu_custom_call" | custom-call | flops 99090432 | bytes 1048576 | tf_op jit(solution)/shard_map/unmix/pallas_call | solution.py:601
  (53 shorter events, 3.7 us)
Async XLA Ops:
  0.6 11.1 %copy-start.8 = (f32[128,128]{1,0:T(8,128)S(1)}, f32[128,128]{1,0:T(8,128)}, u32[]{:S(2)}) copy-start(f32[128,128]{1,0:T(8,128)} %weight_ref) | copy-start | bytes 196612
  0.6 11.1 %copy-start.7 = (f32[128,128]{1,0:T(8,128)S(1)}, f32[128,128]{1,0:T(8,128)}, u32[]{:S(2)}) copy-start(f32[128,128]{1,0:T(8,128)} %aod_ref.2) | copy-start | bytes 196612
  0.7 11.1 %copy-start.6 = (f32[128,128]{1,0:T(8,128)S(1)}, f32[128,128]{1,0:T(8,128)}, u32[]{:S(2)}) copy-start(f32[128,128]{1,0:T(8,128)} %lidar_ref.2) | copy-start | bytes 196612
  0.7 11.1 %copy-start.5 = (s32[128,128]{1,0:T(8,128)S(1)}, s32[128,128]{1,0:T(8,128)}, u32[]{:S(2)}) copy-start(s32[128,128]{1,0:T(8,128)} %level_ref.1) | copy-start | bytes 196612
  0.7 11.1 %copy-start.4 = (s32[128,128]{1,0:T(8,128)S(1)}, s32[128,128]{1,0:T(8,128)}, u32[]{:S(2)}) copy-start(s32[128,128]{1,0:T(8,128)} %column_ref.1) | copy-start | bytes 196612
  0.7 11.1 %copy-start.11 = (s32[1,128]{1,0:T(1,128)S(1)}, s32[1,128]{1,0:T(1,128)}, u32[]{:S(2)}) copy-start(s32[1,128]{1,0:T(1,128)} %count_ref.1) | copy-start | bytes 1540
  3.5 20.8 %all-to-all-start = ((f32[16,48,128]{2,1,0:T(8,128)}), f32[16,48,128]{2,1,0:T(8,128)S(1)}, u32[]{:S(2)}, u32[]{:S(2)}) async-start(f32[16,48,128]{2,1,0:T(8,128)} %mix.1), calls=%async_computation | async-start | bytes 786432 | tf_op jit(solution)/shard_map/all_to_all | solution.py:419
  11.9 6.2 %collective-permute-start.6 = (f32[80,128]{1,0:T(8,128)S(1)}, f32[80,128]{1,0:T(8,128)S(1)}, u32[]{:S(2)}, u32[]{:S(2)}) collective-permute-start(f32[80,128]{1,0:T(8,128)S(1)} %get-tuple-element.50), channel_id=1, source_target_pairs={{0,112},{16,0},{32,16},{48,32},{64,48},{80,64},{96,80},{112,96},{1... | collective-permute-start | bytes 122888 | tf_op jit(solution)/shard_map/ppermute | solution.py:426
  13.8 4.7 %collective-permute-start.5 = (f32[80,128]{1,0:T(8,128)S(1)}, f32[80,128]{1,0:T(8,128)S(1)}, u32[]{:S(2)}, u32[]{:S(2)}) collective-permute-start(f32[80,128]{1,0:T(8,128)S(1)} %get-tuple-element.51), channel_id=1, source_target_pairs={{0,96},{16,112},{32,0},{48,16},{64,32},{80,48},{96,64},{112,80},{1... | collective-permute-start | bytes 122888 | tf_op jit(solution)/shard_map/ppermute | solution.py:426
  14.7 4.8 %collective-permute-start.4 = (f32[80,128]{1,0:T(8,128)S(1)}, f32[80,128]{1,0:T(8,128)S(1)}, u32[]{:S(2)}, u32[]{:S(2)}) collective-permute-start(f32[80,128]{1,0:T(8,128)S(1)} %get-tuple-element.52), channel_id=1, source_target_pairs={{0,80},{16,96},{32,112},{48,0},{64,16},{80,32},{96,48},{112,64},{1... | collective-permute-start | bytes 122888 | tf_op jit(solution)/shard_map/ppermute | solution.py:426
  15.3 5.6 %collective-permute-start.3 = (f32[80,128]{1,0:T(8,128)S(1)}, f32[80,128]{1,0:T(8,128)S(1)}, u32[]{:S(2)}, u32[]{:S(2)}) collective-permute-start(f32[80,128]{1,0:T(8,128)S(1)} %get-tuple-element.53), channel_id=1, source_target_pairs={{0,64},{16,80},{32,96},{48,112},{64,0},{80,16},{96,32},{112,48},{1... | collective-permute-start | bytes 122888 | tf_op jit(solution)/shard_map/ppermute | solution.py:426
  18.0 5.0 %collective-permute-start.2 = (f32[80,128]{1,0:T(8,128)S(1)}, f32[80,128]{1,0:T(8,128)S(1)}, u32[]{:S(2)}, u32[]{:S(2)}) collective-permute-start(f32[80,128]{1,0:T(8,128)S(1)} %get-tuple-element.54), channel_id=1, source_target_pairs={{0,48},{16,64},{32,80},{48,96},{64,112},{80,0},{96,16},{112,32},{1... | collective-permute-start | bytes 122888 | tf_op jit(solution)/shard_map/ppermute | solution.py:426
  18.1 5.8 %collective-permute-start.1 = (f32[80,128]{1,0:T(8,128)S(1)}, f32[80,128]{1,0:T(8,128)S(1)}, u32[]{:S(2)}, u32[]{:S(2)}) collective-permute-start(f32[80,128]{1,0:T(8,128)S(1)} %get-tuple-element.55), channel_id=1, source_target_pairs={{0,32},{16,48},{32,64},{48,80},{64,96},{80,112},{96,0},{112,16},{1... | collective-permute-start | bytes 122888 | tf_op jit(solution)/shard_map/ppermute | solution.py:426
  18.5 5.8 %collective-permute-start = (f32[80,128]{1,0:T(8,128)S(1)}, f32[80,128]{1,0:T(8,128)S(1)}, u32[]{:S(2)}, u32[]{:S(2)}) collective-permute-start(f32[80,128]{1,0:T(8,128)S(1)} %get-tuple-element.56), channel_id=1, source_target_pairs={{0,16},{16,32},{32,48},{48,64},{64,80},{80,96},{96,112},{112,0},{1... | collective-permute-start | bytes 122888 | tf_op jit(solution)/shard_map/ppermute | solution.py:426
  33.2 8.6 %copy-start.12 = (s32[224]{0:T(256)S(1)}, s32[224]{0:T(256)}, u32[]{:S(2)}) copy-start(s32[224]{0:T(256)} %param.18) | copy-start | bytes 2692
  33.2 15.6 %all-to-all-start.1 = ((f32[8,168,128]{2,1,0:T(8,128)}), f32[8,168,128]{2,1,0:T(8,128)S(1)}, u32[]{:S(2)}, u32[]{:S(2)}) async-start(f32[8,168,128]{2,1,0:T(8,128)} %legendre.1), calls=%async_computation.1 | async-start | bytes 1376256 | tf_op jit(solution)/shard_map/all_to_all | solution.py:419
  36.9 8.4 %collective-permute-start.9 = (f32[160,128]{1,0:T(8,128)S(1)}, f32[160,128]{1,0:T(8,128)S(1)}, u32[]{:S(2)}, u32[]{:S(2)}) collective-permute-start(f32[160,128]{1,0:T(8,128)S(1)} %get-tuple-element.46), channel_id=1, source_target_pairs={{0,12},{1,13},{2,14},{3,15},{4,0},{5,1},{6,2},{7,3},{8,4},{9,5},{1... | collective-permute-start | bytes 245768 | tf_op jit(solution)/shard_map/ppermute | solution.py:426
  40.1 6.8 %collective-permute-start.8 = (f32[160,128]{1,0:T(8,128)S(1)}, f32[160,128]{1,0:T(8,128)S(1)}, u32[]{:S(2)}, u32[]{:S(2)}) collective-permute-start(f32[160,128]{1,0:T(8,128)S(1)} %get-tuple-element.47), channel_id=1, source_target_pairs={{0,8},{1,9},{2,10},{3,11},{4,12},{5,13},{6,14},{7,15},{8,0},{9,1},... | collective-permute-start | bytes 245768 | tf_op jit(solution)/shard_map/ppermute | solution.py:426
  40.9 6.9 %collective-permute-start.7 = (f32[160,128]{1,0:T(8,128)S(1)}, f32[160,128]{1,0:T(8,128)S(1)}, u32[]{:S(2)}, u32[]{:S(2)}) collective-permute-start(f32[160,128]{1,0:T(8,128)S(1)} %get-tuple-element.48), channel_id=1, source_target_pairs={{0,4},{1,5},{2,6},{3,7},{4,8},{5,9},{6,10},{7,11},{8,12},{9,13},{1... | collective-permute-start | bytes 245768 | tf_op jit(solution)/shard_map/ppermute | solution.py:426
  45.3 6.1 %copy-start.13 = (bf16[448,1024]{1,0:T(8,128)(2,1)}, bf16[448,1024]{1,0:T(8,128)(2,1)S(1)}, u32[]{:S(2)}) copy-start(bf16[448,1024]{1,0:T(8,128)(2,1)S(1)} %get-tuple-element.34.high_ref) | copy-start | bytes 2752516
  45.3 6.1 %copy-start.15 = (bf16[448,1024]{1,0:T(8,128)(2,1)}, bf16[448,1024]{1,0:T(8,128)(2,1)S(1)}, u32[]{:S(2)}) copy-start(bf16[448,1024]{1,0:T(8,128)(2,1)S(1)} %get-tuple-element.35.low_ref) | copy-start | bytes 2752516
  51.4 42.1 %all-to-all-start.2 = ((f32[128,1,2688]{2,1,0:T(1,128)}), f32[128,1,2688]{2,1,0:T(1,128)S(1)}, u32[]{:S(2)}, u32[]{:S(2)}) async-start(f32[128,1,2688]{2,1,0:T(1,128)} %bitcast.15), calls=%async_computation.2 | async-start | bytes 2752512 | tf_op jit(solution)/shard_map/all_to_all | solution.py:419
  59.8 19.7 %collective-permute-start.12 = (f32[160,128]{1,0:T(8,128)S(1)}, f32[160,128]{1,0:T(8,128)S(1)}, u32[]{:S(2)}, u32[]{:S(2)}) collective-permute-start(f32[160,128]{1,0:T(8,128)S(1)} %get-tuple-element.42), channel_id=1, source_target_pairs={{0,3},{1,0},{2,1},{3,2},{4,7},{5,4},{6,5},{7,6},{8,11},{9,8},{10,9... | collective-permute-start | bytes 245768 | tf_op jit(solution)/shard_map/ppermute | solution.py:426
  62.7 16.8 %collective-permute-start.11 = (f32[160,128]{1,0:T(8,128)S(1)}, f32[160,128]{1,0:T(8,128)S(1)}, u32[]{:S(2)}, u32[]{:S(2)}) collective-permute-start(f32[160,128]{1,0:T(8,128)S(1)} %get-tuple-element.43), channel_id=1, source_target_pairs={{0,2},{1,3},{2,0},{3,1},{4,6},{5,7},{6,4},{7,5},{8,10},{9,11},{10,... | collective-permute-start | bytes 245768 | tf_op jit(solution)/shard_map/ppermute | solution.py:426
  63.0 18.8 %collective-permute-start.10 = (f32[160,128]{1,0:T(8,128)S(1)}, f32[160,128]{1,0:T(8,128)S(1)}, u32[]{:S(2)}, u32[]{:S(2)}) collective-permute-start(f32[160,128]{1,0:T(8,128)S(1)} %get-tuple-element.44), channel_id=1, source_target_pairs={{0,1},{1,2},{2,3},{3,0},{4,5},{5,6},{6,7},{7,4},{8,9},{9,10},{10,1... | collective-permute-start | bytes 245768 | tf_op jit(solution)/shard_map/ppermute | solution.py:426
  81.8 11.6 %copy-start.9 = (f32[12]{0:T(128)S(1)}, f32[12]{0:T(128)}, u32[]{:S(2)}) copy-start(f32[12]{0:T(128)} %lidar_ref.3) | copy-start | bytes 148
  81.8 11.6 %copy-start.10 = (f32[96]{0:T(128)S(1)}, f32[96]{0:T(128)}, u32[]{:S(2)}) copy-start(f32[96]{0:T(128)} %aod_ref.3) | copy-start | bytes 1156
  97.7 29.5 %copy-start.14 = (bf16[448,1024]{1,0:T(8,128)(2,1)S(1)}, bf16[448,1024]{1,0:T(8,128)(2,1)}, u32[]{:S(2)}) copy-start(bf16[448,1024]{1,0:T(8,128)(2,1)} %copy-done.13) | copy-start | bytes 2752516
  97.7 29.5 %copy-start.16 = (bf16[448,1024]{1,0:T(8,128)(2,1)S(1)}, bf16[448,1024]{1,0:T(8,128)(2,1)}, u32[]{:S(2)}) copy-start(bf16[448,1024]{1,0:T(8,128)(2,1)} %copy-done.15) | copy-start | bytes 2752516
  143.2 19.0 %copy-start = (f32[16,28,192]{2,0,1:T(8,128)S(1)}, f32[16,28,192]{2,0,1:T(8,128)}, u32[]{:S(2)}) copy-start(f32[16,28,192]{2,0,1:T(8,128)} %param.14) | copy-start | bytes 1032196
  143.2 19.0 %copy-start.1 = (f32[16,28,192]{2,0,1:T(8,128)S(1)}, f32[16,28,192]{2,0,1:T(8,128)}, u32[]{:S(2)}) copy-start(f32[16,28,192]{2,0,1:T(8,128)} %param.15) | copy-start | bytes 1032196
  143.2 19.0 %copy-start.3 = (f32[96,96]{1,0:T(8,128)S(1)}, f32[96,96]{1,0:T(8,128)}, u32[]{:S(2)}) copy-start(f32[96,96]{1,0:T(8,128)} %root_ref.1) | copy-start | bytes 110596
  (1 other events, 0.7 us)

commit v7 on v5

--- a/solution.py
+++ b/solution.py
@@ -86,6 +86,7 @@
     aod_hbm,
     weight_hbm,
     count_hbm,
+    out_hbm,
     out_ref,
     control_ref,
     scale_ref,
@@ -128,6 +129,10 @@
         for k in range(5):
             rows = obs_ref[k, pl.ds(band, WAVES, stride=BANDS), :]
             out_ref[band, 48 + 8 * k : 56 + 8 * k] = rows
+    done = []
+    for k, at in enumerate((pl.ds(48, 40), pl.ds(0, 48))):
+        done.append(pltpu.make_async_copy(out_ref.at[:, at], out_hbm.at[:, at], sem.at[9 + k]))
+    done[0].start()
 
     for copy in copies[:3]:
         copy.wait()
@@ -145,6 +150,9 @@
         for h in range(24):
             c = 4 * h + j
             out_ref[c // 6, 8 * (c % 6) : 8 * (c % 6) + 8] = z[h]
+    done[1].start()
+    for copy in done:
+        copy.wait()
 
 
 def table_copies(table_hbm, table_ref, sem):
@@ -466,9 +474,10 @@
     modes = pl.pallas_call(
         mix_kernel,
         in_specs=[hbm] * 9,
-        out_specs=whole(BANDS, 88, 128),
+        out_specs=pl.BlockSpec(memory_space=pl.ANY),
         out_shape=shape(BANDS, 88, 128),
         scratch_shapes=[
+            pltpu.VMEM((BANDS, 88, 128), f32),
             pltpu.VMEM((28, 16, 192), f32),
             pltpu.VMEM((28, 16, 192), f32),
             pltpu.VMEM((CH, CH), f32),
@@ -476,7 +485,7 @@
             pltpu.VMEM((3, DEVICES, SLOT), f32),
             pltpu.VMEM((1, DEVICES), jnp.int32),
             pltpu.VMEM((5, DEVICES, SLOT), f32),
-            pltpu.SemaphoreType.DMA((9,)),
+            pltpu.SemaphoreType.DMA((11,)),
         ],
         compiler_params=params(),
         cost_estimate=cost(6 * 448 * 192 * 192, 1 << 20),
@@ -497,15 +506,15 @@
             )
         )
     )
-    modes = exchange(modes, "band")
-
-    high, low = pl.pallas_call(
+    waves = pl.pallas_call(
         wave_table_kernel,
         out_shape=(shape(2 * MW, NLON, kind=bf16), shape(2 * MW, NLON, kind=bf16)),
         compiler_params=params(),
         cost_estimate=cost(20 * 448 * 1024, 2 << 20),
         name="wave_table",
     )(zonal_number.reshape(1, MW))
+    modes, (high, low) = lax.optimization_barrier((exchange(modes, "band"), waves))
+
     legendre_cost = cost(6 * 28 * 448 * 256 * 48, 14 << 20)
     in_order = params(dimension_semantics=("arbitrary",))
     table_scratch = [pltpu.VMEM((28, NLAT, NT), f32), pltpu.SemaphoreType.DMA((GROUPS,))]

time: 152 us -> 152 us (level)
  starting transfers between devices: 9.13 us -> 12.8 us
  waiting for transfers between devices: 21.8 us -> 19.8 us
  blocking collectives: 75.2 us -> 73.6 us
    all_to_all x2, starting transfers between devices: 9.13 us -> 12.8 us  [exchange(): return lax.all_to_all(tiles, axis, split_axis=0, concat_axis=0, tiled=True)]
    all_to_all x2, waiting for transfers between devices: 21.8 us -> 19.8 us  [exchange(): return lax.all_to_all(tiles, axis, split_axis=0, concat_axis=0, tiled=True)]
    all_to_all x4, blocking collectives: 75.2 us -> 73.6 us  [exchange(): return lax.all_to_all(tiles, axis, split_axis=0, concat_axis=0, tiled=True)]
where the time goes in v7:
time: 152 us; the launch traced here: 151 us
  blocking collectives  73.6 us (48%)
  Pallas kernels  43.4 us (29%)
  waiting for transfers between devices  19.8 us (13%)
  starting transfers between devices  12.8 us (8%)
    all_to_all x4, blocking collectives, exchange(): return lax.all_to_all(tiles, axis, split_axis=0, concat_axis=0, tiled=True)  73.6 us
    all_to_all x2, waiting for transfers between devices, exchange(): return lax.all_to_all(tiles, axis, split_axis=0, concat_axis=0, tiled=True)  19.8 us
    all_to_all x2, starting transfers between devices, exchange(): return lax.all_to_all(tiles, axis, split_axis=0, concat_axis=0, tiled=True)  12.8 us
    pallas_call x1, Pallas kernels, body(): pl.pallas_call(sums_kernel, grid=(WAVES,), in_specs=[pl.BlockSpec((1, 248...  9.53 us
    pallas_call x1, Pallas kernels, body(): pl.pallas_call(legendre_kernel, in_specs=[whole(BANDS, 88, 128), hbm], ou...  8.06 us
    pallas_call x1, Pallas kernels, body(): pl.pallas_call(legendre_adjoint_kernel, in_specs=[whole(WAVES, 168, 128),...  6.51 us
    pallas_call x1, Pallas kernels, body(): pl.pallas_call(grid_kernel, grid=(4,), in_specs=[tile_spec, turned, pl.Bl...  4.22 us
    pallas_call x1, Pallas kernels, body(): pl.pallas_call(wave_table_kernel, out_shape=(shape(2 * MW, NLON, kind=bf1...  3.48 us
  transfers between devices with their start and end apart: 2, of which 2 were waited for; matrix products, arithmetic and copies ran while one was open for 0% of the time, Pallas kernels for 10%

profile of v7, /device:TPU:0, one launch (start us, length us, event | category | flops | bytes accessed | tf_op | source)
XLA Modules:
  0.0 151.2 jit_solution(1345925290585238090)
XLA Ops:
  0.6 0.0 copy-start.12
  0.6 3.4 %mix.1 = f32[16,88,128]{2,1,0:T(8,128)} custom-call(f32[28,16,192]{2,1,0:T(8,128)} %bitcast.11, f32[28,16,192]{2,1,0:T(8,128)} %bitcast.13, f32[96,96]{1,0:T(8,128)} %root_ref.1, s32[128,128]{1,0:T(8,128)} %column_hbm.1, s32[128,128]{1,0:T(8,128)} %level_hbm.1, f32[128,128]{1,0:T(8,128)} %lidar_hbm.1, f32[128,128]{1,0:T(8,128)} %aod_hbm.1, ...), custom_call_target="tpu_custom_call" | custom-call | flops 99090432 | bytes 1048576 | tf_op jit(solution)/shard_map/mix/pallas_call | solution.py:474
  4.0 8.1 %all-to-all-start = ((f32[16,88,128]{2,1,0:T(8,128)}), f32[16,88,128]{2,1,0:T(8,128)S(1)}, u32[]{:S(2)}, u32[]{:S(2)}) async-start(f32[16,88,128]{2,1,0:T(8,128)} %mix.1), calls=%async_computation | async-start | bytes 1441792 | tf_op jit(solution)/shard_map/all_to_all | solution.py:447
  12.2 0.0 copy-done.12
  12.2 3.5 %wave_table.1 = (bf16[448,1024]{1,0:T(8,128)(2,1)S(1)}, bf16[448,1024]{1,0:T(8,128)(2,1)S(1)}) custom-call(s32[1,224]{1,0:T(1,128)S(1)} %bitcast.19), custom_call_target="tpu_custom_call" | custom-call | flops 9175040 | bytes 2097152 | tf_op jit(solution)/shard_map/wave_table/pallas_call | solution.py:509
  15.7 0.0 copy-start.4
  15.7 0.0 copy-start.6
  15.7 10.1 %all-to-all-done.modes_ref = f32[16,88,128]{2,1,0:T(8,128)S(1)} async-done(((f32[16,88,128]{2,1,0:T(8,128)}), f32[16,88,128]{2,1,0:T(8,128)S(1)}, u32[]{:S(2)}, u32[]{:S(2)}) %all-to-all-start) | async-done | bytes 720928 | tf_op jit(solution)/shard_map/all_to_all | solution.py:447
  25.8 8.1 %legendre.1 = f32[8,248,128]{2,1,0:T(8,128)S(1)} custom-call(f32[16,88,128]{2,1,0:T(8,128)S(1)} %all-to-all-done.modes_ref, f32[28,448,256]{2,1,0:T(8,128)} %table_hbm.3), custom_call_target="tpu_custom_call" | custom-call | flops 924844032 | bytes 14680064 | tf_op jit(solution)/shard_map/legendre/pallas_call | solution.py:521
  33.8 19.8 %all_to_all.30.spec_ref.obs_ref = f32[8,248,128]{2,1,0:T(8,128)S(1)} all-to-all(f32[8,248,128]{2,1,0:T(8,128)S(1)} %legendre.1), channel_id=1, replica_groups=mesh['wave'=8,'band'=16] {'wave'}, dimensions={0} | all-to-all | bytes 2031616 | tf_op jit(solution)/shard_map/all_to_all | solution.py:447
  53.7 0.0 copy-done.4
  53.7 0.0 copy-done.6
  53.7 2.5 %synthesis.1 = f32[2688,128]{1,0:T(8,128)} custom-call(f32[8,248,128]{2,1,0:T(8,128)S(1)} %all_to_all.30.spec_ref.obs_ref, bf16[448,1024]{1,0:T(8,128)(2,1)S(1)} %get-tuple-element.12.high_ref, bf16[448,1024]{1,0:T(8,128)(2,1)S(1)} %get-tuple-element.13.low_ref), custom_call_target="tpu_custom_call" | custom-call | flops 1056964608 | bytes 4194304 | tf_op jit(solution)/shard_map/synthesis/pallas_call | solution.py:551
  56.2 4.6 %all-to-all-start.2 = ((f32[128,1,2688]{2,1,0:T(1,128)}), f32[128,1,2688]{2,1,0:T(1,128)S(1)}, u32[]{:S(2)}, u32[]{:S(2)}) async-start(f32[128,1,2688]{2,1,0:T(1,128)} %bitcast.3), calls=%async_computation.2 | async-start | bytes 2752512 | tf_op jit(solution)/shard_map/all_to_all | solution.py:447
  60.9 0.0 copy-start.1
  60.9 2.4 %flow.1.flow_ref = f32[384,8,128]{2,1,0:T(8,128)S(1)} custom-call(f32[28,96,128]{2,1,0:T(8,128)} %courant_ref.1), custom_call_target="tpu_custom_call" | custom-call | flops 2064384 | bytes 3145728 | tf_op jit(solution)/shard_map/flow/pallas_call | solution.py:564
  63.3 0.0 copy-start.10
  63.3 0.0 copy-start.11
  63.3 9.5 %sums.1.sums_ref = f32[3,256,128]{2,1,0:T(8,128)S(1)} custom-call(f32[8,248,128]{2,1,0:T(8,128)S(1)} %copy-done.1), custom_call_target="tpu_custom_call" | custom-call | flops 6442450944 | bytes 1048576 | tf_op jit(solution)/shard_map/sums/pallas_call | solution.py:536
  72.8 0.0 copy-start.8
  72.8 0.7 copy-done.8
  73.6 9.7 %all-to-all-done.2 = f32[128,1,2688]{2,1,0:T(1,128)S(1)} async-done(((f32[128,1,2688]{2,1,0:T(1,128)}), f32[128,1,2688]{2,1,0:T(1,128)S(1)}, u32[]{:S(2)}, u32[]{:S(2)}) %all-to-all-start.2) | async-done | bytes 1376288 | tf_op jit(solution)/shard_map/all_to_all | solution.py:447
  83.3 0.0 copy-done.11
  83.3 4.2 %grid_steps.1 = (f32[28,96,128]{2,1,0:T(8,128)}, f32[2688,128]{1,0:T(8,128)S(1)}) custom-call(f32[2688,128]{1,0:T(8,128)S(1)} %bitcast.10, f32[384,8,128]{2,1,0:T(8,128)S(1)} %flow.1.flow_ref, f32[3,256,128]{2,1,0:T(8,128)} %copy-done.8, f32[12]{0:T(128)S(1)} %copy-done.10, f32[96]{0:T(128)S(1)} %copy-done.11), custom_call_target="tpu_custom_call" | custom-call | flops 13762560 | bytes 6291456 | tf_op jit(solution)/shard_map/grid_steps/pallas_call | solution.py:574
  87.5 26.6 %all_to_all.31 = f32[128,1,2688]{2,1,0:T(1,128)S(1)} all-to-all(f32[128,1,2688]{2,1,0:T(1,128)S(1)} %bitcast.16), channel_id=1, replica_groups=mesh['wave'=8,'band'=16] {'wave','band'}, dimensions={0} | all-to-all | bytes 2752512 | tf_op jit(solution)/shard_map/all_to_all | solution.py:447
  114.1 0.0 copy-done.7
  114.1 1.4 analysis.1
  115.5 14.8 %all_to_all.32.spec_ref = f32[8,168,128]{2,1,0:T(8,128)S(1)} all-to-all(f32[8,168,128]{2,1,0:T(8,128)S(1)} %bitcast.18), channel_id=1, replica_groups=mesh['wave'=8,'band'=16] {'wave'}, dimensions={0} | all-to-all | bytes 1376256 | tf_op jit(solution)/shard_map/all_to_all | solution.py:447
  130.3 6.5 %legendre_adjoint.1 = f32[16,48,128]{2,1,0:T(8,128)S(1)} custom-call(f32[8,168,128]{2,1,0:T(8,128)S(1)} %all_to_all.32.spec_ref, f32[28,448,256]{2,1,0:T(8,128)} %table_hbm.3), custom_call_target="tpu_custom_call" | custom-call | flops 924844032 | bytes 14680064 | tf_op jit(solution)/shard_map/legendre_adjoint/pallas_call | solution.py:602
  136.8 12.5 %all_to_all.33 = f32[16,48,128]{2,1,0:T(8,128)S(1)} all-to-all(f32[16,48,128]{2,1,0:T(8,128)S(1)} %legendre_adjoint.1), channel_id=1, replica_groups=mesh['wave'=8,'band'=16] {'band'}, dimensions={0} | all-to-all | bytes 786432 | tf_op jit(solution)/shard_map/all_to_all | solution.py:447
  149.3 0.0 copy-done.3
  149.3 2.0 %unmix.1 = f32[28,16,192]{2,1,0:T(8,128)} custom-call(f32[24,4,8,128]{3,2,1,0:T(8,128)S(1)} %bitcast.15, f32[28,16,192]{2,1,0:T(8,128)S(1)} %bitcast.12, f32[28,16,192]{2,1,0:T(8,128)S(1)} %bitcast.14, f32[96,96]{1,0:T(8,128)S(1)} %copy-done.9), custom_call_target="tpu_custom_call" | custom-call | flops 99090432 | bytes 1048576 | tf_op jit(solution)/shard_map/unmix/pallas_call | solution.py:614
  (12 shorter events, 0.0 us)
Async XLA Ops:
  0.6 11.5 %copy-start.12 = (s32[224]{0:T(256)S(1)}, s32[224]{0:T(256)}, u32[]{:S(2)}) copy-start(s32[224]{0:T(256)} %param.18) | copy-start | bytes 2692
  4.0 21.7 %all-to-all-start = ((f32[16,88,128]{2,1,0:T(8,128)}), f32[16,88,128]{2,1,0:T(8,128)S(1)}, u32[]{:S(2)}, u32[]{:S(2)}) async-start(f32[16,88,128]{2,1,0:T(8,128)} %mix.1), calls=%async_computation | async-start | bytes 1441792 | tf_op jit(solution)/shard_map/all_to_all | solution.py:447
  15.7 38.0 %copy-start.4 = (bf16[448,1024]{1,0:T(8,128)(2,1)}, bf16[448,1024]{1,0:T(8,128)(2,1)S(1)}, u32[]{:S(2)}) copy-start(bf16[448,1024]{1,0:T(8,128)(2,1)S(1)} %get-tuple-element.12.high_ref) | copy-start | bytes 2752516
  15.7 38.0 %copy-start.6 = (bf16[448,1024]{1,0:T(8,128)(2,1)}, bf16[448,1024]{1,0:T(8,128)(2,1)S(1)}, u32[]{:S(2)}) copy-start(bf16[448,1024]{1,0:T(8,128)(2,1)S(1)} %get-tuple-element.13.low_ref) | copy-start | bytes 2752516
  53.7 2.5 %copy-start = (f32[8,248,128]{2,1,0:T(8,128)}, f32[8,248,128]{2,1,0:T(8,128)S(1)}, u32[]{:S(2)}) copy-start(f32[8,248,128]{2,1,0:T(8,128)S(1)} %all_to_all.30.spec_ref.obs_ref) | copy-start | bytes 3047428
  56.2 27.1 %all-to-all-start.2 = ((f32[128,1,2688]{2,1,0:T(1,128)}), f32[128,1,2688]{2,1,0:T(1,128)S(1)}, u32[]{:S(2)}, u32[]{:S(2)}) async-start(f32[128,1,2688]{2,1,0:T(1,128)} %bitcast.3), calls=%async_computation.2 | async-start | bytes 2752512 | tf_op jit(solution)/shard_map/all_to_all | solution.py:447
  60.9 2.4 %copy-start.1 = (f32[8,248,128]{2,1,0:T(8,128)S(1)}, f32[8,248,128]{2,1,0:T(8,128)}, u32[]{:S(2)}) copy-start(f32[8,248,128]{2,1,0:T(8,128)} %copy-done) | copy-start | bytes 3047428
  63.3 20.1 %copy-start.10 = (f32[12]{0:T(128)S(1)}, f32[12]{0:T(128)}, u32[]{:S(2)}) copy-start(f32[12]{0:T(128)} %lidar_ref.1) | copy-start | bytes 148
  63.3 20.0 %copy-start.11 = (f32[96]{0:T(128)S(1)}, f32[96]{0:T(128)}, u32[]{:S(2)}) copy-start(f32[96]{0:T(128)} %aod_ref.1) | copy-start | bytes 1156
  72.8 0.7 copy-start.8
  87.5 26.6 %copy-start.5 = (bf16[448,1024]{1,0:T(8,128)(2,1)S(1)}, bf16[448,1024]{1,0:T(8,128)(2,1)}, u32[]{:S(2)}) copy-start(bf16[448,1024]{1,0:T(8,128)(2,1)} %copy-done.4) | copy-start | bytes 2752516
  87.5 26.6 %copy-start.7 = (bf16[448,1024]{1,0:T(8,128)(2,1)S(1)}, bf16[448,1024]{1,0:T(8,128)(2,1)}, u32[]{:S(2)}) copy-start(bf16[448,1024]{1,0:T(8,128)(2,1)} %copy-done.6) | copy-start | bytes 2752516
  130.3 19.0 %copy-start.2 = (f32[16,28,192]{2,0,1:T(8,128)S(1)}, f32[16,28,192]{2,0,1:T(8,128)}, u32[]{:S(2)}) copy-start(f32[16,28,192]{2,0,1:T(8,128)} %param.14) | copy-start | bytes 1032196
  130.3 19.0 %copy-start.3 = (f32[16,28,192]{2,0,1:T(8,128)S(1)}, f32[16,28,192]{2,0,1:T(8,128)}, u32[]{:S(2)}) copy-start(f32[16,28,192]{2,0,1:T(8,128)} %param.15) | copy-start | bytes 1032196
  130.3 19.0 %copy-start.9 = (f32[96,96]{1,0:T(8,128)S(1)}, f32[96,96]{1,0:T(8,128)}, u32[]{:S(2)}) copy-start(f32[96,96]{1,0:T(8,128)} %root_ref.1) | copy-start | bytes 110596

commit v8 on v7

--- a/solution.py
+++ b/solution.py
@@ -68,12 +68,14 @@
 
 
 def doubled_root(root):
-    rows = (iota((2 * CH, CH), 0) // 2 == iota((2 * CH, CH), 1)).astype(f32)
-    cols = (iota((CH, 2 * CH), 1) // 2 == iota((CH, 2 * CH), 0)).astype(f32)
-    wide = jnp.dot(rows, root, precision=highest, preferred_element_type=f32)
-    wide = jnp.dot(wide, cols, precision=highest, preferred_element_type=f32)
+    rows = (iota((2 * CH, CH), 0) // 2 == iota((2 * CH, CH), 1)).astype(f32).astype(bf16)
+    cols = (iota((CH, 2 * CH), 1) // 2 == iota((CH, 2 * CH), 0)).astype(f32).astype(bf16)
     same = iota((2 * CH, 2 * CH), 0) % 2 == iota((2 * CH, 2 * CH), 1) % 2
-    return jnp.where(same, wide, 0.0)
+    parts = []
+    for part in split(root):
+        wide = mm(mm(rows, part).astype(bf16), cols)
+        parts.append(jnp.where(same, wide, 0.0).astype(bf16))
+    return parts
 
 
 def mix_kernel(
@@ -136,8 +138,7 @@
 
     for copy in copies[:3]:
         copy.wait()
-    root = doubled_root(root_ref[...])
-    rh, rl = split(root)
+    rh, rl = doubled_root(root_ref[...])
     tiles = []
     for m4 in range(4):
         x = jnp.concatenate([control_ref[4 * g + m4] for g in range(GROUPS)], axis=0)
@@ -245,12 +246,13 @@
         low_ref[pl.ds(first, rows), half:] = vl
 
 
-def synthesis_kernel(spec_ref, high_ref, low_ref, out_ref, lhs_ref):
+def synthesis_kernel(spec_ref, high_ref, low_ref, out_hbm, out_ref, lhs_ref, sem):
     rows = spec_ref[:, :168].reshape(WAVES, GROUPS, 3, 8, 128)
     for c in range(3):
         high, low = split(rows[:, :, c].reshape(2 * MW, 128).T)
         lhs_ref[128 * c : 128 * c + 128] = high
         lhs_ref[384 + 128 * c : 512 + 128 * c] = low
+    done = []
     for i in range(4):
         lon = pl.ds(256 * i, 256)
         both = mm(lhs_ref[...], high_ref[:, lon])
@@ -261,6 +263,11 @@
                     row = 128 * c + 8 * band
                     at = TILE * (BANDS * (2 * i + w) + band) + 7 * c
                     out_ref[at : at + 7] = out[row : row + 7, 128 * w : 128 * w + 128]
+        at = pl.ds(2 * BANDS * TILE * i, 2 * BANDS * TILE)
+        done.append(pltpu.make_async_copy(out_ref.at[at], out_hbm.at[at], sem.at[i]))
+        done[i].start()
+    for copy in done:
+        copy.wait()
 
 
 def analysis_kernel(grid_ref, high_ref, low_ref, out_ref):
@@ -317,8 +324,7 @@
 
 
 def unmix_kernel(modes_ref, control_ref, scale_ref, root_ref, out_ref):
-    root = doubled_root(root_ref[...])
-    rh, rl = split(root)
+    rh, rl = doubled_root(root_ref[...])
     tiles = turn([modes_ref[:, j] for j in range(4)], 1, 2)
     for m4 in range(4):
         y = tiles[m4].reshape(2 * CH, 128).T[: 16 * GROUPS]
@@ -378,53 +384,86 @@
 
 
 def grid_kernel(
-    grid_ref, flow_ref, sums_ref, lidar_ref, aod_ref, state_ref, adjoint_ref, hold_ref
+    grid_ref,
+    flow_ref,
+    sums_hbm,
+    lidar_ref,
+    aod_ref,
+    state_hbm,
+    adjoint_ref,
+    hold_ref,
+    state_ref,
+    sums_ref,
+    sem,
 ):
+    fetch = pltpu.make_async_copy(sums_hbm, sums_ref, sem.at[4])
+    fetch.start()
+
     def tile_rows(l, b2, hc, c):
         return pl.ds(TILE * (BANDS * hc + 2 * l + b2) + 7 * c, 7)
 
+    def store(q):
+        target = state_hbm.at[pl.ds(7 * q, 7)]
+        return pltpu.make_async_copy(state_ref.at[q], target, sem.at[q])
+
     blank = jnp.zeros((1, 128), f32)
     chains = [(b2, hc, c) for b2 in range(2) for hc in range(2) for c in range(3)]
-    lidar_sum = [None] * LEV
-    aod_sum = None
-    for b2, hc, c in chains:
-        bin_at = b2 * 6 + hc * 3 + c
-        x = [
-            jnp.concatenate([grid_ref[tile_rows(l, b2, hc, c)], blank], axis=0)
-            for l in range(LEV)
-        ]
-        flow = [flow_ref[BINS * l + bin_at] for l in range(LEV)]
-        for step in range(STEPS):
-            out = [flow[l] * x[l] for l in range(LEV)]
-            x = [x[l] - out[l] if l == 0 else x[l] - out[l] + out[l - 1] for l in range(LEV)]
-        coef = lidar_ref[bin_at]
+
+    @pl.loop(0, 4)
+    def _(q):
+        lidar_sum = [None] * LEV
+        aod_sum = None
+        for b2, hc, c in chains:
+            bin_at = b2 * 6 + hc * 3 + c
+            x = [
+                jnp.concatenate([grid_ref[q, tile_rows(l, b2, hc, c)], blank], axis=0)
+                for l in range(LEV)
+            ]
+            flow = [flow_ref[q, BINS * l + bin_at] for l in range(LEV)]
+            for step in range(STEPS):
+                out = [flow[l] * x[l] for l in range(LEV)]
+                x = [x[l] - out[l] if l == 0 else x[l] - out[l] + out[l - 1] for l in range(LEV)]
+            coef = lidar_ref[bin_at]
+            for l in range(LEV):
+                hold_ref[BINS * l + bin_at] = x[l]
+                term = x[l] * coef
+                lidar_sum[l] = term if lidar_sum[l] is None else lidar_sum[l] + term
+                term = x[l] * aod_ref[BINS * l + bin_at]
+                aod_sum = term if aod_sum is None else aod_sum + term
+
+        for h in range(12):
+            rows = turn([hold_ref[8 * h + j] for j in range(8)], 0, 1)
+            for t in range(7):
+                state_ref[q, t, 8 * h : 8 * h + 8] = rows[t]
+        store(q).start()
+
+        @pl.when(q == 0)
+        def _():
+            fetch.wait()
+
+        def sums(k, l):
+            return sums_ref[k, pl.ds(pl.multiple_of(64 * q + 8 * l, 8), 8), :]
+
+        weight = [sums(0, l) for l in range(LEV)]
+        lidar = [weight[l] * lidar_sum[l] - sums(1, l) for l in range(LEV)]
+        aod = sum(weight[1:], weight[0]) * aod_sum
         for l in range(LEV):
-            hold_ref[BINS * l + bin_at] = x[l]
-            lidar_sum[l] = x[l] * coef if lidar_sum[l] is None else lidar_sum[l] + x[l] * coef
-            term = x[l] * aod_ref[BINS * l + bin_at]
-            aod_sum = term if aod_sum is None else aod_sum + term
-
-    for h in range(12):
-        rows = turn([hold_ref[8 * h + j] for j in range(8)], 0, 1)
-        for t in range(7):
-            state_ref[t, 8 * h : 8 * h + 8] = rows[t]
-
-    weight = [sums_ref[0, 8 * l : 8 * l + 8] for l in range(LEV)]
-    lidar = [weight[l] * lidar_sum[l] - sums_ref[1, 8 * l : 8 * l + 8] for l in range(LEV)]
-    aod = sum(weight[1:], weight[0]) * aod_sum
-    for l in range(LEV):
-        aod = aod - sums_ref[2, 8 * l : 8 * l + 8]
-    for b2, hc, c in chains:
-        bin_at = b2 * 6 + hc * 3 + c
-        coef = lidar_ref[bin_at]
-        flow = [flow_ref[BINS * l + bin_at] for l in range(LEV)]
-        a = [lidar[l] * coef + aod * aod_ref[BINS * l + bin_at] for l in range(LEV)]
-        for step in range(STEPS):
-            a = [
-                a[l] + flow[l] * ((a[l + 1] - a[l]) if l + 1 < LEV else -a[l]) for l in range(LEV)
-            ]
-        for l in range(LEV):
-            adjoint_ref[tile_rows(l, b2, hc, c)] = a[l][:7]
+            aod = aod - sums(2, l)
+        for b2, hc, c in chains:
+            bin_at = b2 * 6 + hc * 3 + c
+            coef = lidar_ref[bin_at]
+            flow = [flow_ref[q, BINS * l + bin_at] for l in range(LEV)]
+            a = [lidar[l] * coef + aod * aod_ref[BINS * l + bin_at] for l in range(LEV)]
+            for step in range(STEPS):
+                a = [
+                    a[l] + flow[l] * ((a[l + 1] - a[l]) if l + 1 < LEV else -a[l])
+                    for l in range(LEV)
+                ]
+            for l in range(LEV):
+                adjoint_ref[q, tile_rows(l, b2, hc, c)] = a[l][:7]
+
+    for q in range(4):
+        store(q).wait()
 
 
 def shape(*lengths, kind=f32):
@@ -545,13 +584,17 @@
         name="sums",
     )(spec)
 
-    tile_spec = pl.BlockSpec((2 * BANDS * TILE, 128), lambda i: (i, 0))
     tiles = shape(DEVICES * TILE, 128)
     wave_cost = cost(6 * 384 * 448 * 1024, 4 << 20)
     grid = pl.pallas_call(
         synthesis_kernel,
+        out_specs=pl.BlockSpec(memory_space=pl.ANY),
         out_shape=tiles,
-        scratch_shapes=[pltpu.VMEM((768, 2 * MW), bf16)],
+        scratch_shapes=[
+            pltpu.VMEM((DEVICES * TILE, 128), f32),
+            pltpu.VMEM((768, 2 * MW), bf16),
+            pltpu.SemaphoreType.DMA((4,)),
+        ],
         compiler_params=params(),
         cost_estimate=wave_cost,
         name="synthesis",
@@ -571,23 +614,29 @@
         cost_estimate=cost(6 * 28 * 96 * 128, 3 << 20),
         name="flow",
     )(in_hbm(courant))
+    quarters = (4, 2 * BANDS * TILE, 128)
     state, adjoint = pl.pallas_call(
         grid_kernel,
-        grid=(4,),
-        in_specs=[
-            tile_spec,
-            turned,
-            pl.BlockSpec((3, 64, 128), lambda q: (0, q, 0)),
-            scalars,
-            scalars,
+        in_specs=[whole(*quarters), whole(4, CH, 8, 128), hbm, scalars, scalars],
+        out_specs=(pl.BlockSpec(memory_space=pl.ANY), whole(*quarters)),
+        out_shape=(shape(28, CH, 128), shape(*quarters)),
+        scratch_shapes=[
+            pltpu.VMEM((CH, 8, 128), f32),
+            pltpu.VMEM((4, 7, CH, 128), f32),
+            pltpu.VMEM((3, 256, 128), f32),
+            pltpu.SemaphoreType.DMA((5,)),
         ],
-        out_specs=(field, tile_spec),
-        out_shape=(shape(28, CH, 128), tiles),
-        scratch_shapes=[pltpu.VMEM((CH, 8, 128), f32)],
-        compiler_params=in_order,
+        compiler_params=params(),
         cost_estimate=cost(40 * 28 * 96 * 128, 6 << 20),
         name="grid_steps",
-    )(grid, flow, in_hbm(sums), lidar_coef, aod_coef)
+    )(
+        grid.reshape(quarters),
+        flow.reshape(4, CH, 8, 128),
+        in_hbm(sums),
+        lidar_coef,
+        aod_coef,
+    )
+    adjoint = adjoint.reshape(DEVICES * TILE, 128)
     adjoint = exchange_tiles(adjoint)
 
     spec = pl.pallas_call(

time: 152 us -> 150 us (0.987)
  no operation moved by 1% of the time
where the time goes in v8:
time: 150 us
  blocking collectives  73.5 us (49%)
  Pallas kernels  42.2 us (28%)
  waiting for transfers between devices  19.8 us (13%)
  starting transfers between devices  12.8 us (9%)
    all_to_all x4, blocking collectives, exchange(): return lax.all_to_all(tiles, axis, split_axis=0, concat_axis=0, tiled=True)  73.5 us
    all_to_all x2, waiting for transfers between devices, exchange(): return lax.all_to_all(tiles, axis, split_axis=0, concat_axis=0, tiled=True)  19.8 us
    all_to_all x2, starting transfers between devices, exchange(): return lax.all_to_all(tiles, axis, split_axis=0, concat_axis=0, tiled=True)  12.8 us
    pallas_call x1, Pallas kernels, body(): pl.pallas_call(sums_kernel, grid=(WAVES,), in_specs=[pl.BlockSpec((1, 248...  9.53 us
    pallas_call x1, Pallas kernels, body(): pl.pallas_call(legendre_kernel, in_specs=[whole(BANDS, 88, 128), hbm], ou...  8.06 us
    pallas_call x1, Pallas kernels, body(): pl.pallas_call(legendre_adjoint_kernel, in_specs=[whole(WAVES, 168, 128),...  6.51 us
    pallas_call x1, Pallas kernels, body(): pl.pallas_call(grid_kernel, in_specs=[whole(*quarters), whole(4, CH, 8, 1...  3.95 us
    pallas_call x1, Pallas kernels, body(): pl.pallas_call(wave_table_kernel, out_shape=(shape(2 * MW, NLON, kind=bf1...  3.48 us
  transfers between devices with their start and end apart: 2, of which 2 were waited for; matrix products, arithmetic and copies ran while one was open for 0% of the time, Pallas kernels for 10%

profile of v8, /device:TPU:0, one launch (start us, length us, event | category | flops | bytes accessed | tf_op | source)
XLA Modules:
  0.0 149.9 jit_solution(4410873752690347310)
XLA Ops:
  0.6 0.0 copy-start.12
  0.6 3.0 %mix.1 = f32[16,88,128]{2,1,0:T(8,128)} custom-call(f32[28,16,192]{2,1,0:T(8,128)} %bitcast.13, f32[28,16,192]{2,1,0:T(8,128)} %bitcast.15, f32[96,96]{1,0:T(8,128)} %root_ref.1, s32[128,128]{1,0:T(8,128)} %column_hbm.1, s32[128,128]{1,0:T(8,128)} %level_hbm.1, f32[128,128]{1,0:T(8,128)} %lidar_hbm.1, f32[128,128]{1,0:T(8,128)} %aod_hbm.1, ...), custom_call_target="tpu_custom_call" | custom-call | flops 99090432 | bytes 1048576 | tf_op jit(solution)/shard_map/mix/pallas_call | solution.py:513
  3.6 8.1 %all-to-all-start = ((f32[16,88,128]{2,1,0:T(8,128)}), f32[16,88,128]{2,1,0:T(8,128)S(1)}, u32[]{:S(2)}, u32[]{:S(2)}) async-start(f32[16,88,128]{2,1,0:T(8,128)} %mix.1), calls=%async_computation | async-start | bytes 1441792 | tf_op jit(solution)/shard_map/all_to_all | solution.py:486
  11.8 0.0 copy-done.12
  11.8 3.5 %wave_table.1 = (bf16[448,1024]{1,0:T(8,128)(2,1)S(1)}, bf16[448,1024]{1,0:T(8,128)(2,1)S(1)}) custom-call(s32[1,224]{1,0:T(1,128)S(1)} %bitcast.21), custom_call_target="tpu_custom_call" | custom-call | flops 9175040 | bytes 2097152 | tf_op jit(solution)/shard_map/wave_table/pallas_call | solution.py:548
  15.3 0.0 copy-start.4
  15.3 0.0 copy-start.6
  15.3 10.1 %all-to-all-done.modes_ref = f32[16,88,128]{2,1,0:T(8,128)S(1)} async-done(((f32[16,88,128]{2,1,0:T(8,128)}), f32[16,88,128]{2,1,0:T(8,128)S(1)}, u32[]{:S(2)}, u32[]{:S(2)}) %all-to-all-start) | async-done | bytes 720928 | tf_op jit(solution)/shard_map/all_to_all | solution.py:486
  25.4 8.1 %legendre.1 = f32[8,248,128]{2,1,0:T(8,128)S(1)} custom-call(f32[16,88,128]{2,1,0:T(8,128)S(1)} %all-to-all-done.modes_ref, f32[28,448,256]{2,1,0:T(8,128)} %table_hbm.3), custom_call_target="tpu_custom_call" | custom-call | flops 924844032 | bytes 14680064 | tf_op jit(solution)/shard_map/legendre/pallas_call | solution.py:560
  33.4 19.9 %all_to_all.30.spec_ref.obs_ref = f32[8,248,128]{2,1,0:T(8,128)S(1)} all-to-all(f32[8,248,128]{2,1,0:T(8,128)S(1)} %legendre.1), channel_id=1, replica_groups=mesh['wave'=8,'band'=16] {'wave'}, dimensions={0} | all-to-all | bytes 2031616 | tf_op jit(solution)/shard_map/all_to_all | solution.py:486
  53.3 0.0 copy-done.4
  53.3 0.0 copy-done.6
  53.3 2.3 %synthesis.1 = f32[2688,128]{1,0:T(8,128)} custom-call(f32[8,248,128]{2,1,0:T(8,128)S(1)} %all_to_all.30.spec_ref.obs_ref, bf16[448,1024]{1,0:T(8,128)(2,1)S(1)} %get-tuple-element.12.high_ref, bf16[448,1024]{1,0:T(8,128)(2,1)S(1)} %get-tuple-element.13.low_ref), custom_call_target="tpu_custom_call" | custom-call | flops 1056964608 | bytes 4194304 | tf_op jit(solution)/shard_map/synthesis/pallas_call | solution.py:589
  55.6 0.0 copy-done
  55.6 4.7 %all-to-all-start.2 = ((f32[128,1,2688]{2,1,0:T(1,128)}), f32[128,1,2688]{2,1,0:T(1,128)S(1)}, u32[]{:S(2)}, u32[]{:S(2)}) async-start(f32[128,1,2688]{2,1,0:T(1,128)} %bitcast.3), calls=%async_computation.2 | async-start | bytes 2752512 | tf_op jit(solution)/shard_map/all_to_all | solution.py:486
  60.3 0.0 copy-start.1
  60.3 2.4 %flow.1 = f32[384,8,128]{2,1,0:T(8,128)S(1)} custom-call(f32[28,96,128]{2,1,0:T(8,128)} %courant_ref.1), custom_call_target="tpu_custom_call" | custom-call | flops 2064384 | bytes 3145728 | tf_op jit(solution)/shard_map/flow/pallas_call | solution.py:607
  62.7 0.0 copy-start.10
  62.7 0.0 copy-start.11
  62.7 9.5 %sums.1.sums_hbm = f32[3,256,128]{2,1,0:T(8,128)S(1)} custom-call(f32[8,248,128]{2,1,0:T(8,128)S(1)} %copy-done.1), custom_call_target="tpu_custom_call" | custom-call | flops 6442450944 | bytes 1048576 | tf_op jit(solution)/shard_map/sums/pallas_call | solution.py:575
  72.3 0.0 copy-start.8
  72.3 0.7 copy-done.8
  73.0 9.7 %all-to-all-done.2 = f32[128,1,2688]{2,1,0:T(1,128)S(1)} async-done(((f32[128,1,2688]{2,1,0:T(1,128)}), f32[128,1,2688]{2,1,0:T(1,128)S(1)}, u32[]{:S(2)}, u32[]{:S(2)}) %all-to-all-start.2) | async-done | bytes 1376288 | tf_op jit(solution)/shard_map/all_to_all | solution.py:486
  82.8 0.0 copy-done.11
  82.8 3.9 %grid_steps.1 = (f32[28,96,128]{2,1,0:T(8,128)}, f32[4,672,128]{2,1,0:T(8,128)S(1)}) custom-call(f32[4,672,128]{2,1,0:T(8,128)S(1)} %bitcast.12, f32[4,96,8,128]{3,2,1,0:T(8,128)S(1)} %bitcast.11, f32[3,256,128]{2,1,0:T(8,128)} %copy-done.8, f32[12]{0:T(128)S(1)} %copy-done.10, f32[96]{0:T(128)S(1)} %copy-done.11), custom_call_target="tpu_custom_call" | custom-call | flops 13762560 | bytes 6291456 | tf_op jit(solution)/shard_map/grid_steps/pallas_call | solution.py:618
  86.7 26.6 %all_to_all.31 = f32[128,1,2688]{2,1,0:T(1,128)S(1)} all-to-all(f32[128,1,2688]{2,1,0:T(1,128)S(1)} %bitcast.18), channel_id=1, replica_groups=mesh['wave'=8,'band'=16] {'wave','band'}, dimensions={0} | all-to-all | bytes 2752512 | tf_op jit(solution)/shard_map/all_to_all | solution.py:486
  113.3 0.0 copy-done.7
  113.3 1.4 analysis.1
  114.7 14.6 %all_to_all.32.spec_ref = f32[8,168,128]{2,1,0:T(8,128)S(1)} all-to-all(f32[8,168,128]{2,1,0:T(8,128)S(1)} %bitcast.20), channel_id=1, replica_groups=mesh['wave'=8,'band'=16] {'wave'}, dimensions={0} | all-to-all | bytes 1376256 | tf_op jit(solution)/shard_map/all_to_all | solution.py:486
  129.3 6.5 %legendre_adjoint.1 = f32[16,48,128]{2,1,0:T(8,128)S(1)} custom-call(f32[8,168,128]{2,1,0:T(8,128)S(1)} %all_to_all.32.spec_ref, f32[28,448,256]{2,1,0:T(8,128)} %table_hbm.3), custom_call_target="tpu_custom_call" | custom-call | flops 924844032 | bytes 14680064 | tf_op jit(solution)/shard_map/legendre_adjoint/pallas_call | solution.py:651
  135.8 12.5 %all_to_all.33 = f32[16,48,128]{2,1,0:T(8,128)S(1)} all-to-all(f32[16,48,128]{2,1,0:T(8,128)S(1)} %legendre_adjoint.1), channel_id=1, replica_groups=mesh['wave'=8,'band'=16] {'band'}, dimensions={0} | all-to-all | bytes 786432 | tf_op jit(solution)/shard_map/all_to_all | solution.py:486
  148.3 1.6 %unmix.1 = f32[28,16,192]{2,1,0:T(8,128)} custom-call(f32[24,4,8,128]{3,2,1,0:T(8,128)S(1)} %bitcast.17, f32[28,16,192]{2,1,0:T(8,128)S(1)} %bitcast.14, f32[28,16,192]{2,1,0:T(8,128)S(1)} %bitcast.16, f32[96,96]{1,0:T(8,128)S(1)} %copy-done.9), custom_call_target="tpu_custom_call" | custom-call | flops 99090432 | bytes 1048576 | tf_op jit(solution)/shard_map/unmix/pallas_call | solution.py:663
  (12 shorter events, 0.0 us)
Async XLA Ops:
  0.6 11.1 %copy-start.12 = (s32[224]{0:T(256)S(1)}, s32[224]{0:T(256)}, u32[]{:S(2)}) copy-start(s32[224]{0:T(256)} %param.18) | copy-start | bytes 2692
  3.6 21.7 %all-to-all-start = ((f32[16,88,128]{2,1,0:T(8,128)}), f32[16,88,128]{2,1,0:T(8,128)S(1)}, u32[]{:S(2)}, u32[]{:S(2)}) async-start(f32[16,88,128]{2,1,0:T(8,128)} %mix.1), calls=%async_computation | async-start | bytes 1441792 | tf_op jit(solution)/shard_map/all_to_all | solution.py:486
  15.3 38.0 %copy-start.4 = (bf16[448,1024]{1,0:T(8,128)(2,1)}, bf16[448,1024]{1,0:T(8,128)(2,1)S(1)}, u32[]{:S(2)}) copy-start(bf16[448,1024]{1,0:T(8,128)(2,1)S(1)} %get-tuple-element.12.high_ref) | copy-start | bytes 2752516
  15.3 38.0 %copy-start.6 = (bf16[448,1024]{1,0:T(8,128)(2,1)}, bf16[448,1024]{1,0:T(8,128)(2,1)S(1)}, u32[]{:S(2)}) copy-start(bf16[448,1024]{1,0:T(8,128)(2,1)S(1)} %get-tuple-element.13.low_ref) | copy-start | bytes 2752516
  53.3 2.3 %copy-start = (f32[8,248,128]{2,1,0:T(8,128)}, f32[8,248,128]{2,1,0:T(8,128)S(1)}, u32[]{:S(2)}) copy-start(f32[8,248,128]{2,1,0:T(8,128)S(1)} %all_to_all.30.spec_ref.obs_ref) | copy-start | bytes 3047428
  55.6 27.1 %all-to-all-start.2 = ((f32[128,1,2688]{2,1,0:T(1,128)}), f32[128,1,2688]{2,1,0:T(1,128)S(1)}, u32[]{:S(2)}, u32[]{:S(2)}) async-start(f32[128,1,2688]{2,1,0:T(1,128)} %bitcast.3), calls=%async_computation.2 | async-start | bytes 2752512 | tf_op jit(solution)/shard_map/all_to_all | solution.py:486
  60.3 2.4 %copy-start.1 = (f32[8,248,128]{2,1,0:T(8,128)S(1)}, f32[8,248,128]{2,1,0:T(8,128)}, u32[]{:S(2)}) copy-start(f32[8,248,128]{2,1,0:T(8,128)} %copy-done) | copy-start | bytes 3047428
  62.7 20.1 %copy-start.10 = (f32[12]{0:T(128)S(1)}, f32[12]{0:T(128)}, u32[]{:S(2)}) copy-start(f32[12]{0:T(128)} %lidar_ref.1) | copy-start | bytes 148
  62.7 20.0 %copy-start.11 = (f32[96]{0:T(128)S(1)}, f32[96]{0:T(128)}, u32[]{:S(2)}) copy-start(f32[96]{0:T(128)} %aod_ref.1) | copy-start | bytes 1156
  72.3 0.7 copy-start.8
  86.7 26.6 %copy-start.5 = (bf16[448,1024]{1,0:T(8,128)(2,1)S(1)}, bf16[448,1024]{1,0:T(8,128)(2,1)}, u32[]{:S(2)}) copy-start(bf16[448,1024]{1,0:T(8,128)(2,1)} %copy-done.4) | copy-start | bytes 2752516
  86.7 26.6 %copy-start.7 = (bf16[448,1024]{1,0:T(8,128)(2,1)S(1)}, bf16[448,1024]{1,0:T(8,128)(2,1)}, u32[]{:S(2)}) copy-start(bf16[448,1024]{1,0:T(8,128)(2,1)} %copy-done.6) | copy-start | bytes 2752516
  129.3 19.0 %copy-start.2 = (f32[16,28,192]{2,0,1:T(8,128)S(1)}, f32[16,28,192]{2,0,1:T(8,128)}, u32[]{:S(2)}) copy-start(f32[16,28,192]{2,0,1:T(8,128)} %param.14) | copy-start | bytes 1032196
  129.3 19.0 %copy-start.3 = (f32[16,28,192]{2,0,1:T(8,128)S(1)}, f32[16,28,192]{2,0,1:T(8,128)}, u32[]{:S(2)}) copy-start(f32[16,28,192]{2,0,1:T(8,128)} %param.15) | copy-start | bytes 1032196
  129.3 19.0 %copy-start.9 = (f32[96,96]{1,0:T(8,128)S(1)}, f32[96,96]{1,0:T(8,128)}, u32[]{:S(2)}) copy-start(f32[96,96]{1,0:T(8,128)} %root_ref.1) | copy-start | bytes 110596

commit v9 on v8

--- a/solution.py
+++ b/solution.py
@@ -132,9 +132,14 @@
             rows = obs_ref[k, pl.ds(band, WAVES, stride=BANDS), :]
             out_ref[band, 48 + 8 * k : 56 + 8 * k] = rows
     done = []
-    for k, at in enumerate((pl.ds(48, 40), pl.ds(0, 48))):
-        done.append(pltpu.make_async_copy(out_ref.at[:, at], out_hbm.at[:, at], sem.at[9 + k]))
-    done[0].start()
+
+    def send(first, count, row, rows):
+        at = (pl.ds(first, count), pl.ds(row, rows))
+        sent = pltpu.make_async_copy(out_ref.at[at], out_hbm.at[at], sem.at[9 + len(done)])
+        sent.start()
+        done.append(sent)
+
+    send(0, BANDS, 48, 40)
 
     for copy in copies[:3]:
         copy.wait()
@@ -147,27 +152,31 @@
         y = (mm(xh, rh) + mm(xl, rh) + mm(xh, rl)) * s
         y = jnp.concatenate([y, jnp.zeros((16, 2 * CH), f32)], axis=0)
         tiles.append(y.T.reshape(24, 8, 128))
-    for j, z in enumerate(turn(tiles, 1, 2)):
-        for h in range(24):
-            c = 4 * h + j
-            out_ref[c // 6, 8 * (c % 6) : 8 * (c % 6) + 8] = z[h]
-    done[1].start()
+    for part in range(2):
+        for j, z in enumerate(turn([t[12 * part : 12 * part + 12] for t in tiles], 1, 2)):
+            for h in range(12):
+                c = 48 * part + 4 * h + j
+                out_ref[c // 6, 8 * (c % 6) : 8 * (c % 6) + 8] = z[h]
+        send(8 * part, 8, 0, 48)
     for copy in done:
         copy.wait()
 
 
-def table_copies(table_hbm, table_ref, sem):
-    copies = []
-    for g in range(GROUPS):
-        at = pl.ds(4 * g, 4)
-        copies.append(pltpu.make_async_copy(table_hbm.at[at], table_ref.at[at], sem.at[g]))
-    for copy in copies:
-        copy.start()
+def table_copies(table_hbm, table_ref, sem, counts):
+    copies = {}
+    first = 0
+    for count in counts:
+        at = pl.ds(4 * first, 4 * count)
+        copies[first] = pltpu.make_async_copy(
+            table_hbm.at[at], table_ref.at[at], sem.at[len(copies)]
+        )
+        copies[first].start()
+        first += count
     return copies
 
 
 def legendre_kernel(modes_ref, table_hbm, out_ref, x_ref, acc_ref, table_ref, sem):
-    copies = table_copies(table_hbm, table_ref, sem)
+    copies = table_copies(table_hbm, table_ref, sem, (1,) * GROUPS)
     for half in range(2):
         for c in range(6):
             got = [modes_ref[8 * half + s, 8 * c : 8 * c + 8] for s in range(8)]
@@ -295,7 +304,7 @@
 
 
 def legendre_adjoint_kernel(spec_ref, table_hbm, out_ref, acc_ref, table_ref, sem):
-    copies = table_copies(table_hbm, table_ref, sem)
+    copies = table_copies(table_hbm, table_ref, sem, (1, 2, 2, 1, 1))
     order = lat_order()
     for hc in range(2):
         s = jnp.concatenate([spec_ref[2 * q + hc] for q in range(4)], axis=1)
@@ -304,16 +313,19 @@
     slot = (iota((48, NLAT), 0) % 8) // 2
     x = []
     for g in range(GROUPS):
-        copies[g].wait()
+        if g in copies:
+            copies[g].wait()
         rows = [acc_ref[168 * hc + 24 * g : 168 * hc + 24 * g + 24] for hc in range(2)]
         mine = jnp.concatenate(rows, axis=0)
         acc = None
         for m4 in range(4):
             xh, xl = split(jnp.where(slot == m4, mine, 0.0))
-            th, tl = split(table_ref[4 * g + m4])
-            both = mm(jnp.concatenate([xh, xl], axis=0), th)
-            part = both[:48] + both[48:] + mm(xh, tl)
-            acc = part if acc is None else acc + part
+            left = jnp.concatenate([xh, xl], axis=0)
+            for first, last in ((0, 256), (256, NLAT)):
+                th, tl = split(table_ref[4 * g + m4, first:last])
+                both = mm(left[:, first:last], th)
+                part = both[:48] + both[48:] + mm(xh[:, first:last], tl)
+                acc = part if acc is None else acc + part
         x.append(acc)
     x.append(jnp.zeros((48, NT), f32))
     for half in range(2):
@@ -524,7 +536,7 @@
             pltpu.VMEM((3, DEVICES, SLOT), f32),
             pltpu.VMEM((1, DEVICES), jnp.int32),
             pltpu.VMEM((5, DEVICES, SLOT), f32),
-            pltpu.SemaphoreType.DMA((11,)),
+            pltpu.SemaphoreType.DMA((12,)),
         ],
         compiler_params=params(),
         cost_estimate=cost(6 * 448 * 192 * 192, 1 << 20),

time: 150 us -> 150 us (level)
  no operation moved by 1% of the time
where the time goes in v9:
time: 150 us
  blocking collectives  73.5 us (49%)
  Pallas kernels  42.1 us (28%)
  waiting for transfers between devices  19.8 us (13%)
  starting transfers between devices  12.8 us (9%)
    all_to_all x4, blocking collectives, exchange(): return lax.all_to_all(tiles, axis, split_axis=0, concat_axis=0, tiled=True)  73.5 us
    all_to_all x2, waiting for transfers between devices, exchange(): return lax.all_to_all(tiles, axis, split_axis=0, concat_axis=0, tiled=True)  19.8 us
    all_to_all x2, starting transfers between devices, exchange(): return lax.all_to_all(tiles, axis, split_axis=0, concat_axis=0, tiled=True)  12.8 us
    pallas_call x1, Pallas kernels, body(): pl.pallas_call(sums_kernel, grid=(WAVES,), in_specs=[pl.BlockSpec((1, 248...  9.52 us
    pallas_call x1, Pallas kernels, body(): pl.pallas_call(legendre_kernel, in_specs=[whole(BANDS, 88, 128), hbm], ou...  8.07 us
    pallas_call x1, Pallas kernels, body(): pl.pallas_call(legendre_adjoint_kernel, in_specs=[whole(WAVES, 168, 128),...  6.45 us
    pallas_call x1, Pallas kernels, body(): pl.pallas_call(grid_kernel, in_specs=[whole(*quarters), whole(4, CH, 8, 1...  3.95 us
    pallas_call x1, Pallas kernels, body(): pl.pallas_call(wave_table_kernel, out_shape=(shape(2 * MW, NLON, kind=bf1...  3.48 us
  transfers between devices with their start and end apart: 2, of which 2 were waited for; matrix products, arithmetic and copies ran while one was open for 0% of the time, Pallas kernels for 10%

profile of v9, /device:TPU:0, one launch (start us, length us, event | category | flops | bytes accessed | tf_op | source)
XLA Modules:
  0.0 149.8 jit_solution(17311526644371414191)
XLA Ops:
  0.6 0.0 copy-start.12
  0.6 3.0 %mix.1 = f32[16,88,128]{2,1,0:T(8,128)} custom-call(f32[28,16,192]{2,1,0:T(8,128)} %bitcast.13, f32[28,16,192]{2,1,0:T(8,128)} %bitcast.15, f32[96,96]{1,0:T(8,128)} %root_ref.1, s32[128,128]{1,0:T(8,128)} %column_hbm.1, s32[128,128]{1,0:T(8,128)} %level_hbm.1, f32[128,128]{1,0:T(8,128)} %lidar_hbm.1, f32[128,128]{1,0:T(8,128)} %aod_hbm.1, ...), custom_call_target="tpu_custom_call" | custom-call | flops 99090432 | bytes 1048576 | tf_op jit(solution)/shard_map/mix/pallas_call | solution.py:525
  3.6 8.1 %all-to-all-start = ((f32[16,88,128]{2,1,0:T(8,128)}), f32[16,88,128]{2,1,0:T(8,128)S(1)}, u32[]{:S(2)}, u32[]{:S(2)}) async-start(f32[16,88,128]{2,1,0:T(8,128)} %mix.1), calls=%async_computation | async-start | bytes 1441792 | tf_op jit(solution)/shard_map/all_to_all | solution.py:498
  11.8 0.0 copy-done.12
  11.8 3.5 %wave_table.1 = (bf16[448,1024]{1,0:T(8,128)(2,1)S(1)}, bf16[448,1024]{1,0:T(8,128)(2,1)S(1)}) custom-call(s32[1,224]{1,0:T(1,128)S(1)} %bitcast.21), custom_call_target="tpu_custom_call" | custom-call | flops 9175040 | bytes 2097152 | tf_op jit(solution)/shard_map/wave_table/pallas_call | solution.py:560
  15.2 0.0 copy-start.4
  15.3 0.0 copy-start.6
  15.3 10.1 %all-to-all-done.modes_ref = f32[16,88,128]{2,1,0:T(8,128)S(1)} async-done(((f32[16,88,128]{2,1,0:T(8,128)}), f32[16,88,128]{2,1,0:T(8,128)S(1)}, u32[]{:S(2)}, u32[]{:S(2)}) %all-to-all-start) | async-done | bytes 720928 | tf_op jit(solution)/shard_map/all_to_all | solution.py:498
  25.3 8.1 %legendre.1 = f32[8,248,128]{2,1,0:T(8,128)S(1)} custom-call(f32[16,88,128]{2,1,0:T(8,128)S(1)} %all-to-all-done.modes_ref, f32[28,448,256]{2,1,0:T(8,128)} %table_hbm.3), custom_call_target="tpu_custom_call" | custom-call | flops 924844032 | bytes 14680064 | tf_op jit(solution)/shard_map/legendre/pallas_call | solution.py:572
  33.4 19.8 %all_to_all.30.spec_ref.obs_ref = f32[8,248,128]{2,1,0:T(8,128)S(1)} all-to-all(f32[8,248,128]{2,1,0:T(8,128)S(1)} %legendre.1), channel_id=1, replica_groups=mesh['wave'=8,'band'=16] {'wave'}, dimensions={0} | all-to-all | bytes 2031616 | tf_op jit(solution)/shard_map/all_to_all | solution.py:498
  53.3 0.0 copy-done.4
  53.3 0.0 copy-done.6
  53.3 2.3 %synthesis.1 = f32[2688,128]{1,0:T(8,128)} custom-call(f32[8,248,128]{2,1,0:T(8,128)S(1)} %all_to_all.30.spec_ref.obs_ref, bf16[448,1024]{1,0:T(8,128)(2,1)S(1)} %get-tuple-element.12.high_ref, bf16[448,1024]{1,0:T(8,128)(2,1)S(1)} %get-tuple-element.13.low_ref), custom_call_target="tpu_custom_call" | custom-call | flops 1056964608 | bytes 4194304 | tf_op jit(solution)/shard_map/synthesis/pallas_call | solution.py:601
  55.6 0.0 copy-done
  55.6 4.7 %all-to-all-start.2 = ((f32[128,1,2688]{2,1,0:T(1,128)}), f32[128,1,2688]{2,1,0:T(1,128)S(1)}, u32[]{:S(2)}, u32[]{:S(2)}) async-start(f32[128,1,2688]{2,1,0:T(1,128)} %bitcast.3), calls=%async_computation.2 | async-start | bytes 2752512 | tf_op jit(solution)/shard_map/all_to_all | solution.py:498
  60.3 0.0 copy-start.1
  60.3 2.4 %flow.1 = f32[384,8,128]{2,1,0:T(8,128)S(1)} custom-call(f32[28,96,128]{2,1,0:T(8,128)} %courant_ref.1), custom_call_target="tpu_custom_call" | custom-call | flops 2064384 | bytes 3145728 | tf_op jit(solution)/shard_map/flow/pallas_call | solution.py:619
  62.7 0.0 copy-done.1
  62.7 0.0 copy-start.10
  62.7 0.0 copy-start.11
  62.7 9.5 %sums.1.sums_hbm = f32[3,256,128]{2,1,0:T(8,128)S(1)} custom-call(f32[8,248,128]{2,1,0:T(8,128)S(1)} %copy-done.1), custom_call_target="tpu_custom_call" | custom-call | flops 6442450944 | bytes 1048576 | tf_op jit(solution)/shard_map/sums/pallas_call | solution.py:587
  72.2 0.0 copy-start.8
  72.3 0.7 copy-done.8
  73.0 9.7 %all-to-all-done.2 = f32[128,1,2688]{2,1,0:T(1,128)S(1)} async-done(((f32[128,1,2688]{2,1,0:T(1,128)}), f32[128,1,2688]{2,1,0:T(1,128)S(1)}, u32[]{:S(2)}, u32[]{:S(2)}) %all-to-all-start.2) | async-done | bytes 1376288 | tf_op jit(solution)/shard_map/all_to_all | solution.py:498
  82.7 3.9 %grid_steps.1 = (f32[28,96,128]{2,1,0:T(8,128)}, f32[4,672,128]{2,1,0:T(8,128)S(1)}) custom-call(f32[4,672,128]{2,1,0:T(8,128)S(1)} %bitcast.12, f32[4,96,8,128]{3,2,1,0:T(8,128)S(1)} %bitcast.11, f32[3,256,128]{2,1,0:T(8,128)} %copy-done.8, f32[12]{0:T(128)S(1)} %copy-done.10, f32[96]{0:T(128)S(1)} %copy-done.11), custom_call_target="tpu_custom_call" | custom-call | flops 13762560 | bytes 6291456 | tf_op jit(solution)/shard_map/grid_steps/pallas_call | solution.py:630
  86.7 26.6 %all_to_all.31 = f32[128,1,2688]{2,1,0:T(1,128)S(1)} all-to-all(f32[128,1,2688]{2,1,0:T(1,128)S(1)} %bitcast.18), channel_id=1, replica_groups=mesh['wave'=8,'band'=16] {'wave','band'}, dimensions={0} | all-to-all | bytes 2752512 | tf_op jit(solution)/shard_map/all_to_all | solution.py:498
  113.3 1.4 analysis.1
  114.7 14.6 %all_to_all.32.spec_ref = f32[8,168,128]{2,1,0:T(8,128)S(1)} all-to-all(f32[8,168,128]{2,1,0:T(8,128)S(1)} %bitcast.20), channel_id=1, replica_groups=mesh['wave'=8,'band'=16] {'wave'}, dimensions={0} | all-to-all | bytes 1376256 | tf_op jit(solution)/shard_map/all_to_all | solution.py:498
  129.3 6.4 %legendre_adjoint.1 = f32[16,48,128]{2,1,0:T(8,128)S(1)} custom-call(f32[8,168,128]{2,1,0:T(8,128)S(1)} %all_to_all.32.spec_ref, f32[28,448,256]{2,1,0:T(8,128)} %table_hbm.3), custom_call_target="tpu_custom_call" | custom-call | flops 924844032 | bytes 14680064 | tf_op jit(solution)/shard_map/legendre_adjoint/pallas_call | solution.py:663
  135.8 12.5 %all_to_all.33 = f32[16,48,128]{2,1,0:T(8,128)S(1)} all-to-all(f32[16,48,128]{2,1,0:T(8,128)S(1)} %legendre_adjoint.1), channel_id=1, replica_groups=mesh['wave'=8,'band'=16] {'band'}, dimensions={0} | all-to-all | bytes 786432 | tf_op jit(solution)/shard_map/all_to_all | solution.py:498
  148.2 0.0 copy-done.3
  148.3 1.6 %unmix.1 = f32[28,16,192]{2,1,0:T(8,128)} custom-call(f32[24,4,8,128]{3,2,1,0:T(8,128)S(1)} %bitcast.17, f32[28,16,192]{2,1,0:T(8,128)S(1)} %bitcast.14, f32[28,16,192]{2,1,0:T(8,128)S(1)} %bitcast.16, f32[96,96]{1,0:T(8,128)S(1)} %copy-done.9), custom_call_target="tpu_custom_call" | custom-call | flops 99090432 | bytes 1048576 | tf_op jit(solution)/shard_map/unmix/pallas_call | solution.py:675
  (12 shorter events, 0.0 us)
Async XLA Ops:
  0.6 11.1 %copy-start.12 = (s32[224]{0:T(256)S(1)}, s32[224]{0:T(256)}, u32[]{:S(2)}) copy-start(s32[224]{0:T(256)} %param.18) | copy-start | bytes 2692
  3.6 21.7 %all-to-all-start = ((f32[16,88,128]{2,1,0:T(8,128)}), f32[16,88,128]{2,1,0:T(8,128)S(1)}, u32[]{:S(2)}, u32[]{:S(2)}) async-start(f32[16,88,128]{2,1,0:T(8,128)} %mix.1), calls=%async_computation | async-start | bytes 1441792 | tf_op jit(solution)/shard_map/all_to_all | solution.py:498
  15.2 38.0 %copy-start.4 = (bf16[448,1024]{1,0:T(8,128)(2,1)}, bf16[448,1024]{1,0:T(8,128)(2,1)S(1)}, u32[]{:S(2)}) copy-start(bf16[448,1024]{1,0:T(8,128)(2,1)S(1)} %get-tuple-element.12.high_ref) | copy-start | bytes 2752516
  15.3 38.0 %copy-start.6 = (bf16[448,1024]{1,0:T(8,128)(2,1)}, bf16[448,1024]{1,0:T(8,128)(2,1)S(1)}, u32[]{:S(2)}) copy-start(bf16[448,1024]{1,0:T(8,128)(2,1)S(1)} %get-tuple-element.13.low_ref) | copy-start | bytes 2752516
  53.3 2.3 %copy-start = (f32[8,248,128]{2,1,0:T(8,128)}, f32[8,248,128]{2,1,0:T(8,128)S(1)}, u32[]{:S(2)}) copy-start(f32[8,248,128]{2,1,0:T(8,128)S(1)} %all_to_all.30.spec_ref.obs_ref) | copy-start | bytes 3047428
  55.6 27.1 %all-to-all-start.2 = ((f32[128,1,2688]{2,1,0:T(1,128)}), f32[128,1,2688]{2,1,0:T(1,128)S(1)}, u32[]{:S(2)}, u32[]{:S(2)}) async-start(f32[128,1,2688]{2,1,0:T(1,128)} %bitcast.3), calls=%async_computation.2 | async-start | bytes 2752512 | tf_op jit(solution)/shard_map/all_to_all | solution.py:498
  60.3 2.4 %copy-start.1 = (f32[8,248,128]{2,1,0:T(8,128)S(1)}, f32[8,248,128]{2,1,0:T(8,128)}, u32[]{:S(2)}) copy-start(f32[8,248,128]{2,1,0:T(8,128)} %copy-done) | copy-start | bytes 3047428
  62.7 20.1 %copy-start.10 = (f32[12]{0:T(128)S(1)}, f32[12]{0:T(128)}, u32[]{:S(2)}) copy-start(f32[12]{0:T(128)} %lidar_ref.1) | copy-start | bytes 148
  62.7 20.0 %copy-start.11 = (f32[96]{0:T(128)S(1)}, f32[96]{0:T(128)}, u32[]{:S(2)}) copy-start(f32[96]{0:T(128)} %aod_ref.1) | copy-start | bytes 1156
  72.2 0.7 copy-start.8
  86.7 26.6 %copy-start.5 = (bf16[448,1024]{1,0:T(8,128)(2,1)S(1)}, bf16[448,1024]{1,0:T(8,128)(2,1)}, u32[]{:S(2)}) copy-start(bf16[448,1024]{1,0:T(8,128)(2,1)} %copy-done.4) | copy-start | bytes 2752516
  86.7 26.6 %copy-start.7 = (bf16[448,1024]{1,0:T(8,128)(2,1)S(1)}, bf16[448,1024]{1,0:T(8,128)(2,1)}, u32[]{:S(2)}) copy-start(bf16[448,1024]{1,0:T(8,128)(2,1)} %copy-done.6) | copy-start | bytes 2752516
  129.3 18.9 %copy-start.2 = (f32[16,28,192]{2,0,1:T(8,128)S(1)}, f32[16,28,192]{2,0,1:T(8,128)}, u32[]{:S(2)}) copy-start(f32[16,28,192]{2,0,1:T(8,128)} %param.14) | copy-start | bytes 1032196
  129.3 18.9 %copy-start.3 = (f32[16,28,192]{2,0,1:T(8,128)S(1)}, f32[16,28,192]{2,0,1:T(8,128)}, u32[]{:S(2)}) copy-start(f32[16,28,192]{2,0,1:T(8,128)} %param.15) | copy-start | bytes 1032196
  129.3 18.9 %copy-start.9 = (f32[96,96]{1,0:T(8,128)S(1)}, f32[96,96]{1,0:T(8,128)}, u32[]{:S(2)}) copy-start(f32[96,96]{1,0:T(8,128)} %root_ref.1) | copy-start | bytes 110596

commit v10 on v9

--- a/solution.py
+++ b/solution.py
@@ -203,7 +203,7 @@
             part = both[:48, :NLAT] + (both[48:, :NLAT] + both[:48, NLAT:])
             acc = part if acc is None else acc + part
         acc_ref[g] = acc
-        for first, last in ((0, 5), (5, 7)):
+        for first, last in ((0, GROUPS),):
             if g + 1 == last:
                 rows = 48 * (last - first)
                 part = acc_ref[first:last].reshape(rows, NLAT)
@@ -335,7 +335,8 @@
                 out_ref[8 * half + s, 8 * c : 8 * c + 8] = z
 
 
-def unmix_kernel(modes_ref, control_ref, scale_ref, root_ref, out_ref):
+def unmix_kernel(modes_ref, control_ref, scale_ref, root_ref, out_hbm, out_ref, sem):
+    done = []
     rh, rl = doubled_root(root_ref[...])
     tiles = turn([modes_ref[:, j] for j in range(4)], 1, 2)
     for m4 in range(4):
@@ -346,6 +347,10 @@
         for g in range(GROUPS):
             m = 4 * g + m4
             out_ref[m] = control_ref[m] + z[16 * g : 16 * g + 16]
+            done.append(pltpu.make_async_copy(out_ref.at[m], out_hbm.at[m], sem.at[m]))
+            done[-1].start()
+    for copy in done:
+        copy.wait()
 
 
 def sums_kernel(obs_ref, out_ref, acc_ref):
@@ -674,7 +679,9 @@
 
     gradient = pl.pallas_call(
         unmix_kernel,
+        out_specs=pl.BlockSpec(memory_space=pl.ANY),
         out_shape=shape(28, 16, 192),
+        scratch_shapes=[pltpu.VMEM((28, 16, 192), f32), pltpu.SemaphoreType.DMA((28,))],
         compiler_params=params(),
         cost_estimate=cost(6 * 448 * 192 * 192, 1 << 20),
         name="unmix",

time: 150 us -> 151 us (level)
  no operation moved by 1% of the time
where the time goes in v10:
time: 151 us; the launch traced here: 150 us
  blocking collectives  73.5 us (49%)
  Pallas kernels  42.1 us (28%)
  waiting for transfers between devices  19.8 us (13%)
  starting transfers between devices  12.8 us (8%)
    all_to_all x4, blocking collectives, exchange(): return lax.all_to_all(tiles, axis, split_axis=0, concat_axis=0, tiled=True)  73.5 us
    all_to_all x2, waiting for transfers between devices, exchange(): return lax.all_to_all(tiles, axis, split_axis=0, concat_axis=0, tiled=True)  19.8 us
    all_to_all x2, starting transfers between devices, exchange(): return lax.all_to_all(tiles, axis, split_axis=0, concat_axis=0, tiled=True)  12.8 us
    pallas_call x1, Pallas kernels, body(): pl.pallas_call(sums_kernel, grid=(WAVES,), in_specs=[pl.BlockSpec((1, 248...  9.53 us
    pallas_call x1, Pallas kernels, body(): pl.pallas_call(legendre_kernel, in_specs=[whole(BANDS, 88, 128), hbm], ou...  7.94 us
    pallas_call x1, Pallas kernels, body(): pl.pallas_call(legendre_adjoint_kernel, in_specs=[whole(WAVES, 168, 128),...  6.45 us
    pallas_call x1, Pallas kernels, body(): pl.pallas_call(grid_kernel, in_specs=[whole(*quarters), whole(4, CH, 8, 1...  3.95 us
    pallas_call x1, Pallas kernels, body(): pl.pallas_call(wave_table_kernel, out_shape=(shape(2 * MW, NLON, kind=bf1...  3.48 us
  transfers between devices with their start and end apart: 2, of which 2 were waited for; matrix products, arithmetic and copies ran while one was open for 0% of the time, Pallas kernels for 10%

profile of v10, /device:TPU:0, one launch (start us, length us, event | category | flops | bytes accessed | tf_op | source)
XLA Modules:
  0.0 150.0 jit_solution(5334928292408388357)
XLA Ops:
  0.6 0.0 copy-start.12
  0.6 3.0 %mix.1 = f32[16,88,128]{2,1,0:T(8,128)} custom-call(f32[28,16,192]{2,1,0:T(8,128)} %bitcast.13, f32[28,16,192]{2,1,0:T(8,128)} %bitcast.15, f32[96,96]{1,0:T(8,128)} %root_ref.1, s32[128,128]{1,0:T(8,128)} %column_hbm.1, s32[128,128]{1,0:T(8,128)} %level_hbm.1, f32[128,128]{1,0:T(8,128)} %lidar_hbm.1, f32[128,128]{1,0:T(8,128)} %aod_hbm.1, ...), custom_call_target="tpu_custom_call" | custom-call | flops 99090432 | bytes 1048576 | tf_op jit(solution)/shard_map/mix/pallas_call | solution.py:530
  3.6 8.1 %all-to-all-start = ((f32[16,88,128]{2,1,0:T(8,128)}), f32[16,88,128]{2,1,0:T(8,128)S(1)}, u32[]{:S(2)}, u32[]{:S(2)}) async-start(f32[16,88,128]{2,1,0:T(8,128)} %mix.1), calls=%async_computation | async-start | bytes 1441792 | tf_op jit(solution)/shard_map/all_to_all | solution.py:503
  11.8 0.0 copy-done.12
  11.8 3.5 %wave_table.1 = (bf16[448,1024]{1,0:T(8,128)(2,1)S(1)}, bf16[448,1024]{1,0:T(8,128)(2,1)S(1)}) custom-call(s32[1,224]{1,0:T(1,128)S(1)} %bitcast.21), custom_call_target="tpu_custom_call" | custom-call | flops 9175040 | bytes 2097152 | tf_op jit(solution)/shard_map/wave_table/pallas_call | solution.py:565
  15.2 0.0 copy-start.4
  15.3 0.0 copy-start.6
  15.3 10.1 %all-to-all-done.modes_ref = f32[16,88,128]{2,1,0:T(8,128)S(1)} async-done(((f32[16,88,128]{2,1,0:T(8,128)}), f32[16,88,128]{2,1,0:T(8,128)S(1)}, u32[]{:S(2)}, u32[]{:S(2)}) %all-to-all-start) | async-done | bytes 720928 | tf_op jit(solution)/shard_map/all_to_all | solution.py:503
  25.3 7.9 %legendre.1 = f32[8,248,128]{2,1,0:T(8,128)S(1)} custom-call(f32[16,88,128]{2,1,0:T(8,128)S(1)} %all-to-all-done.modes_ref, f32[28,448,256]{2,1,0:T(8,128)} %table_hbm.3), custom_call_target="tpu_custom_call" | custom-call | flops 924844032 | bytes 14680064 | tf_op jit(solution)/shard_map/legendre/pallas_call | solution.py:577
  33.3 19.9 %all_to_all.30.spec_ref.obs_ref = f32[8,248,128]{2,1,0:T(8,128)S(1)} all-to-all(f32[8,248,128]{2,1,0:T(8,128)S(1)} %legendre.1), channel_id=1, replica_groups=mesh['wave'=8,'band'=16] {'wave'}, dimensions={0} | all-to-all | bytes 2031616 | tf_op jit(solution)/shard_map/all_to_all | solution.py:503
  53.1 0.0 copy-done.4
  53.1 0.0 copy-done.6
  53.2 2.3 %synthesis.1 = f32[2688,128]{1,0:T(8,128)} custom-call(f32[8,248,128]{2,1,0:T(8,128)S(1)} %all_to_all.30.spec_ref.obs_ref, bf16[448,1024]{1,0:T(8,128)(2,1)S(1)} %get-tuple-element.12.high_ref, bf16[448,1024]{1,0:T(8,128)(2,1)S(1)} %get-tuple-element.13.low_ref), custom_call_target="tpu_custom_call" | custom-call | flops 1056964608 | bytes 4194304 | tf_op jit(solution)/shard_map/synthesis/pallas_call | solution.py:606
  55.5 0.0 copy-done
  55.5 4.7 %all-to-all-start.2 = ((f32[128,1,2688]{2,1,0:T(1,128)}), f32[128,1,2688]{2,1,0:T(1,128)S(1)}, u32[]{:S(2)}, u32[]{:S(2)}) async-start(f32[128,1,2688]{2,1,0:T(1,128)} %bitcast.3), calls=%async_computation.2 | async-start | bytes 2752512 | tf_op jit(solution)/shard_map/all_to_all | solution.py:503
  60.2 0.0 copy-start.1
  60.2 2.4 %flow.1 = f32[384,8,128]{2,1,0:T(8,128)S(1)} custom-call(f32[28,96,128]{2,1,0:T(8,128)} %courant_ref.1), custom_call_target="tpu_custom_call" | custom-call | flops 2064384 | bytes 3145728 | tf_op jit(solution)/shard_map/flow/pallas_call | solution.py:624
  62.6 0.0 copy-done.1
  62.6 0.0 copy-start.10
  62.6 0.0 copy-start.11
  62.6 9.5 %sums.1.sums_hbm = f32[3,256,128]{2,1,0:T(8,128)S(1)} custom-call(f32[8,248,128]{2,1,0:T(8,128)S(1)} %copy-done.1), custom_call_target="tpu_custom_call" | custom-call | flops 6442450944 | bytes 1048576 | tf_op jit(solution)/shard_map/sums/pallas_call | solution.py:592
  72.1 0.0 copy-start.8
  72.1 0.7 copy-done.8
  72.9 9.7 %all-to-all-done.2 = f32[128,1,2688]{2,1,0:T(1,128)S(1)} async-done(((f32[128,1,2688]{2,1,0:T(1,128)}), f32[128,1,2688]{2,1,0:T(1,128)S(1)}, u32[]{:S(2)}, u32[]{:S(2)}) %all-to-all-start.2) | async-done | bytes 1376288 | tf_op jit(solution)/shard_map/all_to_all | solution.py:503
  82.6 0.0 copy-done.10
  82.6 3.9 %grid_steps.1 = (f32[28,96,128]{2,1,0:T(8,128)}, f32[4,672,128]{2,1,0:T(8,128)S(1)}) custom-call(f32[4,672,128]{2,1,0:T(8,128)S(1)} %bitcast.12, f32[4,96,8,128]{3,2,1,0:T(8,128)S(1)} %bitcast.11, f32[3,256,128]{2,1,0:T(8,128)} %copy-done.8, f32[12]{0:T(128)S(1)} %copy-done.10, f32[96]{0:T(128)S(1)} %copy-done.11), custom_call_target="tpu_custom_call" | custom-call | flops 13762560 | bytes 6291456 | tf_op jit(solution)/shard_map/grid_steps/pallas_call | solution.py:635
  86.6 26.6 %all_to_all.31 = f32[128,1,2688]{2,1,0:T(1,128)S(1)} all-to-all(f32[128,1,2688]{2,1,0:T(1,128)S(1)} %bitcast.18), channel_id=1, replica_groups=mesh['wave'=8,'band'=16] {'wave','band'}, dimensions={0} | all-to-all | bytes 2752512 | tf_op jit(solution)/shard_map/all_to_all | solution.py:503
  113.2 1.4 analysis.1
  114.6 14.6 %all_to_all.32.spec_ref = f32[8,168,128]{2,1,0:T(8,128)S(1)} all-to-all(f32[8,168,128]{2,1,0:T(8,128)S(1)} %bitcast.20), channel_id=1, replica_groups=mesh['wave'=8,'band'=16] {'wave'}, dimensions={0} | all-to-all | bytes 1376256 | tf_op jit(solution)/shard_map/all_to_all | solution.py:503
  129.2 6.4 %legendre_adjoint.1 = f32[16,48,128]{2,1,0:T(8,128)S(1)} custom-call(f32[8,168,128]{2,1,0:T(8,128)S(1)} %all_to_all.32.spec_ref, f32[28,448,256]{2,1,0:T(8,128)} %table_hbm.3), custom_call_target="tpu_custom_call" | custom-call | flops 924844032 | bytes 14680064 | tf_op jit(solution)/shard_map/legendre_adjoint/pallas_call | solution.py:668
  135.7 12.5 %all_to_all.33 = f32[16,48,128]{2,1,0:T(8,128)S(1)} all-to-all(f32[16,48,128]{2,1,0:T(8,128)S(1)} %legendre_adjoint.1), channel_id=1, replica_groups=mesh['wave'=8,'band'=16] {'band'}, dimensions={0} | all-to-all | bytes 786432 | tf_op jit(solution)/shard_map/all_to_all | solution.py:503
  148.1 1.7 %unmix.1 = f32[28,16,192]{2,1,0:T(8,128)} custom-call(f32[24,4,8,128]{3,2,1,0:T(8,128)S(1)} %bitcast.17, f32[28,16,192]{2,1,0:T(8,128)S(1)} %bitcast.14, f32[28,16,192]{2,1,0:T(8,128)S(1)} %bitcast.16, f32[96,96]{1,0:T(8,128)S(1)} %copy-done.9), custom_call_target="tpu_custom_call" | custom-call | flops 99090432 | bytes 1048576 | tf_op jit(solution)/shard_map/unmix/pallas_call | solution.py:680
  (12 shorter events, 0.0 us)
Async XLA Ops:
  0.6 11.1 %copy-start.12 = (s32[224]{0:T(256)S(1)}, s32[224]{0:T(256)}, u32[]{:S(2)}) copy-start(s32[224]{0:T(256)} %param.18) | copy-start | bytes 2692
  3.6 21.7 %all-to-all-start = ((f32[16,88,128]{2,1,0:T(8,128)}), f32[16,88,128]{2,1,0:T(8,128)S(1)}, u32[]{:S(2)}, u32[]{:S(2)}) async-start(f32[16,88,128]{2,1,0:T(8,128)} %mix.1), calls=%async_computation | async-start | bytes 1441792 | tf_op jit(solution)/shard_map/all_to_all | solution.py:503
  15.2 37.9 %copy-start.4 = (bf16[448,1024]{1,0:T(8,128)(2,1)}, bf16[448,1024]{1,0:T(8,128)(2,1)S(1)}, u32[]{:S(2)}) copy-start(bf16[448,1024]{1,0:T(8,128)(2,1)S(1)} %get-tuple-element.12.high_ref) | copy-start | bytes 2752516
  15.3 37.9 %copy-start.6 = (bf16[448,1024]{1,0:T(8,128)(2,1)}, bf16[448,1024]{1,0:T(8,128)(2,1)S(1)}, u32[]{:S(2)}) copy-start(bf16[448,1024]{1,0:T(8,128)(2,1)S(1)} %get-tuple-element.13.low_ref) | copy-start | bytes 2752516
  53.2 2.3 %copy-start = (f32[8,248,128]{2,1,0:T(8,128)}, f32[8,248,128]{2,1,0:T(8,128)S(1)}, u32[]{:S(2)}) copy-start(f32[8,248,128]{2,1,0:T(8,128)S(1)} %all_to_all.30.spec_ref.obs_ref) | copy-start | bytes 3047428
  55.5 27.1 %all-to-all-start.2 = ((f32[128,1,2688]{2,1,0:T(1,128)}), f32[128,1,2688]{2,1,0:T(1,128)S(1)}, u32[]{:S(2)}, u32[]{:S(2)}) async-start(f32[128,1,2688]{2,1,0:T(1,128)} %bitcast.3), calls=%async_computation.2 | async-start | bytes 2752512 | tf_op jit(solution)/shard_map/all_to_all | solution.py:503
  60.2 2.4 %copy-start.1 = (f32[8,248,128]{2,1,0:T(8,128)S(1)}, f32[8,248,128]{2,1,0:T(8,128)}, u32[]{:S(2)}) copy-start(f32[8,248,128]{2,1,0:T(8,128)} %copy-done) | copy-start | bytes 3047428
  62.6 20.1 %copy-start.10 = (f32[12]{0:T(128)S(1)}, f32[12]{0:T(128)}, u32[]{:S(2)}) copy-start(f32[12]{0:T(128)} %lidar_ref.1) | copy-start | bytes 148
  62.6 20.0 %copy-start.11 = (f32[96]{0:T(128)S(1)}, f32[96]{0:T(128)}, u32[]{:S(2)}) copy-start(f32[96]{0:T(128)} %aod_ref.1) | copy-start | bytes 1156
  72.1 0.7 copy-start.8
  86.6 26.6 %copy-start.5 = (bf16[448,1024]{1,0:T(8,128)(2,1)S(1)}, bf16[448,1024]{1,0:T(8,128)(2,1)}, u32[]{:S(2)}) copy-start(bf16[448,1024]{1,0:T(8,128)(2,1)} %copy-done.4) | copy-start | bytes 2752516
  86.6 26.6 %copy-start.7 = (bf16[448,1024]{1,0:T(8,128)(2,1)S(1)}, bf16[448,1024]{1,0:T(8,128)(2,1)}, u32[]{:S(2)}) copy-start(bf16[448,1024]{1,0:T(8,128)(2,1)} %copy-done.6) | copy-start | bytes 2752516
  129.2 18.9 %copy-start.2 = (f32[16,28,192]{2,0,1:T(8,128)S(1)}, f32[16,28,192]{2,0,1:T(8,128)}, u32[]{:S(2)}) copy-start(f32[16,28,192]{2,0,1:T(8,128)} %param.14) | copy-start | bytes 1032196
  129.2 18.9 %copy-start.3 = (f32[16,28,192]{2,0,1:T(8,128)S(1)}, f32[16,28,192]{2,0,1:T(8,128)}, u32[]{:S(2)}) copy-start(f32[16,28,192]{2,0,1:T(8,128)} %param.15) | copy-start | bytes 1032196
  129.2 18.9 %copy-start.9 = (f32[96,96]{1,0:T(8,128)S(1)}, f32[96,96]{1,0:T(8,128)}, u32[]{:S(2)}) copy-start(f32[96,96]{1,0:T(8,128)} %root_ref.1) | copy-start | bytes 110596

commit v11 on v9

--- a/solution.py
+++ b/solution.py
@@ -115,22 +115,8 @@
             )
         )
     ]
-    for copy in copies[3:] + copies[:3]:
+    for copy in copies:
         copy.start()
-    for copy in copies[3:]:
-        copy.wait()
-    counts = jnp.broadcast_to(count_ref[...].astype(f32), (DEVICES, DEVICES)).T
-    live = iota((DEVICES, SLOT), 1).astype(f32) < counts
-    weight = jnp.where(live, value_ref[2], 0.0)
-    obs_ref[0] = index_ref[0].astype(f32)
-    obs_ref[1] = index_ref[1].astype(f32)
-    obs_ref[2] = weight
-    obs_ref[3] = weight * value_ref[0]
-    obs_ref[4] = weight * value_ref[1]
-    for band in range(BANDS):
-        for k in range(5):
-            rows = obs_ref[k, pl.ds(band, WAVES, stride=BANDS), :]
-            out_ref[band, 48 + 8 * k : 56 + 8 * k] = rows
     done = []
 
     def send(first, count, row, rows):
@@ -138,8 +124,6 @@
         sent = pltpu.make_async_copy(out_ref.at[at], out_hbm.at[at], sem.at[9 + len(done)])
         sent.start()
         done.append(sent)
-
-    send(0, BANDS, 48, 40)
 
     for copy in copies[:3]:
         copy.wait()
@@ -158,6 +142,22 @@
                 c = 48 * part + 4 * h + j
                 out_ref[c // 6, 8 * (c % 6) : 8 * (c % 6) + 8] = z[h]
         send(8 * part, 8, 0, 48)
+
+    for copy in copies[3:]:
+        copy.wait()
+    counts = jnp.broadcast_to(count_ref[...].astype(f32), (DEVICES, DEVICES)).T
+    live = iota((DEVICES, SLOT), 1).astype(f32) < counts
+    weight = jnp.where(live, value_ref[2], 0.0)
+    obs_ref[0] = index_ref[0].astype(f32)
+    obs_ref[1] = index_ref[1].astype(f32)
+    obs_ref[2] = weight
+    obs_ref[3] = weight * value_ref[0]
+    obs_ref[4] = weight * value_ref[1]
+    for band in range(BANDS):
+        for k in range(5):
+            rows = obs_ref[k, pl.ds(band, WAVES, stride=BANDS), :]
+            out_ref[band, 48 + 8 * k : 56 + 8 * k] = rows
+    send(0, BANDS, 48, 40)
     for copy in done:
         copy.wait()
 
@@ -203,7 +203,7 @@
             part = both[:48, :NLAT] + (both[48:, :NLAT] + both[:48, NLAT:])
             acc = part if acc is None else acc + part
         acc_ref[g] = acc
-        for first, last in ((0, 5), (5, 7)):
+        for first, last in ((0, GROUPS),):
             if g + 1 == last:
                 rows = 48 * (last - first)
                 part = acc_ref[first:last].reshape(rows, NLAT)

time: 150 us -> 150 us (level)
  no operation moved by 1% of the time
where the time goes in v11:
time: 150 us
  blocking collectives  73.5 us (49%)
  Pallas kernels  42 us (28%)
  waiting for transfers between devices  19.8 us (13%)
  starting transfers between devices  12.8 us (9%)
    all_to_all x4, blocking collectives, exchange(): return lax.all_to_all(tiles, axis, split_axis=0, concat_axis=0, tiled=True)  73.5 us
    all_to_all x2, waiting for transfers between devices, exchange(): return lax.all_to_all(tiles, axis, split_axis=0, concat_axis=0, tiled=True)  19.8 us
    all_to_all x2, starting transfers between devices, exchange(): return lax.all_to_all(tiles, axis, split_axis=0, concat_axis=0, tiled=True)  12.8 us
    pallas_call x1, Pallas kernels, body(): pl.pallas_call(sums_kernel, grid=(WAVES,), in_specs=[pl.BlockSpec((1, 248...  9.52 us
    pallas_call x1, Pallas kernels, body(): pl.pallas_call(legendre_kernel, in_specs=[whole(BANDS, 88, 128), hbm], ou...  7.94 us
    pallas_call x1, Pallas kernels, body(): pl.pallas_call(legendre_adjoint_kernel, in_specs=[whole(WAVES, 168, 128),...  6.45 us
    pallas_call x1, Pallas kernels, body(): pl.pallas_call(grid_kernel, in_specs=[whole(*quarters), whole(4, CH, 8, 1...  3.95 us
    pallas_call x1, Pallas kernels, body(): pl.pallas_call(wave_table_kernel, out_shape=(shape(2 * MW, NLON, kind=bf1...  3.48 us
  transfers between devices with their start and end apart: 2, of which 2 were waited for; matrix products, arithmetic and copies ran while one was open for 0% of the time, Pallas kernels for 10%

profile of v11, /device:TPU:0, one launch (start us, length us, event | category | flops | bytes accessed | tf_op | source)
XLA Modules:
  0.0 149.7 jit_solution(8165189198576750928)
XLA Ops:
  0.6 0.0 copy-start.12
  0.6 3.0 %mix.1 = f32[16,88,128]{2,1,0:T(8,128)} custom-call(f32[28,16,192]{2,1,0:T(8,128)} %bitcast.13, f32[28,16,192]{2,1,0:T(8,128)} %bitcast.15, f32[96,96]{1,0:T(8,128)} %root_ref.1, s32[128,128]{1,0:T(8,128)} %column_hbm.1, s32[128,128]{1,0:T(8,128)} %level_hbm.1, f32[128,128]{1,0:T(8,128)} %lidar_hbm.1, f32[128,128]{1,0:T(8,128)} %aod_hbm.1, ...), custom_call_target="tpu_custom_call" | custom-call | flops 99090432 | bytes 1048576 | tf_op jit(solution)/shard_map/mix/pallas_call | solution.py:525
  3.6 8.1 %all-to-all-start = ((f32[16,88,128]{2,1,0:T(8,128)}), f32[16,88,128]{2,1,0:T(8,128)S(1)}, u32[]{:S(2)}, u32[]{:S(2)}) async-start(f32[16,88,128]{2,1,0:T(8,128)} %mix.1), calls=%async_computation | async-start | bytes 1441792 | tf_op jit(solution)/shard_map/all_to_all | solution.py:498
  11.8 0.0 copy-done.12
  11.8 3.5 %wave_table.1 = (bf16[448,1024]{1,0:T(8,128)(2,1)S(1)}, bf16[448,1024]{1,0:T(8,128)(2,1)S(1)}) custom-call(s32[1,224]{1,0:T(1,128)S(1)} %bitcast.21), custom_call_target="tpu_custom_call" | custom-call | flops 9175040 | bytes 2097152 | tf_op jit(solution)/shard_map/wave_table/pallas_call | solution.py:560
  15.3 0.0 copy-start.4
  15.3 0.0 copy-start.6
  15.3 10.1 %all-to-all-done.modes_ref = f32[16,88,128]{2,1,0:T(8,128)S(1)} async-done(((f32[16,88,128]{2,1,0:T(8,128)}), f32[16,88,128]{2,1,0:T(8,128)S(1)}, u32[]{:S(2)}, u32[]{:S(2)}) %all-to-all-start) | async-done | bytes 720928 | tf_op jit(solution)/shard_map/all_to_all | solution.py:498
  25.4 7.9 %legendre.1 = f32[8,248,128]{2,1,0:T(8,128)S(1)} custom-call(f32[16,88,128]{2,1,0:T(8,128)S(1)} %all-to-all-done.modes_ref, f32[28,448,256]{2,1,0:T(8,128)} %table_hbm.3), custom_call_target="tpu_custom_call" | custom-call | flops 924844032 | bytes 14680064 | tf_op jit(solution)/shard_map/legendre/pallas_call | solution.py:572
  33.3 19.8 %all_to_all.30.spec_ref.obs_ref = f32[8,248,128]{2,1,0:T(8,128)S(1)} all-to-all(f32[8,248,128]{2,1,0:T(8,128)S(1)} %legendre.1), channel_id=1, replica_groups=mesh['wave'=8,'band'=16] {'wave'}, dimensions={0} | all-to-all | bytes 2031616 | tf_op jit(solution)/shard_map/all_to_all | solution.py:498
  53.2 0.0 copy-done.4
  53.2 0.0 copy-done.6
  53.2 2.3 %synthesis.1 = f32[2688,128]{1,0:T(8,128)} custom-call(f32[8,248,128]{2,1,0:T(8,128)S(1)} %all_to_all.30.spec_ref.obs_ref, bf16[448,1024]{1,0:T(8,128)(2,1)S(1)} %get-tuple-element.12.high_ref, bf16[448,1024]{1,0:T(8,128)(2,1)S(1)} %get-tuple-element.13.low_ref), custom_call_target="tpu_custom_call" | custom-call | flops 1056964608 | bytes 4194304 | tf_op jit(solution)/shard_map/synthesis/pallas_call | solution.py:601
  55.5 0.0 copy-done
  55.5 4.7 %all-to-all-start.2 = ((f32[128,1,2688]{2,1,0:T(1,128)}), f32[128,1,2688]{2,1,0:T(1,128)S(1)}, u32[]{:S(2)}, u32[]{:S(2)}) async-start(f32[128,1,2688]{2,1,0:T(1,128)} %bitcast.3), calls=%async_computation.2 | async-start | bytes 2752512 | tf_op jit(solution)/shard_map/all_to_all | solution.py:498
  60.2 0.0 copy-start.1
  60.2 2.4 %flow.1 = f32[384,8,128]{2,1,0:T(8,128)S(1)} custom-call(f32[28,96,128]{2,1,0:T(8,128)} %courant_ref.1), custom_call_target="tpu_custom_call" | custom-call | flops 2064384 | bytes 3145728 | tf_op jit(solution)/shard_map/flow/pallas_call | solution.py:619
  62.6 0.0 copy-start.10
  62.6 0.0 copy-start.11
  62.6 9.5 %sums.1.sums_hbm = f32[3,256,128]{2,1,0:T(8,128)S(1)} custom-call(f32[8,248,128]{2,1,0:T(8,128)S(1)} %copy-done.1), custom_call_target="tpu_custom_call" | custom-call | flops 6442450944 | bytes 1048576 | tf_op jit(solution)/shard_map/sums/pallas_call | solution.py:587
  72.1 0.0 copy-start.8
  72.1 0.7 copy-done.8
  72.9 9.7 %all-to-all-done.2 = f32[128,1,2688]{2,1,0:T(1,128)S(1)} async-done(((f32[128,1,2688]{2,1,0:T(1,128)}), f32[128,1,2688]{2,1,0:T(1,128)S(1)}, u32[]{:S(2)}, u32[]{:S(2)}) %all-to-all-start.2) | async-done | bytes 1376288 | tf_op jit(solution)/shard_map/all_to_all | solution.py:498
  82.6 0.0 copy-done.10
  82.6 3.9 %grid_steps.1 = (f32[28,96,128]{2,1,0:T(8,128)}, f32[4,672,128]{2,1,0:T(8,128)S(1)}) custom-call(f32[4,672,128]{2,1,0:T(8,128)S(1)} %bitcast.12, f32[4,96,8,128]{3,2,1,0:T(8,128)S(1)} %bitcast.11, f32[3,256,128]{2,1,0:T(8,128)} %copy-done.8, f32[12]{0:T(128)S(1)} %copy-done.10, f32[96]{0:T(128)S(1)} %copy-done.11), custom_call_target="tpu_custom_call" | custom-call | flops 13762560 | bytes 6291456 | tf_op jit(solution)/shard_map/grid_steps/pallas_call | solution.py:630
  86.6 26.6 %all_to_all.31 = f32[128,1,2688]{2,1,0:T(1,128)S(1)} all-to-all(f32[128,1,2688]{2,1,0:T(1,128)S(1)} %bitcast.18), channel_id=1, replica_groups=mesh['wave'=8,'band'=16] {'wave','band'}, dimensions={0} | all-to-all | bytes 2752512 | tf_op jit(solution)/shard_map/all_to_all | solution.py:498
  113.2 0.0 copy-done.5
  113.2 1.4 analysis.1
  114.6 14.6 %all_to_all.32.spec_ref = f32[8,168,128]{2,1,0:T(8,128)S(1)} all-to-all(f32[8,168,128]{2,1,0:T(8,128)S(1)} %bitcast.20), channel_id=1, replica_groups=mesh['wave'=8,'band'=16] {'wave'}, dimensions={0} | all-to-all | bytes 1376256 | tf_op jit(solution)/shard_map/all_to_all | solution.py:498
  129.2 6.4 %legendre_adjoint.1 = f32[16,48,128]{2,1,0:T(8,128)S(1)} custom-call(f32[8,168,128]{2,1,0:T(8,128)S(1)} %all_to_all.32.spec_ref, f32[28,448,256]{2,1,0:T(8,128)} %table_hbm.3), custom_call_target="tpu_custom_call" | custom-call | flops 924844032 | bytes 14680064 | tf_op jit(solution)/shard_map/legendre_adjoint/pallas_call | solution.py:663
  135.7 12.5 %all_to_all.33 = f32[16,48,128]{2,1,0:T(8,128)S(1)} all-to-all(f32[16,48,128]{2,1,0:T(8,128)S(1)} %legendre_adjoint.1), channel_id=1, replica_groups=mesh['wave'=8,'band'=16] {'band'}, dimensions={0} | all-to-all | bytes 786432 | tf_op jit(solution)/shard_map/all_to_all | solution.py:498
  148.1 1.6 %unmix.1 = f32[28,16,192]{2,1,0:T(8,128)} custom-call(f32[24,4,8,128]{3,2,1,0:T(8,128)S(1)} %bitcast.17, f32[28,16,192]{2,1,0:T(8,128)S(1)} %bitcast.14, f32[28,16,192]{2,1,0:T(8,128)S(1)} %bitcast.16, f32[96,96]{1,0:T(8,128)S(1)} %copy-done.9), custom_call_target="tpu_custom_call" | custom-call | flops 99090432 | bytes 1048576 | tf_op jit(solution)/shard_map/unmix/pallas_call | solution.py:675
  (12 shorter events, 0.0 us)
Async XLA Ops:
  0.6 11.1 %copy-start.12 = (s32[224]{0:T(256)S(1)}, s32[224]{0:T(256)}, u32[]{:S(2)}) copy-start(s32[224]{0:T(256)} %param.18) | copy-start | bytes 2692
  3.6 21.8 %all-to-all-start = ((f32[16,88,128]{2,1,0:T(8,128)}), f32[16,88,128]{2,1,0:T(8,128)S(1)}, u32[]{:S(2)}, u32[]{:S(2)}) async-start(f32[16,88,128]{2,1,0:T(8,128)} %mix.1), calls=%async_computation | async-start | bytes 1441792 | tf_op jit(solution)/shard_map/all_to_all | solution.py:498
  15.3 37.9 %copy-start.4 = (bf16[448,1024]{1,0:T(8,128)(2,1)}, bf16[448,1024]{1,0:T(8,128)(2,1)S(1)}, u32[]{:S(2)}) copy-start(bf16[448,1024]{1,0:T(8,128)(2,1)S(1)} %get-tuple-element.12.high_ref) | copy-start | bytes 2752516
  15.3 37.9 %copy-start.6 = (bf16[448,1024]{1,0:T(8,128)(2,1)}, bf16[448,1024]{1,0:T(8,128)(2,1)S(1)}, u32[]{:S(2)}) copy-start(bf16[448,1024]{1,0:T(8,128)(2,1)S(1)} %get-tuple-element.13.low_ref) | copy-start | bytes 2752516
  53.2 2.3 %copy-start = (f32[8,248,128]{2,1,0:T(8,128)}, f32[8,248,128]{2,1,0:T(8,128)S(1)}, u32[]{:S(2)}) copy-start(f32[8,248,128]{2,1,0:T(8,128)S(1)} %all_to_all.30.spec_ref.obs_ref) | copy-start | bytes 3047428
  55.5 27.1 %all-to-all-start.2 = ((f32[128,1,2688]{2,1,0:T(1,128)}), f32[128,1,2688]{2,1,0:T(1,128)S(1)}, u32[]{:S(2)}, u32[]{:S(2)}) async-start(f32[128,1,2688]{2,1,0:T(1,128)} %bitcast.3), calls=%async_computation.2 | async-start | bytes 2752512 | tf_op jit(solution)/shard_map/all_to_all | solution.py:498
  60.2 2.4 %copy-start.1 = (f32[8,248,128]{2,1,0:T(8,128)S(1)}, f32[8,248,128]{2,1,0:T(8,128)}, u32[]{:S(2)}) copy-start(f32[8,248,128]{2,1,0:T(8,128)} %copy-done) | copy-start | bytes 3047428
  62.6 20.1 %copy-start.10 = (f32[12]{0:T(128)S(1)}, f32[12]{0:T(128)}, u32[]{:S(2)}) copy-start(f32[12]{0:T(128)} %lidar_ref.1) | copy-start | bytes 148
  62.6 20.0 %copy-start.11 = (f32[96]{0:T(128)S(1)}, f32[96]{0:T(128)}, u32[]{:S(2)}) copy-start(f32[96]{0:T(128)} %aod_ref.1) | copy-start | bytes 1156
  72.1 0.7 copy-start.8
  86.6 26.6 %copy-start.5 = (bf16[448,1024]{1,0:T(8,128)(2,1)S(1)}, bf16[448,1024]{1,0:T(8,128)(2,1)}, u32[]{:S(2)}) copy-start(bf16[448,1024]{1,0:T(8,128)(2,1)} %copy-done.4) | copy-start | bytes 2752516
  86.6 26.6 %copy-start.7 = (bf16[448,1024]{1,0:T(8,128)(2,1)S(1)}, bf16[448,1024]{1,0:T(8,128)(2,1)}, u32[]{:S(2)}) copy-start(bf16[448,1024]{1,0:T(8,128)(2,1)} %copy-done.6) | copy-start | bytes 2752516
  129.2 18.9 %copy-start.2 = (f32[16,28,192]{2,0,1:T(8,128)S(1)}, f32[16,28,192]{2,0,1:T(8,128)}, u32[]{:S(2)}) copy-start(f32[16,28,192]{2,0,1:T(8,128)} %param.14) | copy-start | bytes 1032196
  129.2 18.9 %copy-start.3 = (f32[16,28,192]{2,0,1:T(8,128)S(1)}, f32[16,28,192]{2,0,1:T(8,128)}, u32[]{:S(2)}) copy-start(f32[16,28,192]{2,0,1:T(8,128)} %param.15) | copy-start | bytes 1032196
  129.2 18.9 %copy-start.9 = (f32[96,96]{1,0:T(8,128)S(1)}, f32[96,96]{1,0:T(8,128)}, u32[]{:S(2)}) copy-start(f32[96,96]{1,0:T(8,128)} %root_ref.1) | copy-start | bytes 110596
